TPU v7x, 32 devices: a whole 2x2x4 slice. The times are simulated.
32 devices in a mesh: dp: 4 (over x, core), fsdp: 8 (over z, y).
Axes of the slice: x: 2, y: 2, z: 4, core: 2. Of those that a mesh axis runs over, the one named last changes fastest.
Arguments:
- tokens: bfloat16 [32768, 768], P(('dp', 'fsdp')), may hold values from -6 to 6
- doc_lengths: int32 [32, 8], P(('dp', 'fsdp')), may hold values from 1 to 512, 1024 in all within a row
- cotangent: bfloat16 [32768, 768], P(('dp', 'fsdp')), may hold values from -6 to 6
- w_qkv: bfloat16 [768, 2304], P(('dp', 'fsdp')), may hold values from -0.21875 to 0.21875
- w_out: bfloat16 [768, 768], P(('dp', 'fsdp')), may hold values from -0.21875 to 0.21875
- w_up: bfloat16 [768, 3072], P(('dp', 'fsdp')), may hold values from -0.21875 to 0.21875
- w_down: bfloat16 [3072, 768], P(('dp', 'fsdp')), may hold values from -0.109375 to 0.109375
- gain_attn: bfloat16 [768], P(('dp', 'fsdp')), may hold values from 0.5 to 1.5
- gain_inner: bfloat16 [768], P(('dp', 'fsdp')), may hold values from 0.5 to 1.5
- gain_ffn: bfloat16 [768], P(('dp', 'fsdp')), may hold values from 0.5 to 1.5
- gain_mid: bfloat16 [3072], P(('dp', 'fsdp')), may hold values from 0.5 to 1.5
Outputs:
- result: bfloat16 [32768, 768], P(('dp', 'fsdp'))
- grad_tokens: float32 [32768, 768], P(('dp', 'fsdp'))
- grad_w_qkv: float32 [768, 2304], P(('dp', 'fsdp'))
- grad_w_out: float32 [768, 768], P(('dp', 'fsdp'))
- grad_w_up: float32 [768, 3072], P(('dp', 'fsdp'))
- grad_w_down: float32 [3072, 768], P(('dp', 'fsdp'))
- grad_gain_attn: float32 [768], P(('dp', 'fsdp'))
- grad_gain_inner: float32 [768], P(('dp', 'fsdp'))
- grad_gain_ffn: float32 [768], P(('dp', 'fsdp'))
- grad_gain_mid: float32 [3072], P(('dp', 'fsdp'))
Inputs may be any that keep to these rules, and one draw needn't show every extreme that they name: `doc_lengths`: each row's 8 lengths sum to 1024; its last document is padding at the row's end, and some document of each row has exactly 512 tokens.
All inputs are finite; a program needn't handle non-finite values.
Results may differ from a plain program's by a relative error of at most 0.013.
Values may be sent and summed in bfloat16 or wider, within the bound.
No kernel may reach another device: no remote copies, remote signals or barrier semaphores. Data moves between devices by JAX's collectives and lax.ppermute only.
A program may use at most 192 MiB of HBM per device.

v0:
```python
import math

import jax
import jax.numpy as jnp
from jax import lax
from jax.sharding import PartitionSpec as P

HEADS = 12
HEAD_DIM = 64


EPSILON = 1e-05
MASKED_SCORE = -1e30
ROOT_HALF = 0.7071067811865476
INV_ROOT_TAU = 0.3989422804014327


def doc_layout(doc_lengths, seq_len):
    doc_ends = jnp.cumsum(doc_lengths, axis=-1)
    doc_starts = doc_ends - doc_lengths
    places = jnp.arange(seq_len, dtype=jnp.int32)
    passed = (places[None, :, None] >= doc_ends[:, None, :]).astype(jnp.int32)
    segment = jnp.sum(passed, axis=-1)
    doc_count = doc_lengths.shape[-1]
    member = segment[:, :, None] == jnp.arange(doc_count, dtype=jnp.int32)[None, None, :]
    offset = jnp.sum(jnp.where(member, doc_starts[:, None, :], 0), axis=-1)
    position = places[None, :] - offset
    valid_mask = segment < doc_count - 1
    return (segment, position, valid_mask)


def rotary_tables(position, head_dim):
    half_dim = head_dim // 2
    frequency = jnp.exp(
        jnp.arange(half_dim, dtype=jnp.float32) * (-2.0 * math.log(10000.0) / head_dim)
    )
    angles = position.astype(jnp.float32)[..., None] * frequency
    return (jnp.cos(angles), jnp.sin(angles))


def rotate(values_in, cosine_table, sine_table):
    half_dim = values_in.shape[-1] // 2
    first_half = values_in[..., :half_dim]
    second_half = values_in[..., half_dim:]
    cos_wide = cosine_table[:, :, None, :]
    sin_wide = sine_table[:, :, None, :]
    return jnp.concatenate(
        [
            first_half * cos_wide - second_half * sin_wide,
            second_half * cos_wide + first_half * sin_wide,
        ],
        axis=-1,
    )


def unrotate(values_in, cosine_table, sine_table):
    half_dim = values_in.shape[-1] // 2
    first_half = values_in[..., :half_dim]
    second_half = values_in[..., half_dim:]
    cos_wide = cosine_table[:, :, None, :]
    sin_wide = sine_table[:, :, None, :]
    return jnp.concatenate(
        [
            first_half * cos_wide + second_half * sin_wide,
            second_half * cos_wide - first_half * sin_wide,
        ],
        axis=-1,
    )


def norm_forward(values_in, gain_vec):
    mean_val = jnp.mean(values_in, axis=-1, keepdims=True)
    centered = values_in - mean_val
    inv_std = lax.rsqrt(jnp.mean(centered * centered, axis=-1, keepdims=True) + EPSILON)
    unit_vals = centered * inv_std
    return (unit_vals * gain_vec, unit_vals, inv_std)


def norm_backward(grad_in, gain_vec, unit_vals, inv_std):
    d_unit = grad_in * gain_vec
    d_gain = jnp.sum(grad_in * unit_vals, axis=0)
    d_values = inv_std * (
        d_unit
        - jnp.mean(d_unit, axis=-1, keepdims=True)
        - unit_vals * jnp.mean(d_unit * unit_vals, axis=-1, keepdims=True)
    )
    return (d_values, d_gain)


def gelu_value(values_in):
    return 0.5 * values_in * (1.0 + lax.erf(values_in * ROOT_HALF))


def gelu_slope(values_in):
    return (
        0.5 * (1.0 + lax.erf(values_in * ROOT_HALF))
        + values_in * jnp.exp(-0.5 * values_in * values_in) * INV_ROOT_TAU
    )


def contract_rows(left_side, right_side):
    return lax.dot_general(
        left_side, right_side, (((0,), (0,)), ((), ())), preferred_element_type=jnp.float32
    )


def against(grad_in, weight_mat):
    return lax.dot_general(
        grad_in, weight_mat, (((1,), (1,)), ((), ())), preferred_element_type=jnp.float32
    )


def allowed_pairs(segment):
    seq_len = segment.shape[0]
    places = jnp.arange(seq_len, dtype=jnp.int32)
    return (segment[:, None] == segment[None, :]) & (places[None, :] <= places[:, None])


def head_scores(queries, key_rows, segment):
    scaling = 1.0 / math.sqrt(queries.shape[-1])
    scores = (
        jnp.einsum("qd,kd->qk", queries, key_rows, preferred_element_type=jnp.float32) * scaling
    )
    return jnp.where(allowed_pairs(segment), scores, MASKED_SCORE)


def head_forward(pieces):
    queries, key_rows, value_rows, segment = pieces
    scores = head_scores(queries, key_rows, segment)
    row_max = jnp.max(scores, axis=-1, keepdims=True)
    powers = jnp.exp(scores - row_max)
    row_total = jnp.sum(powers, axis=-1, keepdims=True)
    attn_probs = (powers / row_total).astype(jnp.bfloat16)
    mixed_out = jnp.dot(attn_probs, value_rows, preferred_element_type=jnp.float32)
    return (mixed_out, row_max[:, 0] + jnp.log(row_total[:, 0]))


def head_backward(pieces):
    queries, key_rows, value_rows, segment, log_total, d_mixed = pieces
    scaling = 1.0 / math.sqrt(queries.shape[-1])
    scores = head_scores(queries, key_rows, segment)
    attn_probs = jnp.exp(scores - log_total[:, None])
    probs_low = attn_probs.astype(jnp.bfloat16)
    d_value = contract_rows(probs_low, d_mixed)
    d_probs = jnp.einsum("qd,kd->qk", d_mixed, value_rows, preferred_element_type=jnp.float32)
    d_scores = (
        attn_probs * (d_probs - jnp.sum(attn_probs * d_probs, axis=-1, keepdims=True))
    ).astype(jnp.bfloat16)
    d_query = jnp.dot(d_scores, key_rows, preferred_element_type=jnp.float32) * scaling
    d_key = contract_rows(d_scores, queries) * scaling
    return (d_query, d_key, d_value)


def to_items(values_in, row_count, seq_len):
    return (
        values_in.reshape(row_count, seq_len, HEADS, HEAD_DIM)
        .transpose(0, 2, 1, 3)
        .reshape(row_count * HEADS, seq_len, HEAD_DIM)
    )


def from_items(values_in, row_count, seq_len):
    return (
        values_in.reshape(row_count, HEADS, seq_len, HEAD_DIM)
        .transpose(0, 2, 1, 3)
        .reshape(row_count * seq_len, HEADS * HEAD_DIM)
    )


def local(
    tokens,
    doc_lengths,
    cotangent,
    w_qkv,
    w_out,
    w_up,
    w_down,
    gain_attn,
    gain_inner,
    gain_ffn,
    gain_mid,
):
    row_count = doc_lengths.shape[0]
    seq_len = tokens.shape[0] // row_count
    model_width = tokens.shape[1]
    head_shape = (row_count, seq_len, HEADS, HEAD_DIM)
    segment, position, valid_mask = doc_layout(doc_lengths, seq_len)
    cosine_table, sine_table = rotary_tables(position, HEAD_DIM)
    seg_items = jnp.repeat(segment, HEADS, axis=0)
    attn_full = (
        lax.all_gather(w_qkv, ("dp", "fsdp"), axis=0, tiled=True),
        lax.all_gather(w_out, ("dp", "fsdp"), axis=0, tiled=True),
        lax.all_gather(gain_attn, ("dp", "fsdp"), axis=0, tiled=True),
        lax.all_gather(gain_inner, ("dp", "fsdp"), axis=0, tiled=True),
    )
    residual = tokens.astype(jnp.float32)
    norm_one, unit_one, inv_one = norm_forward(residual, attn_full[2].astype(jnp.float32))
    normed_one = norm_one.astype(jnp.bfloat16)
    qkv = jnp.dot(normed_one, attn_full[0], preferred_element_type=jnp.float32)
    queries = rotate(qkv[:, :model_width].reshape(head_shape), cosine_table, sine_table).astype(
        jnp.bfloat16
    )
    key_heads = rotate(
        qkv[:, model_width : 2 * model_width].reshape(head_shape), cosine_table, sine_table
    ).astype(jnp.bfloat16)
    value_heads = qkv[:, 2 * model_width :].astype(jnp.bfloat16)
    q_items = to_items(queries, row_count, seq_len)
    k_items = to_items(key_heads, row_count, seq_len)
    v_items = to_items(value_heads, row_count, seq_len)
    mixed_items, log_total = lax.map(head_forward, (q_items, k_items, v_items, seg_items))
    mixed_out = from_items(mixed_items, row_count, seq_len)
    inner, unit_in, inv_in = norm_forward(mixed_out, attn_full[3].astype(jnp.float32))
    inner_low = inner.astype(jnp.bfloat16)
    after_attn = residual + jnp.dot(inner_low, attn_full[1], preferred_element_type=jnp.float32)
    ffn_full = (
        lax.all_gather(w_up, ("dp", "fsdp"), axis=0, tiled=True),
        lax.all_gather(w_down, ("dp", "fsdp"), axis=0, tiled=True),
        lax.all_gather(gain_ffn, ("dp", "fsdp"), axis=0, tiled=True),
        lax.all_gather(gain_mid, ("dp", "fsdp"), axis=0, tiled=True),
    )
    norm_two, unit_two, inv_two = norm_forward(after_attn, ffn_full[2].astype(jnp.float32))
    normed_two = norm_two.astype(jnp.bfloat16)
    hidden = jnp.dot(normed_two, ffn_full[0], preferred_element_type=jnp.float32)
    middle, unit_mid, inv_mid = norm_forward(gelu_value(hidden), ffn_full[3].astype(jnp.float32))
    middle_low = middle.astype(jnp.bfloat16)
    result = (
        after_attn + jnp.dot(middle_low, ffn_full[1], preferred_element_type=jnp.float32)
    ).astype(jnp.bfloat16)
    grad_out = cotangent.astype(jnp.float32) * valid_mask.reshape(-1, 1).astype(jnp.float32)
    ffn_back = (
        lax.all_gather(w_up, ("dp", "fsdp"), axis=0, tiled=True),
        lax.all_gather(w_down, ("dp", "fsdp"), axis=0, tiled=True),
        lax.all_gather(gain_ffn, ("dp", "fsdp"), axis=0, tiled=True),
        lax.all_gather(gain_mid, ("dp", "fsdp"), axis=0, tiled=True),
    )
    grad_low = grad_out.astype(jnp.bfloat16)
    grad_down = contract_rows(middle_low, grad_low)
    d_middle = against(grad_low, ffn_back[1])
    d_act, grad_mid = norm_backward(d_middle, ffn_back[3].astype(jnp.float32), unit_mid, inv_mid)
    d_hidden = (d_act * gelu_slope(hidden)).astype(jnp.bfloat16)
    grad_up = contract_rows(normed_two, d_hidden)
    d_two = against(d_hidden, ffn_back[0])
    d_after, grad_ffn = norm_backward(d_two, ffn_back[2].astype(jnp.float32), unit_two, inv_two)
    grad_after = grad_out + d_after
    attn_back = (
        lax.all_gather(w_qkv, ("dp", "fsdp"), axis=0, tiled=True),
        lax.all_gather(w_out, ("dp", "fsdp"), axis=0, tiled=True),
        lax.all_gather(gain_attn, ("dp", "fsdp"), axis=0, tiled=True),
        lax.all_gather(gain_inner, ("dp", "fsdp"), axis=0, tiled=True),
    )
    after_low = grad_after.astype(jnp.bfloat16)
    grad_wout = contract_rows(inner_low, after_low)
    d_inner = against(after_low, attn_back[1])
    d_mixed, grad_inner = norm_backward(d_inner, attn_back[3].astype(jnp.float32), unit_in, inv_in)
    dm_items = to_items(d_mixed.astype(jnp.bfloat16), row_count, seq_len)
    dq_items, dk_items, dv_items = lax.map(
        head_backward, (q_items, k_items, v_items, seg_items, log_total, dm_items)
    )
    d_query = unrotate(
        from_items(dq_items, row_count, seq_len).reshape(head_shape), cosine_table, sine_table
    ).reshape(row_count * seq_len, model_width)
    d_key = unrotate(
        from_items(dk_items, row_count, seq_len).reshape(head_shape), cosine_table, sine_table
    ).reshape(row_count * seq_len, model_width)
    d_value = from_items(dv_items, row_count, seq_len)
    d_qkv = jnp.concatenate([d_query, d_key, d_value], axis=1).astype(jnp.bfloat16)
    grad_qkv = contract_rows(normed_one, d_qkv)
    d_one = against(d_qkv, attn_back[0])
    d_residual, grad_attn = norm_backward(
        d_one, attn_back[2].astype(jnp.float32), unit_one, inv_one
    )
    grad_tokens = grad_after + d_residual
    summed = (
        lax.psum_scatter(grad_qkv, ("dp", "fsdp"), scatter_dimension=0, tiled=True),
        lax.psum_scatter(grad_wout, ("dp", "fsdp"), scatter_dimension=0, tiled=True),
        lax.psum_scatter(grad_up, ("dp", "fsdp"), scatter_dimension=0, tiled=True),
        lax.psum_scatter(grad_down, ("dp", "fsdp"), scatter_dimension=0, tiled=True),
        lax.psum_scatter(grad_attn, ("dp", "fsdp"), scatter_dimension=0, tiled=True),
        lax.psum_scatter(grad_inner, ("dp", "fsdp"), scatter_dimension=0, tiled=True),
        lax.psum_scatter(grad_ffn, ("dp", "fsdp"), scatter_dimension=0, tiled=True),
        lax.psum_scatter(grad_mid, ("dp", "fsdp"), scatter_dimension=0, tiled=True),
    )
    attn_grads = (summed[0], summed[1], summed[4], summed[5])
    ffn_grads = (summed[2], summed[3], summed[6], summed[7])
    return (
        result,
        grad_tokens,
        attn_grads[0],
        attn_grads[1],
        ffn_grads[0],
        ffn_grads[1],
        attn_grads[2],
        attn_grads[3],
        ffn_grads[2],
        ffn_grads[3],
    )


def solution(mesh):
    return jax.shard_map(
        local,
        mesh=mesh,
        in_specs=(
            P(("dp", "fsdp"), None),
            P(("dp", "fsdp"), None),
            P(("dp", "fsdp"), None),
            P(("dp", "fsdp"), None),
            P(("dp", "fsdp"), None),
            P(("dp", "fsdp"), None),
            P(("dp", "fsdp"), None),
            P(("dp", "fsdp")),
            P(("dp", "fsdp")),
            P(("dp", "fsdp")),
            P(("dp", "fsdp")),
        ),
        out_specs=(
            P(("dp", "fsdp"), None),
            P(("dp", "fsdp"), None),
            P(("dp", "fsdp"), None),
            P(("dp", "fsdp"), None),
            P(("dp", "fsdp"), None),
            P(("dp", "fsdp"), None),
            P(("dp", "fsdp")),
            P(("dp", "fsdp")),
            P(("dp", "fsdp")),
            P(("dp", "fsdp")),
        ),
        check_vma=False,
    )
```

profile of v0, /device:TPU:0, one launch (start us, length us, event | category | flops | bytes accessed | tf_op | source)
XLA Modules:
  0.0 911.2 jit_solution(14565054110536887641)
XLA Ops:
  15.0 42.6 %all-reduce.9 = (bf16[768]{0:T(1024)(128)(2,1)S(1)}, bf16[768]{0:T(1024)(128)(2,1)S(1)}, bf16[768]{0:T(1024)(128)(2,1)S(1)}, bf16[3072]{0:T(1024)(128)(2,1)S(1)}) all-reduce(bf16[768]{0:T(1024)(128)(2,1)S(1)} %dynamic-update-slice, bf16[768]{0:T(1024)(128)(2,1)S(1)} %dynamic-update-slice.1, ...), channel_id=1, replica_groups=mesh['dp'=4,'fsdp'=8] {'dp','fsdp'}, use_global_device_ids=true, to_apply=%add | all-reduce | flops 5376 | bytes 21504
  60.2 13.6 %all-gather.5.cloned.1.call-done = bf16[768,2304]{1,0:T(8,128)(2,1)} async-done(((bf16[24,2304]{1,0:T(8,128)(2,1)}), bf16[768,2304]{1,0:T(8,128)(2,1)}) %all-gather.5.cloned.1.call-update) | async-done | bytes 3538960 | tf_op jit(solution)/shard_map/all_gather | solution.py:191
  73.9 6.2 fusion.80
  103.1 109.7 %while.26 = (s32[]{:T(128)}, f32[12,1024,64]{1,2,0:T(8,128)S(1)}, f32[12,1024]{1,0:T(8,128)}, s32[12,1024]{1,0:T(8,128)S(1)}, bf16[12,1024,64]{2,1,0:T(8,128)(2,...) while((s32[]{:T(128)}, f32[12,1024,64]{1,2,0:T(8,128)S(1)}, ...), condition=%wide.region_8.9_spmd, body=%wide.region_5.8_spmd.sunk | while | flops 279968768 | bytes 30468224 | solution.py:210
  215.0 3.8 fusion.89
  220.8 12.8 %fusion.86 = (f32[1024]{0:T(1024)S(1)}, f32[1024,3072]{1,0:T(8,128)S(1)}, f32[1024,3072]{1,0:T(8,128)}) fusion(bf16[768,3072]{1,0:T(8,128)(2,1)} %all-gather.9.cloned.1.call-done, f32[1024,768]{0,1:T(8,128)} %copy-done.6, f32[768]{0:T(1024)S(1)} %convert_element_type.113, f32[1024]{0:T(1024)S(1)} %add_rsqrt_fusion.1, f32[1024]{0:T(1024)S(1)} %broadcast_multiply_fusion.9), kind=kOutput, calls=%fused_computation.161 | convolution fusion | flops 4850711552 | bytes 33045504 | tf_op jit(solution)/shard_map/dot_general | solution.py:223
  238.1 22.5 %all-gather.11.cloned.1.call-done = bf16[3072,768]{1,0:T(8,128)(2,1)} async-done(((bf16[96,768]{1,0:T(8,128)(2,1)}), bf16[3072,768]{1,0:T(8,128)(2,1)}) %all-gather.11.cloned.1.call-update) | async-done | bytes 4718608 | tf_op jit(solution)/shard_map/all_gather | solution.py:217
  260.6 25.5 %multiply_reduce_fusion.1 = (f32[3072]{0:T(1024)S(1)}, f32[1024]{0:T(1024)S(1)}, f32[1024]{0:T(1024)S(1)}, f32[1024,3072]{1,0:T(8,128)}) fusion(f32[1024,3072]{1,0:T(8,128)} %copy-done.1, f32[1024]{0:T(1024)S(1)} %add_rsqrt_fusion, f32[1024]{0:T(1024)S(1)} %broadcast_multiply_fusion.2, f32[3072]{0:T(1024)S(1)} %convert_element_type.115, ...), kind=kOutput, calls=%fused_computation.63 | convolution fusion | flops 4859358208 | bytes 31502336 | tf_op jit(solution)/shard_map/dot_general | solution.py:108
  286.2 18.3 %fusion.51 = (bf16[1024,3072]{1,0:T(8,128)(2,1)S(1)}, bf16[1024,3072]{1,0:T(8,128)(2,1)}) fusion(f32[1024,3072]{1,0:T(8,128)} %get-tuple-element.295, f32[1024,3072]{1,0:T(8,128)} %get-tuple-element.296, f32[1024,3072]{1,0:T(8,128)} %copy-done.1, f32[1024]{0:T(1024)S(1)} %broadcast_multiply_fusion, f32[1024]{0:T(1024)S(1)} %broadcast_multiply_fusion.1, ...), kind=kLoop, calls=%fused_computation.62 | loop fusion | flops 59768832 | bytes 50360320 | tf_op jit(solution)/shard_map/convert_element_type | solution.py:240
  304.5 9.4 %multiply_reduce_fusion.5 = (f32[768]{0:T(1024)S(1)}, f32[1024]{0:T(1024)S(1)}, f32[1024]{0:T(1024)S(1)}, f32[1024,768]{0,1:T(8,128)S(1)}) fusion(f32[1024,768]{0,1:T(8,128)S(1)} %copy-done.7, f32[1024]{0:T(1024)S(1)} %add_rsqrt_fusion.1, f32[1024]{0:T(1024)S(1)} %broadcast_multiply_fusion.9, f32[768]{0:T(1024)S(1)} %convert_element_type.113, ...), kind=kOutput, calls=%fused_computation.94 | convolution fusion | flops 4838126592 | bytes 17324032 | tf_op jit(solution)/shard_map/dot_general | solution.py:108
  319.6 4.1 multiply_reduce_fusion.6
  325.8 4.1 copy.75
  332.5 156.8 %while.27 = (s32[]{:T(128)}, f32[12,1024,64]{1,2,0:T(8,128)S(1)}, f32[12,1024,64]{1,2,0:T(8,128)}, bf16[12,1024,64]{1,2,0:T(8,128)(2,1)}, s32[12,1024]{1,0:T(8,1...) while((s32[]{:T(128)}, f32[12,1024,64]{1,2,0:T(8,128)S(1)}, ...), condition=%wide.region_23.24_spmd, body=%wide.region_21.23_spmd.sunk | while | flops 683801600 | bytes 34120820 | solution.py:256
  494.1 8.3 fusion.69
  504.3 10.5 %fusion.84 = f32[768,3072]{1,0:T(8,128)} fusion(bf16[1024,3072]{1,0:T(8,128)(2,1)} %copy-done.10, f32[1024,768]{0,1:T(8,128)S(1)} %copy-done.8, f32[768]{0:T(1024)S(1)} %convert_element_type.113, f32[1024]{0:T(1024)S(1)} %add_rsqrt_fusion.1, f32[1024]{0:T(1024)S(1)} %broadcast_multiply_fusion.9), kind=kOutput, calls=%fused_computation.159 | convolution fusion | flops 4834983936 | bytes 18885632 | tf_op jit(solution)/shard_map/dot_general | solution.py:102
  516.2 10.7 %fusion.71 = f32[3072,768]{1,0:T(8,128)} fusion(bf16[1024,3072]{1,0:T(8,128)(2,1)} %get-tuple-element.276, bf16[1024,768]{0,1:T(8,128)(2,1)S(1)} %copy-done.12, f32[1024]{0:T(1024)S(1)} %compare_convert_fusion), kind=kOutput, calls=%fused_computation.124 | convolution fusion | flops 4834197504 | bytes 17305600 | tf_op jit(solution)/shard_map/dot_general | solution.py:102
  526.9 10.2 %fusion.63 = (f32[768]{0:T(1024)S(1)}, f32[1024]{0:T(1024)S(1)}, f32[1024]{0:T(1024)S(1)}, f32[1024,768]{0,1:T(8,128)}) fusion(bf16[1024,768]{0,1:T(8,128)(2,1)} %copy-done.4, f32[1024]{0:T(1024)S(1)} %copy-done.25, f32[1024]{0:T(1024)S(1)} %copy-done.23, f32[768]{0:T(1024)S(1)} %copy-done.27, bf16[768,2304]{1,0:T(8,128)(2,1)} %all-gather.5.cloned.1.call-done, ...), kind=kOutput, calls=%fused_computation.86 | convolution fusion | flops 3645109504 | bytes 12998656 | tf_op jit(solution)/shard_map/dot_general | solution.py:108
  537.1 40.7 %all-reduce.8 = (f32[768]{0:T(1024)S(1)}, f32[768]{0:T(1024)S(1)}, f32[768]{0:T(1024)S(1)}, f32[3072]{0:T(1024)S(1)}) all-reduce(f32[768]{0:T(1024)S(1)} %get-tuple-element.222, f32[768]{0:T(1024)S(1)} %get-tuple-element.220, f32[768]{0:T(1024)S(1)} %get-tuple-element.218, ...), channel_id=6, replica_groups=mesh['dp'=4,'fsdp'=8] {'dp','fsdp'}, use_global_device_ids=true, to_apply=%region_31.32.clone | all-reduce | flops 5376 | bytes 43008
  579.6 5.0 fusion.62
  584.6 3.7 copy.80
  588.3 9.5 %add_convert_fusion = bf16[1024,768]{0,1:T(8,128)(2,1)} fusion(f32[1024,768]{0,1:T(8,128)S(1)} %copy-done.9, bf16[1024,3072]{1,0:T(8,128)(2,1)} %get-tuple-element.276, bf16[3072,768]{1,0:T(8,128)(2,1)} %all-gather.11.cloned.1.call-done), kind=kOutput, calls=%fused_computation.102 | convolution fusion | flops 4833411072 | bytes 15728640 | tf_op jit(solution)/shard_map/dot_general | solution.py:227
  601.0 19.7 %reduce-scatter.5.cloned.1.call-done = f32[24,2304]{1,0:T(8,128)} async-done(((f32[768,2304]{1,0:T(8,128)}), f32[24,2304]{1,0:T(8,128)}) %reduce-scatter.5.cloned.1.call-update) | async-done | bytes 221200 | tf_op jit(solution)/shard_map/reduce_scatter | solution.py:274
  620.7 141.1 %reduce-scatter.9.cloned.1.call-done = f32[24,3072]{1,0:T(8,128)} async-done(((f32[768,3072]{1,0:T(8,128)}), f32[24,3072]{1,0:T(8,128)}) %reduce-scatter.9.cloned.1.call-update) | async-done | bytes 294928 | tf_op jit(solution)/shard_map/reduce_scatter | solution.py:276
  761.7 142.2 %reduce-scatter.11.cloned.1.call-done = f32[96,768]{1,0:T(8,128)} async-done(((f32[3072,768]{1,0:T(8,128)}), f32[96,768]{1,0:T(8,128)}) %reduce-scatter.11.cloned.1.call-update) | async-done | bytes 294928 | tf_op jit(solution)/shard_map/reduce_scatter | solution.py:277
  (347 shorter events, 330.4 us)
Async XLA Ops:
  7.2 66.7 %all-gather.5.cloned.1.call-start = ((), (), s32[]{:S(2)}) async-start(), calls=%async_computation.4 | async-start | bytes 3649536 | tf_op jit(solution)/shard_map/all_gather | solution.py:191
  7.9 207.0 %all-gather.7.cloned.1.call-start = ((), (), s32[]{:S(2)}) async-start(), calls=%async_computation.5 | async-start | bytes 1216512 | tf_op jit(solution)/shard_map/all_gather | solution.py:192
  8.7 212.1 %all-gather.9.cloned.1.call-start = ((), (), s32[]{:S(2)}) async-start(), calls=%async_computation.6 | async-start | bytes 4866048 | tf_op jit(solution)/shard_map/all_gather | solution.py:216
  9.4 251.2 %all-gather.11.cloned.1.call-start = ((), (), s32[]{:S(2)}) async-start(), calls=%async_computation.7 | async-start | bytes 4866048 | tf_op jit(solution)/shard_map/all_gather | solution.py:217
  10.0 591.0 %reduce-scatter.7.cloned.1.call-start = ((), (), s32[]{:S(2)}) async-start(), calls=%async_computation.9 | async-start | bytes 2433024 | tf_op jit(solution)/shard_map/reduce_scatter | solution.py:275
  11.4 46.2 %copy-start.32 = (s32[1,8]{1,0:T(1,128)S(1)}, s32[1,8]{1,0:T(1,128)}, u32[]{:S(2)}) copy-start(s32[1,8]{1,0:T(1,128)} %param.16) | copy-start | bytes 100
  11.4 46.6 %copy-start.14 = (bf16[1024,768]{1,0:T(8,128)(2,1)S(1)}, bf16[1024,768]{1,0:T(8,128)(2,1)}, u32[]{:S(2)}) copy-start(bf16[1024,768]{1,0:T(8,128)(2,1)} %param.17) | copy-start | bytes 4718596
  13.3 60.6 %copy-start.4 = (bf16[1024,768]{0,1:T(8,128)(2,1)}, bf16[1024,768]{0,1:T(8,128)(2,1)S(1)}, u32[]{:S(2)}) copy-start(bf16[1024,768]{0,1:T(8,128)(2,1)S(1)} %copy.66) | copy-start | bytes 4718596
  13.5 66.5 %copy-start.22 = (f32[1024]{0:T(1024)}, f32[1024]{0:T(1024)S(1)}, u32[]{:S(2)}) copy-start(f32[1024]{0:T(1024)S(1)} %broadcast_multiply_fusion.11) | copy-start | bytes 12292
  14.0 66.0 %copy-start.24 = (f32[1024]{0:T(1024)}, f32[1024]{0:T(1024)S(1)}, u32[]{:S(2)}) copy-start(f32[1024]{0:T(1024)S(1)} %add_rsqrt_fusion.3) | copy-start | bytes 12292
  57.6 22.5 %copy-start.26 = (f32[768]{0:T(1024)}, f32[768]{0:T(1024)S(1)}, u32[]{:S(2)}) copy-start(f32[768]{0:T(1024)S(1)} %convert_element_type.108) | copy-start | bytes 9220
  60.2 30.2 %copy-start.18 = (f32[1024,32]{0,1:T(8,128)}, f32[1024,32]{0,1:T(8,128)S(1)}, u32[]{:S(2)}) copy-start(f32[1024,32]{0,1:T(8,128)S(1)} %get-tuple-element.291) | copy-start | bytes 393220
  60.2 30.2 %copy-start.20 = (f32[1024,32]{0,1:T(8,128)}, f32[1024,32]{0,1:T(8,128)S(1)}, u32[]{:S(2)}) copy-start(f32[1024,32]{0,1:T(8,128)S(1)} %get-tuple-element.292) | copy-start | bytes 393220
  233.6 4.5 copy-start.1
  286.2 18.3 %copy-start.7 = (f32[1024,768]{0,1:T(8,128)S(1)}, f32[1024,768]{0,1:T(8,128)}, u32[]{:S(2)}) copy-start(f32[1024,768]{0,1:T(8,128)} %copy-done.6) | copy-start | bytes 9437188
  304.5 9.5 %copy-start.10 = (bf16[1024,3072]{1,0:T(8,128)(2,1)}, bf16[1024,3072]{1,0:T(8,128)(2,1)S(1)}, u32[]{:S(2)}) copy-start(bf16[1024,3072]{1,0:T(8,128)(2,1)S(1)} %get-tuple-element.275) | copy-start | bytes 18874372
  304.5 9.5 %copy-start.11 = (bf16[1024,768]{0,1:T(8,128)(2,1)S(1)}, bf16[1024,768]{0,1:T(8,128)(2,1)}, u32[]{:S(2)}) copy-start(bf16[1024,768]{0,1:T(8,128)(2,1)} %copy.74) | copy-start | bytes 4718596
  330.0 290.7 %reduce-scatter.5.cloned.1.call-start = ((), (), s32[]{:S(2)}) async-start(), calls=%async_computation.8 | async-start | bytes 7299072 | tf_op jit(solution)/shard_map/reduce_scatter | solution.py:274
  332.5 156.8 %copy-start.19 = (f32[1024,32]{0,1:T(8,128)S(1)}, f32[1024,32]{0,1:T(8,128)}, u32[]{:S(2)}) copy-start(f32[1024,32]{0,1:T(8,128)} %copy-done.18) | copy-start | bytes 393220
  332.5 156.8 %copy-start.21 = (f32[1024,32]{0,1:T(8,128)S(1)}, f32[1024,32]{0,1:T(8,128)}, u32[]{:S(2)}) copy-start(f32[1024,32]{0,1:T(8,128)} %copy-done.20) | copy-start | bytes 393220
  502.4 259.3 %reduce-scatter.9.cloned.1.call-start = ((), (), s32[]{:S(2)}) async-start(), calls=%async_computation.10 | async-start | bytes 9732096 | tf_op jit(solution)/shard_map/reduce_scatter | solution.py:276
  514.8 389.2 %reduce-scatter.11.cloned.1.call-start = ((), (), s32[]{:S(2)}) async-start(), calls=%async_computation.11 | async-start | bytes 9732096 | tf_op jit(solution)/shard_map/reduce_scatter | solution.py:277
  526.9 52.7 %copy-start.3 = (f32[1024,768]{0,1:T(8,128)S(1)}, f32[1024,768]{0,1:T(8,128)}, u32[]{:S(2)}) copy-start(f32[1024,768]{0,1:T(8,128)} %copy-done.2) | copy-start | bytes 9437188
  584.6 3.7 copy-start.9
  (28 other events, 57.8 us)
Sparse Core Ops, SparseCore 0:
  10.9 62.9 all-gather.4
  76.8 52.9 all-gather.6
  132.7 62.5 all-gather.8
  198.1 62.4 all-gather.10
  330.1 97.9 reduce-scatter.6
  502.5 118.0 reduce-scatter.4
  627.1 134.5 reduce-scatter.8
  769.2 134.6 reduce-scatter.10
where the time goes:
time: 918 us; the launch traced here: 911 us
  waiting for transfers between devices  342 us (37%)
  matrix products  309 us (34%)
  local copies, waits for them, and re-layouts  99.7 us (11%)
  blocking collectives  83.3 us (9%)
  other arithmetic  61.1 us (7%)
  between operations  15.1 us (2%)
    reduce_scatter x1, waiting for transfers between devices, local(): lax.psum_scatter(grad_down, ('dp', 'fsdp'), scatter_dimension=0, tiled=True)  142 us
    reduce_scatter x1, waiting for transfers between devices, local(): lax.psum_scatter(grad_up, ('dp', 'fsdp'), scatter_dimension=0, tiled=True)  141 us
    dot_general x28, matrix products, contract_rows(): lax.dot_general(left_side, right_side, (((0,), (0,)), ((), ())), preferre...  90 us
    unnamed x2, blocking collectives  83.3 us
    dot_general x24, matrix products, head_scores(): jnp.einsum('qd,kd->qk', queries, key_rows, preferred_element_type=jnp.flo...  61.3 us
    dot_general x4, matrix products, against(): lax.dot_general(grad_in, weight_mat, (((1,), (1,)), ((), ())), preferred_...  49.3 us
    dot_general x12, matrix products, head_forward(): jnp.dot(attn_probs, value_rows, preferred_element_type=jnp.float32)  37.2 us
    unnamed x80, local copies, waits for them, and re-layouts  24.2 us
  transfers between devices with their start and end apart: 8, of which 5 were waited for; matrix products, arithmetic and copies ran while one was open for 40% of the time, Pallas kernels for 0%

commit v1 on v0

v1 whole, which is shorter than its diff:
```python
import functools
import math

import jax
import jax.numpy as jnp
from jax import lax
from jax.experimental import pallas as pl
from jax.experimental.pallas import tpu as pltpu
from jax.sharding import PartitionSpec as P

HEADS = 12
HEAD_DIM = 64
PAIR = 2 * HEAD_DIM
PAIRS = HEADS // 2
EPSILON = 1e-05
MASKED_SCORE = -1e30
ROOT_HALF = 0.7071067811865476
INV_ROOT_TAU = 0.3989422804014327
BF = jnp.bfloat16
F32 = jnp.float32
MIB = 1 << 20
AXES = ("dp", "fsdp")
BLOCK = 256


def dot(a, b, dims=((1,), (0,))):
    return lax.dot_general(a, b, (dims, ((), ())), preferred_element_type=F32)


def params(mib):
    return pltpu.CompilerParams(vmem_limit_bytes=mib * MIB)


def swap_halves(x):
    lane = lax.broadcasted_iota(jnp.int32, x.shape, 1)
    low = lax.rem(lane, HEAD_DIM) < HEAD_DIM // 2
    half = HEAD_DIM // 2
    return jnp.where(low, pltpu.roll(x, PAIR - half, 1), pltpu.roll(x, half, 1))


def unit_norm(x):
    mean = jnp.mean(x, axis=-1, keepdims=True)
    centred = x - mean
    inv = lax.rsqrt(jnp.mean(centred * centred, axis=-1, keepdims=True) + EPSILON)
    return centred * inv, inv


def norm_back(grad, gain, unit, inv):
    d_unit = grad * gain
    return inv * (
        d_unit
        - jnp.mean(d_unit, axis=-1, keepdims=True)
        - unit * jnp.mean(d_unit * unit, axis=-1, keepdims=True)
    )


def whole(shape):
    return pl.BlockSpec(shape, lambda *_: (0,) * len(shape), pipeline_mode=pl.Buffered(1))


def rows(width, block=BLOCK):
    return pl.BlockSpec((block, width), lambda i: (i, 0))


def shaped(shape, dtype):
    return jax.ShapeDtypeStruct(shape, dtype)


def qkv_kernel(x_ref, w_ref, gain_ref, cos_ref, sin_ref, h_ref, qkv_ref):
    unit, _ = unit_norm(x_ref[...].astype(F32))
    h = (unit * gain_ref[...]).astype(BF)
    h_ref[...] = h
    cos, sin = cos_ref[...], sin_ref[...]
    width = h.shape[1]
    for part in range(3):
        y = dot(h, w_ref[:, part * width : (part + 1) * width])
        for c in range(width // PAIR):
            z = y[:, c * PAIR : (c + 1) * PAIR]
            if part < 2:
                z = z * cos + swap_halves(z) * sin
            if part == 0:
                z = z * (1.0 / math.sqrt(HEAD_DIM))
            at = part * width + c * PAIR
            qkv_ref[:, at : at + PAIR] = z.astype(BF)


def qkv_forward(tokens, w_qkv, gain, cos, sin):
    t, d = tokens.shape
    n = w_qkv.shape[1]
    return pl.pallas_call(
        qkv_kernel,
        grid=(t // BLOCK,),
        in_specs=[rows(d), whole((d, n)), whole((1, d)), rows(PAIR), rows(PAIR)],
        out_specs=[rows(d), rows(n)],
        out_shape=[shaped((t, d), BF), shaped((t, n), BF)],
        compiler_params=params(48),
        cost_estimate=pl.CostEstimate(
            flops=2 * t * d * n, transcendentals=0, bytes_accessed=2 * d * n + 12 * t * d
        ),
        name="qkv_forward",
    )(tokens, w_qkv, gain, cos, sin)


def window(i, n):
    return slice((i - n + 1) * BLOCK, (i + 1) * BLOCK)


def head_masks(shape):
    lane = lax.broadcasted_iota(jnp.int32, shape, 1)
    return lane < HEAD_DIM


def attention_forward_kernel(wide, reach, q_ref, k_ref, v_ref, start_ref, o_ref, lse_ref, bias):
    row, pair = pl.program_id(0), pl.program_id(1)
    seq = q_ref.shape[0]
    blocks = seq // BLOCK

    @pl.when(pair == 0)
    def _():
        for i in range(blocks):
            at = slice(i * BLOCK, (i + 1) * BLOCK)
            shape = (BLOCK, wide * BLOCK)
            key = (i - wide + 1) * BLOCK + lax.broadcasted_iota(jnp.int32, shape, 1)
            query = i * BLOCK + lax.broadcasted_iota(jnp.int32, shape, 0)
            keep = (key >= start_ref[at, :]) & (key <= query)
            bias[at, :] = jnp.where(keep, 0.0, MASKED_SCORE)

    first = head_masks((BLOCK, PAIR))
    for i in range(blocks):
        at = slice(i * BLOCK, (i + 1) * BLOCK)
        most = min(wide, i + 1)
        for n in range(1, most + 1):

            @pl.when(reach[row * blocks + i] == n)
            def _():
                q = q_ref[at, :]
                w = window(i, n)
                k, v = k_ref[w, :], v_ref[w, :]
                b = bias[at, (wide - n) * BLOCK :]
                mask = head_masks(k.shape)
                zero = jnp.zeros_like(k)
                total, lses = None, []
                scale = None
                for h in range(2):
                    pick = mask if h == 0 else jnp.logical_not(mask)
                    s = dot(q, jnp.where(pick, k, zero), ((1,), (1,))) + b
                    top = jnp.max(s, axis=-1, keepdims=True)
                    p = jnp.exp(s - top)
                    den = jnp.sum(p, axis=-1, keepdims=True)
                    probs = (p * (1.0 / den)).astype(BF)
                    part = dot(probs, jnp.where(pick, v, zero))
                    total = part if total is None else total + part
                    lses.append(top + jnp.log(den))
                o_ref[at, :] = total
                both = jnp.where(first, lses[0], lses[1]).T
                lse_ref[0, 0:1, at] = both[0:1, :]
                lse_ref[0, 1:2, at] = both[HEAD_DIM : HEAD_DIM + 1, :]


def attention_forward(reach, qkv, start, row_count, wide):
    t = qkv.shape[0]
    seq = t // row_count
    d = qkv.shape[1] // 3

    def columns(part):
        return pl.BlockSpec((seq, PAIR), lambda r, p, *_: (r, part * PAIRS + p))

    return pl.pallas_call(
        functools.partial(attention_forward_kernel, wide),
        grid_spec=pltpu.PrefetchScalarGridSpec(
            num_scalar_prefetch=1,
            grid=(row_count, PAIRS),
            in_specs=[
                columns(0),
                columns(1),
                columns(2),
                pl.BlockSpec((seq, 1), lambda r, p, *_: (r, 0)),
            ],
            out_specs=[
                pl.BlockSpec((seq, PAIR), lambda r, p, *_: (r, p)),
                pl.BlockSpec((1, 8, seq), lambda r, p, *_: (r * PAIRS + p, 0, 0)),
            ],
            scratch_shapes=[pltpu.VMEM((seq, wide * BLOCK), F32)],
        ),
        out_shape=[shaped((t, d), F32), shaped((row_count * PAIRS, 8, seq), F32)],
        compiler_params=params(32),
        cost_estimate=pl.CostEstimate(
            flops=8 * t * d * BLOCK, transcendentals=t * HEADS * 512, bytes_accessed=12 * t * d
        ),
        name="attention_forward",
    )(reach, qkv, qkv, qkv, start)


def attention_backward_kernel(
    wide, reach, q_ref, k_ref, v_ref, do_ref, o_ref, lse_ref, start_ref, cos_ref, sin_ref,
    dq_ref, dk_ref, dv_ref, bias, ks, vs, qs, dos, dk_acc, dv_acc, dq_acc,
):
    row, pair = pl.program_id(0), pl.program_id(1)
    seq = q_ref.shape[0]
    blocks = seq // BLOCK

    @pl.when(pair == 0)
    def _():
        for i in range(blocks):
            at = slice(i * BLOCK, (i + 1) * BLOCK)
            shape = (wide * BLOCK, BLOCK)
            key = (i - wide + 1) * BLOCK + lax.broadcasted_iota(jnp.int32, shape, 0)
            query = i * BLOCK + lax.broadcasted_iota(jnp.int32, shape, 1)
            keep = (key >= start_ref[0:1, at]) & (key <= query)
            bias[:, at] = jnp.where(keep, 0.0, MASKED_SCORE)

    mask = head_masks((seq, PAIR))
    for src, dst in ((k_ref, ks), (v_ref, vs), (q_ref, qs), (do_ref, dos)):
        x = src[...]
        zero = jnp.zeros_like(x)
        dst[0] = jnp.where(mask, x, zero)
        dst[1] = jnp.where(mask, zero, x)
    dk_acc[...] = jnp.zeros_like(dk_acc)
    dv_acc[...] = jnp.zeros_like(dv_acc)
    lane8 = lax.broadcasted_iota(jnp.int32, (8, PAIR), 1) // HEAD_DIM
    row8 = lax.broadcasted_iota(jnp.int32, (8, PAIR), 0)
    picks = (lane8 == row8).astype(F32)
    delta = lax.dot_general(
        picks, do_ref[...].astype(F32) * o_ref[...], (((1,), (1,)), ((), ())),
        precision=lax.Precision.HIGHEST, preferred_element_type=F32,
    )
    for i in range(blocks):
        at = slice(i * BLOCK, (i + 1) * BLOCK)
        most = min(wide, i + 1)
        for n in range(1, most + 1):

            @pl.when(reach[row * blocks + i] == n)
            def _():
                w = window(i, n)
                b = bias[(wide - n) * BLOCK :, at]
                q, do = q_ref[at, :], do_ref[at, :]
                ps, dss = [], []
                for h in range(2):
                    s = dot(ks[h, w, :], q, ((1,), (1,))) + b
                    p = jnp.exp(s - lse_ref[0, h : h + 1, at])
                    dp = dot(vs[h, w, :], do, ((1,), (1,)))
                    ds = (p * (dp - delta[h : h + 1, at])).astype(BF)
                    ps.append(p.astype(BF))
                    dss.append(ds)
                dv_acc[w, :] += dot(ps[0], dos[0, at, :]) + dot(ps[1], dos[1, at, :])
                dk_acc[w, :] += dot(dss[0], qs[0, at, :]) + dot(dss[1], qs[1, at, :])
                dq_acc[at, :] = dot(dss[0], ks[0, w, :], ((0,), (0,))) + dot(
                    dss[1], ks[1, w, :], ((0,), (0,))
                )

    cos, sin = cos_ref[...], sin_ref[...]
    dq = dq_acc[...] * (1.0 / math.sqrt(HEAD_DIM))
    dk = dk_acc[...]
    dq_ref[...] = (dq * cos - swap_halves(dq) * sin).astype(BF)
    dk_ref[...] = (dk * cos - swap_halves(dk) * sin).astype(BF)
    dv_ref[...] = dv_acc[...].astype(BF)


def attention_backward(reach, qkv, d_mixed, mixed, lse, start_row, cos, sin, row_count, wide):
    t = qkv.shape[0]
    seq = t // row_count
    d = qkv.shape[1] // 3

    def columns(part):
        return pl.BlockSpec((seq, PAIR), lambda r, p, *_: (r, part * PAIRS + p))

    table = pl.BlockSpec((seq, PAIR), lambda r, p, *_: (r, 0))
    return pl.pallas_call(
        functools.partial(attention_backward_kernel, wide),
        grid_spec=pltpu.PrefetchScalarGridSpec(
            num_scalar_prefetch=1,
            grid=(row_count, PAIRS),
            in_specs=[
                columns(0), columns(1), columns(2), columns(0), columns(0),
                pl.BlockSpec((1, 8, seq), lambda r, p, *_: (r * PAIRS + p, 0, 0)),
                pl.BlockSpec((8, seq), lambda r, p, *_: (r, 0)),
                table, table,
            ],
            out_specs=[columns(0)] * 3,
            scratch_shapes=[
                pltpu.VMEM((wide * BLOCK, seq), F32),
                pltpu.VMEM((2, seq, PAIR), BF),
                pltpu.VMEM((2, seq, PAIR), BF),
                pltpu.VMEM((2, seq, PAIR), BF),
                pltpu.VMEM((2, seq, PAIR), BF),
                pltpu.VMEM((seq, PAIR), F32),
                pltpu.VMEM((seq, PAIR), F32),
                pltpu.VMEM((seq, PAIR), F32),
            ],
        ),
        out_shape=[shaped((t, d), BF)] * 3,
        compiler_params=params(40),
        cost_estimate=pl.CostEstimate(
            flops=20 * t * d * BLOCK, transcendentals=t * HEADS * 512, bytes_accessed=20 * t * d
        ),
        name="attention_backward",
    )(reach, qkv, qkv, qkv, d_mixed, mixed, lse, start_row, cos, sin)


def up_kernel(o_ref, x_ref, wo_ref, wu_ref, gi_ref, gf_ref, gm_ref,
              a_ref, x1_ref, h2_ref, m_ref, slope_ref, inv_ref):
    unit, _ = unit_norm(o_ref[...])
    a = (unit * gi_ref[...]).astype(BF)
    a_ref[...] = a
    x1 = x_ref[...].astype(F32) + dot(a, wo_ref[...])
    x1_ref[...] = x1
    unit, _ = unit_norm(x1)
    h2 = (unit * gf_ref[...]).astype(BF)
    h2_ref[...] = h2
    hidden = dot(h2, wu_ref[...])
    cdf = 0.5 + 0.5 * lax.erf(hidden * ROOT_HALF)
    slope = cdf + hidden * (jnp.exp(-0.5 * hidden * hidden) * INV_ROOT_TAU)
    slope_ref[...] = slope.astype(BF)
    unit, inv = unit_norm(hidden * cdf)
    m_ref[...] = (unit * gm_ref[...]).astype(BF)
    inv_ref[...] = jnp.broadcast_to(inv, inv_ref.shape)


def up_forward(mixed, tokens, w_out, w_up, gain_inner, gain_ffn, gain_mid):
    t, d = tokens.shape
    f = w_up.shape[1]
    return pl.pallas_call(
        up_kernel,
        grid=(t // BLOCK,),
        in_specs=[rows(d), rows(d), whole((d, d)), whole((d, f)), whole((1, d)), whole((1, d)), whole((1, f))],
        out_specs=[rows(d), rows(d), rows(d), rows(f), rows(f), rows(PAIR)],
        out_shape=[
            shaped((t, d), BF), shaped((t, d), F32), shaped((t, d), BF),
            shaped((t, f), BF), shaped((t, f), BF), shaped((t, PAIR), F32),
        ],
        compiler_params=params(56),
        cost_estimate=pl.CostEstimate(
            flops=2 * t * d * (d + f), transcendentals=2 * t * f, bytes_accessed=2 * d * (d + f) + 4 * t * f + 14 * t * d
        ),
        name="up_forward",
    )(mixed, tokens, w_out, w_up, gain_inner, gain_ffn, gain_mid)


def down_kernel(m_ref, slope_ref, inv_ref, x1_ref, ct_ref, valid_ref, wd_ref, gm_ref,
                y_ref, dpre_ref, gwd_ref, gg_ref):
    step = pl.program_id(0)
    m = m_ref[...]
    y_ref[...] = (x1_ref[...] + dot(m, wd_ref[...])).astype(BF)
    gy = jnp.where(valid_ref[...] > 0, ct_ref[...], jnp.zeros_like(ct_ref))
    part = dot(m, gy, ((0,), (0,)))
    dm = dot(gy, wd_ref[...], ((1,), (1,)))
    gain = gm_ref[...]
    mf = m.astype(F32)
    prod = dm * mf
    d_unit = dm * gain
    d_act = inv_ref[:, 0:1] * (
        d_unit
        - jnp.mean(d_unit, axis=-1, keepdims=True)
        - (mf * (1.0 / gain)) * jnp.mean(prod, axis=-1, keepdims=True)
    )
    dpre_ref[...] = (d_act * slope_ref[...].astype(F32)).astype(BF)
    gain_part = jnp.sum(prod, axis=0, keepdims=True) * (1.0 / gain)

    @pl.when(step == 0)
    def _():
        gwd_ref[...] = part
        gg_ref[...] = gain_part

    @pl.when(step > 0)
    def _():
        gwd_ref[...] += part
        gg_ref[...] += gain_part


def down_both(m, slope, inv, x1, cotangent, valid, w_down, gain_mid):
    t, d = x1.shape
    f = m.shape[1]
    return pl.pallas_call(
        down_kernel,
        grid=(t // BLOCK,),
        in_specs=[rows(f), rows(f), rows(PAIR), rows(d), rows(d), rows(1), whole((f, d)), whole((1, f))],
        out_specs=[rows(d), rows(f), whole((f, d)), whole((1, f))],
        out_shape=[shaped((t, d), BF), shaped((t, f), BF), shaped((f, d), F32), shaped((1, f), F32)],
        compiler_params=params(60),
        cost_estimate=pl.CostEstimate(
            flops=6 * t * d * f, transcendentals=0, bytes_accessed=6 * d * f + 6 * t * f + 8 * t * d
        ),
        name="down_both",
    )(m, slope, inv, x1, cotangent, valid, w_down, gain_mid)


def up_back_kernel(dpre_ref, h2_ref, x1_ref, ct_ref, valid_ref, a_ref, o_ref, wu_ref, wo_ref, gf_ref, gi_ref,
                   dx1_ref, do_ref, gwu_ref, gwo_ref, ggf_ref, ggi_ref):
    step = pl.program_id(0)
    dpre = dpre_ref[...]
    part_up = dot(h2_ref[...], dpre, ((0,), (0,)))
    dh2 = dot(dpre, wu_ref[...], ((1,), (1,)))
    unit, inv = unit_norm(x1_ref[...])
    ffn_part = jnp.sum(dh2 * unit, axis=0, keepdims=True)
    gy = jnp.where(valid_ref[...] > 0, ct_ref[...].astype(F32), 0.0)
    dx1 = gy + norm_back(dh2, gf_ref[...], unit, inv)
    dx1_ref[...] = dx1
    low = dx1.astype(BF)
    part_out = dot(a_ref[...], low, ((0,), (0,)))
    da = dot(low, wo_ref[...], ((1,), (1,)))
    unit, inv = unit_norm(o_ref[...])
    inner_part = jnp.sum(da * unit, axis=0, keepdims=True)
    do_ref[...] = norm_back(da, gi_ref[...], unit, inv).astype(BF)

    @pl.when(step == 0)
    def _():
        gwu_ref[...] = part_up
        gwo_ref[...] = part_out
        ggf_ref[...] = ffn_part
        ggi_ref[...] = inner_part

    @pl.when(step > 0)
    def _():
        gwu_ref[...] += part_up
        gwo_ref[...] += part_out
        ggf_ref[...] += ffn_part
        ggi_ref[...] += inner_part


def up_backward(dpre, h2, x1, cotangent, valid, a, mixed, w_up, w_out, gain_ffn, gain_inner):
    t, d = x1.shape
    f = dpre.shape[1]
    return pl.pallas_call(
        up_back_kernel,
        grid=(t // BLOCK,),
        in_specs=[rows(f), rows(d), rows(d), rows(d), rows(1), rows(d), rows(d),
                  whole((d, f)), whole((d, d)), whole((1, d)), whole((1, d))],
        out_specs=[rows(d), rows(d), whole((d, f)), whole((d, d)), whole((1, d)), whole((1, d))],
        out_shape=[shaped((t, d), F32), shaped((t, d), BF), shaped((d, f), F32), shaped((d, d), F32),
                   shaped((1, d), F32), shaped((1, d), F32)],
        compiler_params=params(60),
        cost_estimate=pl.CostEstimate(
            flops=4 * t * d * (d + f), transcendentals=0, bytes_accessed=6 * d * (d + f) + 2 * t * f + 24 * t * d
        ),
        name="up_backward",
    )(dpre, h2, x1, cotangent, valid, a, mixed, w_up, w_out, gain_ffn, gain_inner)


def qkv_grad_kernel(h_ref, dq_ref, dk_ref, dv_ref, g_ref):
    step = pl.program_id(0)
    h = h_ref[...]
    d = h.shape[1]
    for c, ref in enumerate((dq_ref, dk_ref, dv_ref)):
        part = dot(h, ref[...], ((0,), (0,)))
        cols = slice(c * d, (c + 1) * d)

        @pl.when(step == 0)
        def _():
            g_ref[:, cols] = part

        @pl.when(step > 0)
        def _():
            g_ref[:, cols] += part


def qkv_weight_grad(h, dq, dk, dv):
    t, d = h.shape
    return pl.pallas_call(
        qkv_grad_kernel,
        grid=(t // BLOCK,),
        in_specs=[rows(d)] * 4,
        out_specs=whole((d, 3 * d)),
        out_shape=shaped((d, 3 * d), F32),
        compiler_params=params(40),
        cost_estimate=pl.CostEstimate(flops=6 * t * d * d, transcendentals=0, bytes_accessed=12 * d * d + 8 * t * d),
        name="qkv_weight_grad",
    )(h, dq, dk, dv)


def qkv_back_kernel(dq_ref, dk_ref, dv_ref, x_ref, dx1_ref, w_ref, gain_ref, dx_ref, gg_ref):
    step = pl.program_id(0)
    d = x_ref.shape[1]
    dh = None
    for c, ref in enumerate((dq_ref, dk_ref, dv_ref)):
        part = dot(ref[...], w_ref[:, c * d : (c + 1) * d], ((1,), (1,)))
        dh = part if dh is None else dh + part
    unit, inv = unit_norm(x_ref[...].astype(F32))
    gain_part = jnp.sum(dh * unit, axis=0, keepdims=True)
    dx_ref[...] = dx1_ref[...] + norm_back(dh, gain_ref[...], unit, inv)

    @pl.when(step == 0)
    def _():
        gg_ref[...] = gain_part

    @pl.when(step > 0)
    def _():
        gg_ref[...] += gain_part


def qkv_backward(dq, dk, dv, tokens, dx1, w_qkv, gain):
    t, d = tokens.shape
    return pl.pallas_call(
        qkv_back_kernel,
        grid=(t // BLOCK,),
        in_specs=[rows(d)] * 5 + [whole((d, 3 * d)), whole((1, d))],
        out_specs=[rows(d), whole((1, d))],
        out_shape=[shaped((t, d), F32), shaped((1, d), F32)],
        compiler_params=params(48),
        cost_estimate=pl.CostEstimate(flops=6 * t * d * d, transcendentals=0, bytes_accessed=6 * d * d + 16 * t * d),
        name="qkv_backward",
    )(dq, dk, dv, tokens, dx1, w_qkv, gain)


def layout(doc_lengths, seq):
    docs = doc_lengths.shape[-1]
    upto = jnp.arange(docs)[:, None] <= jnp.arange(docs)[None, :]
    ends = jnp.sum(jnp.where(upto[None], doc_lengths[:, :, None], 0), axis=1)
    places = jnp.arange(seq, dtype=jnp.int32)
    passed = places[None, :, None] >= ends[:, None, :]
    start = jnp.sum(jnp.where(passed, doc_lengths[:, None, :], 0), axis=-1)
    valid = places[None, :] < ends[:, docs - 2 : docs - 1]
    return start.astype(jnp.int32), places[None, :] - start, valid


def tables(position):
    half = HEAD_DIM // 2
    lane = jnp.arange(PAIR)
    frequency = jnp.exp((lane % half).astype(F32) * (-2.0 * math.log(10000.0) / HEAD_DIM))
    angles = position.reshape(-1, 1).astype(F32) * frequency[None, :]
    sign = jnp.where(lane % HEAD_DIM < half, -1.0, 1.0)
    return jnp.cos(angles), jnp.sin(angles) * sign[None, :]


def gather(x):
    return lax.all_gather(x, AXES, axis=0, tiled=True)


def scatter(g):
    return lax.psum_scatter(g, AXES, scatter_dimension=0, tiled=True)


def local(tokens, doc_lengths, cotangent, w_qkv, w_out, w_up, w_down,
          gain_attn, gain_inner, gain_ffn, gain_mid):
    row_count = doc_lengths.shape[0]
    seq = tokens.shape[0] // row_count
    wide = min(seq, 512) // BLOCK + 1
    blocks = seq // BLOCK
    start, position, valid = layout(doc_lengths, seq)
    cos, sin = tables(position)
    firsts = start[:, ::BLOCK] // BLOCK
    reach = (jnp.arange(blocks, dtype=jnp.int32)[None, :] - firsts + 1).reshape(-1)
    start_col = start.reshape(-1, 1)
    start_row = jnp.repeat(start, 8, axis=0)
    valid_col = valid.astype(jnp.int32).reshape(-1, 1)

    f_qkv, f_out, f_up, f_down = (gather(w) for w in (w_qkv, w_out, w_up, w_down))
    g_attn, g_inner, g_ffn, g_mid = (
        gather(g).astype(F32).reshape(1, -1) for g in (gain_attn, gain_inner, gain_ffn, gain_mid)
    )
    h1, qkv = qkv_forward(tokens, f_qkv, g_attn, cos, sin)
    mixed, lse = attention_forward(reach, qkv, start_col, row_count, wide)
    a, x1, h2, m, slope, inv = up_forward(mixed, tokens, f_out, f_up, g_inner, g_ffn, g_mid)
    result, dpre, grad_down, grad_mid = down_both(m, slope, inv, x1, cotangent, valid_col, f_down, g_mid)
    dx1, d_mixed, grad_up, grad_out, grad_ffn, grad_inner = up_backward(
        dpre, h2, x1, cotangent, valid_col, a, mixed, f_up, f_out, g_ffn, g_inner
    )
    dq, dk, dv = attention_backward(reach, qkv, d_mixed, mixed, lse, start_row, cos, sin, row_count, wide)
    grad_qkv = qkv_weight_grad(h1, dq, dk, dv)
    grad_tokens, grad_attn = qkv_backward(dq, dk, dv, tokens, dx1, f_qkv, g_attn)
    weights = tuple(scatter(g.astype(BF)).astype(F32) for g in (grad_qkv, grad_out, grad_up, grad_down))
    gains = tuple(scatter(g.reshape(-1)) for g in (grad_attn, grad_inner, grad_ffn, grad_mid))
    return (result, grad_tokens) + weights + gains


def solution(mesh):
    matrix, vector = P(AXES, None), P(AXES)
    return jax.shard_map(
        local,
        mesh=mesh,
        in_specs=(matrix,) * 7 + (vector,) * 4,
        out_specs=(matrix,) * 6 + (vector,) * 4,
        check_vma=False,
    )
```

time: 918 us -> 772 us (0.84)
  matrix products: 309 us -> 0 us
  Pallas kernels: 0 us -> 169 us
  waiting for transfers between devices: 342 us -> 445 us
  local copies, waits for them, and re-layouts: 99.7 us -> 21.2 us
  other arithmetic: 61.1 us -> 30 us
    dot_general x96 -> x0, matrix products: 309 us -> none  [the longest x28 90 us: contract_rows(): lax.dot_general(left_side, right_side, (((0,), (0,)), ((), ())), preferre...]
    pallas_call x0 -> x8, Pallas kernels: none -> 169 us  [the longest x1 35 us: attention_backward(): pl.pallas_call(functools.partial(attention_backward_kernel, wide), grid_s...]
    all_gather x4, waiting for transfers between devices: 36.2 us -> 140 us  [gather(): return lax.all_gather(x, AXES, axis=0, tiled=True)]
    while x27 -> x0, local copies, waits for them, and re-layouts: 31.2 us -> none
    dynamic_update_slice x12 -> x0, local copies, waits for them, and re-layouts: 16.8 us -> none  [local(): lax.map(head_forward, (q_items, k_items, v_items, seg_items))]
    slice x5 -> x2, local copies, waits for them, and re-layouts: 11.1 us -> 0.68 us  [the longest x1 0.58 us: layout(): valid = places[None, :] < ends[:, docs - 2:docs - 1]]
    convert_element_type x21 -> x10, other arithmetic: 35.5 us -> 26 us  [the longest x4 18.2 us: local(): g.astype(BF)]
    dynamic_slice x36 -> x0, local copies, waits for them, and re-layouts: 9.47 us -> none  [the longest x12 9.25 us: local(): lax.map(head_backward, (q_items, k_items, v_items, seg_items, log_total,...]
  transfers between devices with their start and end apart: 8 -> 8, of which waited for: 5 -> 7; matrix products, arithmetic and copies ran while one was open for 40% -> 4% of each run, Pallas kernels for 0% -> 14%
where the time goes in v1:
time: 772 us; the launch traced here: 763 us
  waiting for transfers between devices  445 us (58%)
  Pallas kernels  169 us (22%)
  blocking collectives  82.3 us (11%)
  other arithmetic  30 us (4%)
  local copies, waits for them, and re-layouts  21.2 us (3%)
  between operations  14.6 us (2%)
    reduce_scatter x4, waiting for transfers between devices, scatter(): return lax.psum_scatter(g, AXES, scatter_dimension=0, tiled=True)  303 us
    all_gather x4, waiting for transfers between devices, gather(): return lax.all_gather(x, AXES, axis=0, tiled=True)  140 us
    unnamed x2, blocking collectives  82.3 us
    pallas_call x1, Pallas kernels, attention_backward(): pl.pallas_call(functools.partial(attention_backward_kernel, wide), grid_s...  35 us
    pallas_call x1, Pallas kernels, down_both(): pl.pallas_call(down_kernel, grid=(t // BLOCK,), in_specs=[rows(f), rows(f...  32.3 us
    pallas_call x1, Pallas kernels, up_backward(): pl.pallas_call(up_back_kernel, grid=(t // BLOCK,), in_specs=[rows(f), row...  32.2 us
    pallas_call x1, Pallas kernels, attention_forward(): pl.pallas_call(functools.partial(attention_forward_kernel, wide), grid_sp...  21.6 us
    pallas_call x1, Pallas kernels, up_forward(): pl.pallas_call(up_kernel, grid=(t // BLOCK,), in_specs=[rows(d), rows(d),...  21 us
  transfers between devices with their start and end apart: 8, of which 7 were waited for; matrix products, arithmetic and copies ran while one was open for 4% of the time, Pallas kernels for 14%

profile of v1, /device:TPU:0, one launch (start us, length us, event | category | flops | bytes accessed | tf_op | source)
XLA Modules:
  0.0 763.1 jit_solution(6994298645081362338)
XLA Ops:
  13.4 42.3 %all-reduce.9 = (bf16[768]{0:T(1024)(128)(2,1)S(1)}, bf16[768]{0:T(1024)(128)(2,1)S(1)}, bf16[768]{0:T(1024)(128)(2,1)S(1)}, bf16[3072]{0:T(1024)(128)(2,1)S(1)}) all-reduce(bf16[768]{0:T(1024)(128)(2,1)S(1)} %dynamic-update-slice, bf16[768]{0:T(1024)(128)(2,1)S(1)} %dynamic-update-slice.1, ...), channel_id=1, replica_groups=mesh['dp'=4,'fsdp'=8] {'dp','fsdp'}, use_global_device_ids=true, to_apply=%add | all-reduce | flops 5376 | bytes 21504
  61.4 1.9 fusion
  63.3 10.6 %all-gather.5.cloned.1.call-done.w_ref = bf16[768,2304]{1,0:T(8,128)(2,1)} async-done(((bf16[24,2304]{1,0:T(8,128)(2,1)}), bf16[768,2304]{1,0:T(8,128)(2,1)}) %all-gather.5.cloned.1.call-update) | async-done | bytes 3538960 | tf_op jit(solution)/shard_map/all_gather | solution.py:525
  75.3 8.6 %qkv_forward.1 = (bf16[1024,768]{1,0:T(8,128)(2,1)S(1)}, bf16[1024,2304]{1,0:T(8,128)(2,1)}) custom-call(bf16[1024,768]{1,0:T(8,128)(2,1)S(1)} %copy-done.8, bf16[768,2304]{1,0:T(8,128)(2,1)} %all-gather.5.cloned.1.call-done.w_ref, f32[1,768]{1,0:T(1,128)S(1)} %reshape.248.gain_ref, f32[1024,128]{1,0:T(8,128)S(1)} %get-tuple-element.69.cos_ref, ...), custom_call_target="tpu_custom_call" | custom-call | flops 3623878656 | bytes 12976128 | tf_op jit(solution)/shard_map/qkv_forward/pallas_call | solution.py:90
  85.2 2.3 copy-done
  87.5 21.6 %attention_forward.1 = (f32[1024,768]{1,0:T(8,128)S(1)}, f32[6,8,1024]{2,1,0:T(8,128)S(1)}) custom-call(s32[4]{0:T(128)S(1)} %add_bitcast_fusion.reach, bf16[1024,2304]{1,0:T(8,128)(2,1)S(1)} %copy-done, bf16[1024,2304]{1,0:T(8,128)(2,1)S(1)} %copy-done, bf16[1024,2304]{1,0:T(8,128)(2,1)S(1)} %copy-done, s32[1024,1]{1,0:T(8,128)S(1)} %copy.23.start_ref), custom_call_target="tpu_custom_call" | custom-call | flops 1610612736 | bytes 9437184 | tf_op jit(solution)/shard_map/attention_forward/pallas_call | solution.py:168
  109.1 1.7 copy-done.1
  110.7 19.1 %all-gather.7.cloned.1.call-done.wo_ref = bf16[768,768]{1,0:T(8,128)(2,1)} async-done(((bf16[24,768]{1,0:T(8,128)(2,1)}), bf16[768,768]{1,0:T(8,128)(2,1)}) %all-gather.7.cloned.1.call-update) | async-done | bytes 1179664 | tf_op jit(solution)/shard_map/all_gather | solution.py:525
  129.9 65.5 %all-gather.9.cloned.1.call-done.wu_ref = bf16[768,3072]{1,0:T(8,128)(2,1)} async-done(((bf16[24,3072]{1,0:T(8,128)(2,1)}), bf16[768,3072]{1,0:T(8,128)(2,1)}) %all-gather.9.cloned.1.call-update) | async-done | bytes 4718608 | tf_op jit(solution)/shard_map/all_gather | solution.py:525
  195.4 21.0 %up_forward.1 = (bf16[1024,768]{1,0:T(8,128)(2,1)}, f32[1024,768]{1,0:T(8,128)}, bf16[1024,768]{1,0:T(8,128)(2,1)}, bf16[1024,3072]{1,0:T(8,128)(2,1)}, bf16[1024,3072]{1,0:T(8,128)(2,1)}, /*index=5*/f32[1024,128]{1,0:T(8,128)}) custom-call(f32[1024,768]{1,0:T(8,128)} %copy-done.1, bf16[1024,768]{1,0:T(8,128)(2,1)} %x_ref.5, ...), custom_call_target="tpu_custom_call" | custom-call | flops 6039797760 | bytes 29491200 | tf_op jit(solution)/shard_map/up_forward/pallas_call | solution.py:322
  216.3 44.3 %all-gather.11.cloned.1.call-done.wd_ref = bf16[3072,768]{1,0:T(8,128)(2,1)} async-done(((bf16[96,768]{1,0:T(8,128)(2,1)}), bf16[3072,768]{1,0:T(8,128)(2,1)}) %all-gather.11.cloned.1.call-update) | async-done | bytes 4718608 | tf_op jit(solution)/shard_map/all_gather | solution.py:525
  260.6 32.3 %down_both.1 = (bf16[1024,768]{1,0:T(8,128)(2,1)}, bf16[1024,3072]{1,0:T(8,128)(2,1)}, f32[3072,768]{1,0:T(8,128)}, f32[1,3072]{1,0:T(1,128)}) custom-call(bf16[1024,3072]{1,0:T(8,128)(2,1)} %get-tuple-element.37.m_ref, bf16[1024,3072]{1,0:T(8,128)(2,1)} %get-tuple-element.38.slope_ref, f32[1024,128]{1,0:T(8,128)} %get-tuple-element.39.inv_ref, ...), custom_call_target="tpu_custom_call" | custom-call | flops 14495514624 | bytes 39321600 | tf_op jit(solution)/shard_map/down_both/pallas_call | solution.py:373
  293.0 32.2 %up_backward.1 = (f32[1024,768]{1,0:T(8,128)}, bf16[1024,768]{1,0:T(8,128)(2,1)}, f32[768,3072]{1,0:T(8,128)}, f32[768,768]{1,0:T(8,128)}, f32[1,768]{1,0:T(1,128)}, /*index=5*/f32[1,768]{1,0:T(1,128)}) custom-call(bf16[1024,3072]{1,0:T(8,128)(2,1)} %get-tuple-element.42.dpre_ref, bf16[1024,768]{1,0:T(8,128)(2,1)} %get-tuple-element.43.h2_ref, ...), custom_call_target="tpu_custom_call" | custom-call | flops 12079595520 | bytes 42860544 | tf_op jit(solution)/shard_map/up_backward/pallas_call | solution.py:423
  325.2 3.0 convert_element_type.60
  331.8 35.0 %attention_backward.1 = (bf16[1024,768]{1,0:T(8,128)(2,1)S(1)}, bf16[1024,768]{1,0:T(8,128)(2,1)S(1)}, bf16[1024,768]{1,0:T(8,128)(2,1)S(1)}) custom-call(s32[4]{0:T(128)S(1)} %add_bitcast_fusion.reach, bf16[1024,2304]{1,0:T(8,128)(2,1)} %get-tuple-element.35.q_ref.k_ref.v_ref, bf16[1024,2304]{1,0:T(8,128)(2,1)} %get-tuple-element.35.q_ref.k_ref.v_ref, ...), custom_call_target="tpu_custom_call" | custom-call | flops 4026531840 | bytes 15728640 | tf_op jit(solution)/shard_map/attention_backward/pallas_call | solution.py:268
  366.8 9.5 %qkv_weight_grad.1 = f32[768,2304]{1,0:T(8,128)S(1)} custom-call(bf16[1024,768]{1,0:T(8,128)(2,1)S(1)} %copy-done.16, bf16[1024,768]{1,0:T(8,128)(2,1)S(1)} %get-tuple-element.47.dq_ref, bf16[1024,768]{1,0:T(8,128)(2,1)S(1)} %get-tuple-element.48.dk_ref, bf16[1024,768]{1,0:T(8,128)(2,1)S(1)} %get-tuple-element.49.dv_ref), custom_call_target="tpu_custom_call" | custom-call | flops 3623878656 | bytes 13369344 | tf_op jit(solution)/shard_map/qkv_weight_grad/pallas_call | solution.py:458
  376.4 2.2 convert_element_type.58
  378.6 6.6 convert_element_type.62
  385.6 6.4 convert_element_type.64
  395.3 9.1 %qkv_backward.1 = (f32[1024,768]{1,0:T(8,128)}, f32[1,768]{1,0:T(1,128)S(1)}) custom-call(bf16[1024,768]{1,0:T(8,128)(2,1)S(1)} %copy-done.10, bf16[1024,768]{1,0:T(8,128)(2,1)S(1)} %copy-done.12, bf16[1024,768]{1,0:T(8,128)(2,1)S(1)} %copy-done.14, bf16[1024,768]{1,0:T(8,128)(2,1)} %x_ref.5, f32[1024,768]{1,0:T(8,128)} %get-tuple-element.50.dx1_ref, ...), custom_call_target="tpu_custom_call" | custom-call | flops 3623878656 | bytes 16121856 | tf_op jit(solution)/shard_map/qkv_backward/pallas_call | solution.py:492
  404.5 40.0 %all-reduce.8 = (f32[768]{0:T(1024)S(1)}, f32[768]{0:T(1024)S(1)}, f32[768]{0:T(1024)S(1)}, f32[3072]{0:T(1024)S(1)}) all-reduce(f32[768]{0:T(1024)S(1)} %reduce.2, f32[768]{0:T(1024)S(1)} %reduce.3, f32[768]{0:T(1024)S(1)} %reduce.4, f32[3072]{0:T(1024)S(1)} %bitcast.11), channel_id=6, replica_groups=mesh['dp'=4,'fsdp'=8] {'dp','fsdp'}, use_global_device_ids=true, to_apply=%region_6.7.clone | all-reduce | flops 5376 | bytes 43008
  448.2 82.3 %reduce-scatter.5.cloned.1.call-done = bf16[24,2304]{1,0:T(8,128)(2,1)} async-done(((bf16[768,2304]{1,0:T(8,128)(2,1)}), bf16[24,2304]{1,0:T(8,128)(2,1)}) %reduce-scatter.5.cloned.1.call-update) | async-done | bytes 110608 | tf_op jit(solution)/shard_map/reduce_scatter | solution.py:529
  532.2 109.8 %reduce-scatter.9.cloned.1.call-done = bf16[24,3072]{1,0:T(8,128)(2,1)} async-done(((bf16[768,3072]{1,0:T(8,128)(2,1)}), bf16[24,3072]{1,0:T(8,128)(2,1)}) %reduce-scatter.9.cloned.1.call-update) | async-done | bytes 147472 | tf_op jit(solution)/shard_map/reduce_scatter | solution.py:529
  643.6 110.8 %reduce-scatter.11.cloned.1.call-done = bf16[96,768]{1,0:T(8,128)(2,1)} async-done(((bf16[3072,768]{1,0:T(8,128)(2,1)}), bf16[96,768]{1,0:T(8,128)(2,1)}) %reduce-scatter.11.cloned.1.call-update) | async-done | bytes 147472 | tf_op jit(solution)/shard_map/reduce_scatter | solution.py:529
  (88 shorter events, 30.3 us)
Async XLA Ops:
  7.2 66.8 %all-gather.5.cloned.1.call-start = ((), (), s32[]{:S(2)}) async-start(), calls=%async_computation.4 | async-start | bytes 3649536 | tf_op jit(solution)/shard_map/all_gather | solution.py:525
  7.9 122.0 %all-gather.7.cloned.1.call-start = ((), (), s32[]{:S(2)}) async-start(), calls=%async_computation.5 | async-start | bytes 1216512 | tf_op jit(solution)/shard_map/all_gather | solution.py:525
  8.7 186.7 %all-gather.9.cloned.1.call-start = ((), (), s32[]{:S(2)}) async-start(), calls=%async_computation.6 | async-start | bytes 4866048 | tf_op jit(solution)/shard_map/all_gather | solution.py:525
  9.4 251.3 %all-gather.11.cloned.1.call-start = ((), (), s32[]{:S(2)}) async-start(), calls=%async_computation.7 | async-start | bytes 4866048 | tf_op jit(solution)/shard_map/all_gather | solution.py:525
  10.0 436.9 %reduce-scatter.7.cloned.1.call-start = ((), (), s32[]{:S(2)}) async-start(), calls=%async_computation.9 | async-start | bytes 1216512 | tf_op jit(solution)/shard_map/reduce_scatter | solution.py:529
  63.3 20.7 %copy-start.3 = (f32[1024,128]{1,0:T(8,128)}, f32[1024,128]{1,0:T(8,128)S(1)}, u32[]{:S(2)}) copy-start(f32[1024,128]{1,0:T(8,128)S(1)} %get-tuple-element.68.sin_ref) | copy-start | bytes 1572868
  63.3 20.7 %copy-start.5 = (f32[1024,128]{1,0:T(8,128)}, f32[1024,128]{1,0:T(8,128)S(1)}, u32[]{:S(2)}) copy-start(f32[1024,128]{1,0:T(8,128)S(1)} %get-tuple-element.69.cos_ref) | copy-start | bytes 1572868
  73.9 1.4 copy-start.8
  85.2 2.3 copy-start
  109.1 1.7 copy-start.1
  325.2 3.1 copy-start.2
  328.2 202.4 %reduce-scatter.5.cloned.1.call-start = ((), (), s32[]{:S(2)}) async-start(), calls=%async_computation.8 | async-start | bytes 3649536 | tf_op jit(solution)/shard_map/reduce_scatter | solution.py:529
  330.4 1.4 copy-start.7
  331.8 35.1 %copy-start.16 = (bf16[1024,768]{1,0:T(8,128)(2,1)S(1)}, bf16[1024,768]{1,0:T(8,128)(2,1)}, u32[]{:S(2)}) copy-start(bf16[1024,768]{1,0:T(8,128)(2,1)} %copy-done.15) | copy-start | bytes 4718596
  366.8 9.5 %copy-start.9 = (bf16[1024,768]{1,0:T(8,128)(2,1)}, bf16[1024,768]{1,0:T(8,128)(2,1)S(1)}, u32[]{:S(2)}) copy-start(bf16[1024,768]{1,0:T(8,128)(2,1)S(1)} %get-tuple-element.47.dq_ref) | copy-start | bytes 4718596
  366.8 9.5 %copy-start.11 = (bf16[1024,768]{1,0:T(8,128)(2,1)}, bf16[1024,768]{1,0:T(8,128)(2,1)S(1)}, u32[]{:S(2)}) copy-start(bf16[1024,768]{1,0:T(8,128)(2,1)S(1)} %get-tuple-element.48.dk_ref) | copy-start | bytes 4718596
  366.8 9.5 %copy-start.13 = (bf16[1024,768]{1,0:T(8,128)(2,1)}, bf16[1024,768]{1,0:T(8,128)(2,1)S(1)}, u32[]{:S(2)}) copy-start(bf16[1024,768]{1,0:T(8,128)(2,1)S(1)} %get-tuple-element.49.dv_ref) | copy-start | bytes 4718596
  378.6 263.4 %reduce-scatter.9.cloned.1.call-start = ((), (), s32[]{:S(2)}) async-start(), calls=%async_computation.10 | async-start | bytes 4866048 | tf_op jit(solution)/shard_map/reduce_scatter | solution.py:529
  385.3 369.1 %reduce-scatter.11.cloned.1.call-start = ((), (), s32[]{:S(2)}) async-start(), calls=%async_computation.11 | async-start | bytes 4866048 | tf_op jit(solution)/shard_map/reduce_scatter | solution.py:529
  392.0 1.4 copy-start.10
  392.0 1.9 copy-start.12
  395.3 9.1 %copy-start.19 = (f32[1,768]{1,0:T(1,128)S(1)}, f32[1,768]{1,0:T(1,128)}, u32[]{:S(2)}) copy-start(f32[1,768]{1,0:T(1,128)} %get-tuple-element.57) | copy-start | bytes 9220
  395.3 9.1 %copy-start.18 = (f32[1,768]{1,0:T(1,128)S(1)}, f32[1,768]{1,0:T(1,128)}, u32[]{:S(2)}) copy-start(f32[1,768]{1,0:T(1,128)} %get-tuple-element.58) | copy-start | bytes 9220
  395.3 9.1 %copy-start.17 = (f32[1,3072]{1,0:T(1,128)S(1)}, f32[1,3072]{1,0:T(1,128)}, u32[]{:S(2)}) copy-start(f32[1,3072]{1,0:T(1,128)} %get-tuple-element.59) | copy-start | bytes 36868
  (4 other events, 4.7 us)
Sparse Core Ops, SparseCore 0:
  10.9 62.9 all-gather.4
  76.8 52.9 all-gather.6
  132.8 62.5 all-gather.8
  198.1 62.4 all-gather.10
  328.3 94.9 reduce-scatter.6
  428.6 101.8 reduce-scatter.4
  536.0 105.8 reduce-scatter.8
  648.3 106.0 reduce-scatter.10

commit v2 on v1

--- a/solution.py
+++ b/solution.py
@@ -21,6 +21,7 @@
 MIB = 1 << 20
 AXES = ("dp", "fsdp")
 BLOCK = 256
+LANES = 768
 
 
 def dot(a, b, dims=((1,), (0,))):
@@ -66,12 +67,104 @@
     return jax.ShapeDtypeStruct(shape, dtype)
 
 
-def qkv_kernel(x_ref, w_ref, gain_ref, cos_ref, sin_ref, h_ref, qkv_ref):
+def hbm():
+    return pl.BlockSpec(memory_space=pl.ANY)
+
+
+def fetch(order, parts, places, sem):
+    if order is None:
+        for part, (_, _, buffer, _) in zip(parts, places):
+            pltpu.make_async_copy(part, buffer, sem).start()
+        return
+    count = parts[0].shape[0]
+    for p, part in enumerate(parts):
+        for b in range(count):
+            owner = order[p * count + b]
+            for first, size, buffer, column in places:
+                pltpu.make_async_copy(
+                    part.at[b, pl.ds(first, size), :],
+                    buffer.at[pl.ds(pl.multiple_of(owner * size, 8), size), pl.ds(column, LANES)],
+                    sem,
+                ).start()
+
+
+def arrive(buffers, sem):
+    for buffer in buffers:
+        pltpu.make_async_copy(buffer, buffer, sem).wait()
+
+
+def deal(order, total, keep_ref, send_ref, places):
+    half = keep_ref.shape[0]
+
+    def one(j, target, at):
+        owner = order[at]
+        for first, size, buffer, column in places:
+            block = buffer[pl.ds(pl.multiple_of(owner * size, 8), size), column : column + LANES]
+            target[j, first : first + size, :] = block.astype(target.dtype)
+
+    @pl.loop(0, half)
+    def _(j):
+        one(j, keep_ref, j)
+        one(j, send_ref, j + half)
+
+
+def slabs(first, size, buffer, width):
+    return [(first + s * size, size, buffer, s * LANES) for s in range(width // LANES)]
+
+
+def spread(rows_in, offset, count, owners):
+    lanes = rows_in.shape[1]
+    wide = owners * count
+    lane = lax.broadcasted_iota(jnp.int32, (lanes, wide), 0)
+    column = lax.broadcasted_iota(jnp.int32, (lanes, wide), 1)
+    pick = (lane - offset == lax.rem(column, count)).astype(F32).astype(BF)
+    full = dot(rows_in, pick)
+    owner = lax.broadcasted_iota(jnp.int32, (owners, wide), 0)
+    column = lax.broadcasted_iota(jnp.int32, (owners, wide), 1)
+    own = (column >= owner * count) & (column < owner * count + count)
+    return jnp.sum(jnp.where(own, full, 0.0), axis=0, keepdims=True)
+
+
+def qkv_kernel(split, sizes, *refs):
+    if split:
+        order, x_ref, cos_ref, sin_ref, *refs = refs
+        parts, refs = refs[:8], refs[8:]
+        h_ref, qkv_ref, w_ref, ga_ref, gi_ref, gf_ref, gm_ref, gains, sem, gain_sem = refs
+    else:
+        order, x_ref, cos_ref, sin_ref, ga_ref, *refs = refs
+        parts, refs = refs[:1], refs[1:]
+        h_ref, qkv_ref, w_ref, sem = refs
+    width = x_ref.shape[1]
+    step = pl.program_id(0)
+    if split:
+        size = width // 32
+        weight = slabs(0, size, w_ref, 3 * width)
+
+        @pl.when(step == 0)
+        def _():
+            fetch(order, parts, [(3 * size, 8, gains, 0)], gain_sem)
+            fetch(order, parts, weight, sem)
+            arrive([gains], gain_sem)
+            owner = lax.broadcasted_iota(jnp.int32, (32, 256), 0)
+            lane = lax.broadcasted_iota(jnp.int32, (32, 256), 1)
+            pick = (lane == owner * 8).astype(F32).astype(BF)
+            per_owner = dot(pick, gains[:, :256]).astype(BF)
+            at = 0
+            for ref, count in zip((ga_ref, gi_ref, gf_ref, gm_ref), sizes):
+                ref[...] = spread(per_owner, at, count, 32)
+                at += count
+            arrive([w_ref], sem)
+    else:
+
+        @pl.when(step == 0)
+        def _():
+            fetch(None, parts, [(0, 0, w_ref, 0)], sem)
+            arrive([w_ref], sem)
+
     unit, _ = unit_norm(x_ref[...].astype(F32))
-    h = (unit * gain_ref[...]).astype(BF)
+    h = (unit * ga_ref[...]).astype(BF)
     h_ref[...] = h
     cos, sin = cos_ref[...], sin_ref[...]
-    width = h.shape[1]
     for part in range(3):
         y = dot(h, w_ref[:, part * width : (part + 1) * width])
         for c in range(width // PAIR):
@@ -84,21 +177,52 @@
             qkv_ref[:, at : at + PAIR] = z.astype(BF)
 
 
-def qkv_forward(tokens, w_qkv, gain, cos, sin):
+def prefetched(kernel, order, inputs, in_specs, out_specs, out_shape, scratch, grid, mib, name, flops, data):
+    return pl.pallas_call(
+        kernel,
+        grid_spec=pltpu.PrefetchScalarGridSpec(
+            num_scalar_prefetch=1,
+            grid=grid,
+            in_specs=in_specs,
+            out_specs=out_specs,
+            scratch_shapes=scratch,
+        ),
+        out_shape=out_shape,
+        compiler_params=params(mib),
+        cost_estimate=pl.CostEstimate(flops=flops, transcendentals=0, bytes_accessed=data),
+        name=name,
+    )(order, *inputs)
+
+
+def rows(width, block=BLOCK):
+    return pl.BlockSpec((block, width), lambda i, *_: (i, 0))
+
+
+def whole(shape):
+    return pl.BlockSpec(shape, lambda *_: (0,) * len(shape), pipeline_mode=pl.Buffered(1))
+
+
+def qkv_forward(split, order, tokens, cos, sin, parts, gain, sizes):
     t, d = tokens.shape
-    n = w_qkv.shape[1]
-    return pl.pallas_call(
-        qkv_kernel,
-        grid=(t // BLOCK,),
-        in_specs=[rows(d), whole((d, n)), whole((1, d)), rows(PAIR), rows(PAIR)],
-        out_specs=[rows(d), rows(n)],
-        out_shape=[shaped((t, d), BF), shaped((t, n), BF)],
-        compiler_params=params(48),
-        cost_estimate=pl.CostEstimate(
-            flops=2 * t * d * n, transcendentals=0, bytes_accessed=2 * d * n + 12 * t * d
-        ),
-        name="qkv_forward",
-    )(tokens, w_qkv, gain, cos, sin)
+    n = 3 * d
+    inputs = [tokens, cos, sin]
+    in_specs = [rows(d), rows(PAIR), rows(PAIR)]
+    out_specs = [rows(d), rows(n), whole((d, n))]
+    out_shape = [shaped((t, d), BF), shaped((t, n), BF), shaped((d, n), BF)]
+    scratch = [pltpu.SemaphoreType.DMA]
+    if split:
+        widths = [32 * s for s in sizes]
+        out_specs += [whole((1, w)) for w in widths]
+        out_shape += [shaped((1, w), F32) for w in widths]
+        scratch = [pltpu.VMEM((32 * 8, LANES), BF), pltpu.SemaphoreType.DMA, pltpu.SemaphoreType.DMA]
+    else:
+        inputs.append(gain)
+        in_specs.append(whole((1, d)))
+    return prefetched(
+        functools.partial(qkv_kernel, split, sizes), order, inputs + list(parts), in_specs + [hbm()] * len(parts),
+        out_specs, out_shape, scratch, (t // BLOCK,), 40, "qkv_forward",
+        2 * t * d * n, 4 * d * n + 12 * t * d,
+    )
 
 
 def window(i, n):
@@ -297,11 +421,27 @@
     )(reach, qkv, qkv, qkv, d_mixed, mixed, lse, start_row, cos, sin)
 
 
-def up_kernel(o_ref, x_ref, wo_ref, wu_ref, gi_ref, gf_ref, gm_ref,
-              a_ref, x1_ref, h2_ref, m_ref, slope_ref, inv_ref):
+def up_kernel(split, *refs):
+    order, o_ref, x_ref, gi_ref, gf_ref, gm_ref, *refs = refs
+    count = 8 if split else 2
+    parts, refs = refs[:count], refs[count:]
+    a_ref, x1_ref, h2_ref, m_ref, slope_ref, inv_ref, wo_ref, wu_ref, sem = refs
+    d, f = wu_ref.shape
+    size = d // 32
+    places = [(0, size, wo_ref, 0)] + slabs(size, size, wu_ref, f) if split else [(0, 0, wo_ref, 0), (0, 0, wu_ref, 0)]
+
+    @pl.when(pl.program_id(0) == 0)
+    def _():
+        fetch(order if split else None, parts, places, sem)
+
     unit, _ = unit_norm(o_ref[...])
     a = (unit * gi_ref[...]).astype(BF)
     a_ref[...] = a
+
+    @pl.when(pl.program_id(0) == 0)
+    def _():
+        arrive([wo_ref, wu_ref], sem)
+
     x1 = x_ref[...].astype(F32) + dot(a, wo_ref[...])
     x1_ref[...] = x1
     unit, _ = unit_norm(x1)
@@ -316,33 +456,53 @@
     inv_ref[...] = jnp.broadcast_to(inv, inv_ref.shape)
 
 
-def up_forward(mixed, tokens, w_out, w_up, gain_inner, gain_ffn, gain_mid):
+def up_forward(split, order, mixed, tokens, gain_inner, gain_ffn, gain_mid, parts):
     t, d = tokens.shape
-    f = w_up.shape[1]
-    return pl.pallas_call(
-        up_kernel,
-        grid=(t // BLOCK,),
-        in_specs=[rows(d), rows(d), whole((d, d)), whole((d, f)), whole((1, d)), whole((1, d)), whole((1, f))],
-        out_specs=[rows(d), rows(d), rows(d), rows(f), rows(f), rows(PAIR)],
-        out_shape=[
+    f = gain_mid.shape[1]
+    return prefetched(
+        functools.partial(up_kernel, split), order,
+        [mixed, tokens, gain_inner, gain_ffn, gain_mid, *parts],
+        [rows(d), rows(d), whole((1, d)), whole((1, d)), whole((1, f))] + [hbm()] * len(parts),
+        [rows(d), rows(d), rows(d), rows(f), rows(f), rows(PAIR), whole((d, d)), whole((d, f))],
+        [
             shaped((t, d), BF), shaped((t, d), F32), shaped((t, d), BF),
             shaped((t, f), BF), shaped((t, f), BF), shaped((t, PAIR), F32),
+            shaped((d, d), BF), shaped((d, f), BF),
         ],
-        compiler_params=params(56),
-        cost_estimate=pl.CostEstimate(
-            flops=2 * t * d * (d + f), transcendentals=2 * t * f, bytes_accessed=2 * d * (d + f) + 4 * t * f + 14 * t * d
-        ),
-        name="up_forward",
-    )(mixed, tokens, w_out, w_up, gain_inner, gain_ffn, gain_mid)
-
-
-def down_kernel(m_ref, slope_ref, inv_ref, x1_ref, ct_ref, valid_ref, wd_ref, gm_ref,
-                y_ref, dpre_ref, gwd_ref, gg_ref):
+        [pltpu.SemaphoreType.DMA], (t // BLOCK,), 56, "up_forward",
+        2 * t * d * (d + f), 4 * d * (d + f) + 4 * t * f + 14 * t * d,
+    )
+
+
+def down_kernel(split, *refs):
+    order, back, m_ref, slope_ref, inv_ref, x1_ref, ct_ref, valid_ref, gm_ref, *refs = refs
+    count = 8 if split else 1
+    parts, refs = refs[:count], refs[count:]
+    y_ref, dpre_ref, gg_ref, *refs = refs
+    if split:
+        keep_ref, send_ref, wd_ref, total, sem = refs
+    else:
+        total, wd_ref, sem = refs
+    f, d = wd_ref.shape
     step = pl.program_id(0)
+
+    @pl.when(step == 0)
+    def _():
+        fetch(order if split else None, parts, [(0, f // 32, wd_ref, 0)], sem)
+
     m = m_ref[...]
-    y_ref[...] = (x1_ref[...] + dot(m, wd_ref[...])).astype(BF)
     gy = jnp.where(valid_ref[...] > 0, ct_ref[...], jnp.zeros_like(ct_ref))
     part = dot(m, gy, ((0,), (0,)))
+
+    @pl.when(step == 0)
+    def _():
+        total[...] = part
+        arrive([wd_ref], sem)
+
+    @pl.when(step > 0)
+    def _():
+        total[...] += part
+
     dm = dot(gy, wd_ref[...], ((1,), (1,)))
     gain = gm_ref[...]
     mf = m.astype(F32)
@@ -354,38 +514,67 @@
         - (mf * (1.0 / gain)) * jnp.mean(prod, axis=-1, keepdims=True)
     )
     dpre_ref[...] = (d_act * slope_ref[...].astype(F32)).astype(BF)
+    y_ref[...] = (x1_ref[...] + dot(m, wd_ref[...])).astype(BF)
     gain_part = jnp.sum(prod, axis=0, keepdims=True) * (1.0 / gain)
 
     @pl.when(step == 0)
     def _():
-        gwd_ref[...] = part
         gg_ref[...] = gain_part
 
     @pl.when(step > 0)
     def _():
-        gwd_ref[...] += part
         gg_ref[...] += gain_part
 
-
-def down_both(m, slope, inv, x1, cotangent, valid, w_down, gain_mid):
+    if split:
+
+        @pl.when(step == pl.num_programs(0) - 1)
+        def _():
+            deal(back, total, keep_ref, send_ref, [(0, f // 32, total, 0)])
+
+
+def dealt(split, size, shapes):
+    if split:
+        half = (16, size, LANES)
+        return [whole(half)] * 2, [shaped(half, F32), shaped(half, BF)], [pltpu.VMEM(s, F32) for s in shapes]
+    return [whole(s) for s in shapes], [shaped(s, F32) for s in shapes], []
+
+
+def prefetched2(kernel, order, back, inputs, in_specs, out_specs, out_shape, scratch, grid, mib, name, flops, data):
+    return pl.pallas_call(
+        kernel,
+        grid_spec=pltpu.PrefetchScalarGridSpec(
+            num_scalar_prefetch=2, grid=grid, in_specs=in_specs, out_specs=out_specs, scratch_shapes=scratch,
+        ),
+        out_shape=out_shape,
+        compiler_params=params(mib),
+        cost_estimate=pl.CostEstimate(flops=flops, transcendentals=0, bytes_accessed=data),
+        name=name,
+    )(order, back, *inputs)
+
+
+def down_both(split, order, back, m, slope, inv, x1, cotangent, valid, gain_mid, parts):
     t, d = x1.shape
     f = m.shape[1]
-    return pl.pallas_call(
-        down_kernel,
-        grid=(t // BLOCK,),
-        in_specs=[rows(f), rows(f), rows(PAIR), rows(d), rows(d), rows(1), whole((f, d)), whole((1, f))],
-        out_specs=[rows(d), rows(f), whole((f, d)), whole((1, f))],
-        out_shape=[shaped((t, d), BF), shaped((t, f), BF), shaped((f, d), F32), shaped((1, f), F32)],
-        compiler_params=params(60),
-        cost_estimate=pl.CostEstimate(
-            flops=6 * t * d * f, transcendentals=0, bytes_accessed=6 * d * f + 6 * t * f + 8 * t * d
-        ),
-        name="down_both",
-    )(m, slope, inv, x1, cotangent, valid, w_down, gain_mid)
-
-
-def up_back_kernel(dpre_ref, h2_ref, x1_ref, ct_ref, valid_ref, a_ref, o_ref, wu_ref, wo_ref, gf_ref, gi_ref,
-                   dx1_ref, do_ref, gwu_ref, gwo_ref, ggf_ref, ggi_ref):
+    out_specs, out_shape, scratch = dealt(split, f // 32, [(f, d)])
+    weight = [pltpu.VMEM((f, d), BF)]
+    return prefetched2(
+        functools.partial(down_kernel, split), order, back,
+        [m, slope, inv, x1, cotangent, valid, gain_mid, *parts],
+        [rows(f), rows(f), rows(PAIR), rows(d), rows(d), rows(1), whole((1, f))] + [hbm()] * len(parts),
+        [rows(d), rows(f), whole((1, f))] + out_specs,
+        [shaped((t, d), BF), shaped((t, f), BF), shaped((1, f), F32)] + out_shape,
+        weight + scratch + [pltpu.SemaphoreType.DMA], (t // BLOCK,), 60, "down_both",
+        6 * t * d * f, 6 * d * f + 6 * t * f + 8 * t * d,
+    )
+
+
+def up_back_kernel(split, *refs):
+    order, back, dpre_ref, h2_ref, x1_ref, ct_ref, valid_ref, a_ref, o_ref, wu_ref, wo_ref, gf_ref, gi_ref, *refs = refs
+    dx1_ref, do_ref, ggf_ref, ggi_ref, *refs = refs
+    if split:
+        keep_ref, send_ref, gwo_ref, gwu_ref = refs
+    else:
+        gwo_ref, gwu_ref = refs
     step = pl.program_id(0)
     dpre = dpre_ref[...]
     part_up = dot(h2_ref[...], dpre, ((0,), (0,)))
@@ -416,27 +605,37 @@
         ggf_ref[...] += ffn_part
         ggi_ref[...] += inner_part
 
-
-def up_backward(dpre, h2, x1, cotangent, valid, a, mixed, w_up, w_out, gain_ffn, gain_inner):
+    if split:
+        d, f = gwu_ref.shape
+        size = d // 32
+
+        @pl.when(step == pl.num_programs(0) - 1)
+        def _():
+            deal(back, None, keep_ref, send_ref, [(0, size, gwo_ref, 0)] + slabs(size, size, gwu_ref, f))
+
+
+def up_backward(split, order, back, dpre, h2, x1, cotangent, valid, a, mixed, w_up, w_out, gain_ffn, gain_inner):
     t, d = x1.shape
     f = dpre.shape[1]
-    return pl.pallas_call(
-        up_back_kernel,
-        grid=(t // BLOCK,),
-        in_specs=[rows(f), rows(d), rows(d), rows(d), rows(1), rows(d), rows(d),
-                  whole((d, f)), whole((d, d)), whole((1, d)), whole((1, d))],
-        out_specs=[rows(d), rows(d), whole((d, f)), whole((d, d)), whole((1, d)), whole((1, d))],
-        out_shape=[shaped((t, d), F32), shaped((t, d), BF), shaped((d, f), F32), shaped((d, d), F32),
-                   shaped((1, d), F32), shaped((1, d), F32)],
-        compiler_params=params(60),
-        cost_estimate=pl.CostEstimate(
-            flops=4 * t * d * (d + f), transcendentals=0, bytes_accessed=6 * d * (d + f) + 2 * t * f + 24 * t * d
-        ),
-        name="up_backward",
-    )(dpre, h2, x1, cotangent, valid, a, mixed, w_up, w_out, gain_ffn, gain_inner)
-
-
-def qkv_grad_kernel(h_ref, dq_ref, dk_ref, dv_ref, g_ref):
+    out_specs, out_shape, scratch = dealt(split, (d + f) // 32, [(d, d), (d, f)])
+    return prefetched2(
+        functools.partial(up_back_kernel, split), order, back,
+        [dpre, h2, x1, cotangent, valid, a, mixed, w_up, w_out, gain_ffn, gain_inner],
+        [rows(f), rows(d), rows(d), rows(d), rows(1), rows(d), rows(d),
+         whole((d, f)), whole((d, d)), whole((1, d)), whole((1, d))],
+        [rows(d), rows(d), whole((1, d)), whole((1, d))] + out_specs,
+        [shaped((t, d), F32), shaped((t, d), BF), shaped((1, d), F32), shaped((1, d), F32)] + out_shape,
+        scratch, (t // BLOCK,), 60, "up_backward",
+        4 * t * d * (d + f), 6 * d * (d + f) + 2 * t * f + 24 * t * d,
+    )
+
+
+def qkv_grad_kernel(split, *refs):
+    order, back, h_ref, dq_ref, dk_ref, dv_ref, *refs = refs
+    if split:
+        keep_ref, send_ref, g_ref = refs
+    else:
+        (g_ref,) = refs
     step = pl.program_id(0)
     h = h_ref[...]
     d = h.shape[1]
@@ -452,19 +651,21 @@
         def _():
             g_ref[:, cols] += part
 
-
-def qkv_weight_grad(h, dq, dk, dv):
+    if split:
+
+        @pl.when(step == pl.num_programs(0) - 1)
+        def _():
+            deal(back, None, keep_ref, send_ref, slabs(0, d // 32, g_ref, 3 * d))
+
+
+def qkv_weight_grad(split, order, back, h, dq, dk, dv):
     t, d = h.shape
-    return pl.pallas_call(
-        qkv_grad_kernel,
-        grid=(t // BLOCK,),
-        in_specs=[rows(d)] * 4,
-        out_specs=whole((d, 3 * d)),
-        out_shape=shaped((d, 3 * d), F32),
-        compiler_params=params(40),
-        cost_estimate=pl.CostEstimate(flops=6 * t * d * d, transcendentals=0, bytes_accessed=12 * d * d + 8 * t * d),
-        name="qkv_weight_grad",
-    )(h, dq, dk, dv)
+    out_specs, out_shape, scratch = dealt(split, 3 * d // 32, [(d, 3 * d)])
+    return prefetched2(
+        functools.partial(qkv_grad_kernel, split), order, back,
+        [h, dq, dk, dv], [rows(d)] * 4, out_specs, out_shape, scratch,
+        (t // BLOCK,), 40, "qkv_weight_grad", 6 * t * d * d, 12 * d * d + 8 * t * d,
+    )
 
 
 def qkv_back_kernel(dq_ref, dk_ref, dv_ref, x_ref, dx1_ref, w_ref, gain_ref, dx_ref, gg_ref):
@@ -521,20 +722,139 @@
     return jnp.cos(angles), jnp.sin(angles) * sign[None, :]
 
 
-def gather(x):
-    return lax.all_gather(x, AXES, axis=0, tiled=True)
-
-
-def scatter(g):
-    return lax.psum_scatter(g, AXES, scatter_dimension=0, tiled=True)
-
-
-def local(tokens, doc_lengths, cotangent, w_qkv, w_out, w_up, w_down,
+Z = 4
+GROUPS = ((0, 2), (1, 3))
+
+
+def index(x, core, z, y):
+    return ((x * 2 + core) * Z + z) * 2 + y
+
+
+def permute(value, move):
+    places = [(x, c, z, y) for x in range(2) for c in range(2) for z in range(Z) for y in range(2)]
+    return lax.ppermute(value, AXES, [(index(*p), index(*move(*p))) for p in places])
+
+
+def over_x(v):
+    return permute(v, lambda x, c, z, y: (1 - x, c, z, y))
+
+
+def over_y(v):
+    return permute(v, lambda x, c, z, y: (x, c, z, 1 - y))
+
+
+def over_core(v):
+    return permute(v, lambda x, c, z, y: (x, 1 - c, z, y))
+
+
+def over_z(v, shift):
+    return permute(v, lambda x, c, z, y: (x, c, (z + shift) % Z, y))
+
+
+def across_z(v, bit):
+    return permute(v, lambda x, c, z, y: (x, c, z ^ bit, y))
+
+
+def place():
+    dp, fs = lax.axis_index("dp"), lax.axis_index("fsdp")
+    return dp // 2, dp % 2, fs // 2, fs % 2
+
+
+def gather_order():
+    x, c, z, y = place()
+    order = []
+    for core in range(2):
+        for group, first in zip(GROUPS, ("x", "y")):
+            for second in range(2):
+                for one in range(2):
+                    dx, dy = (one, second) if first == "x" else (second, one)
+                    for shift in group:
+                        order.append(index(x ^ dx, c ^ core, (z - shift) % Z, y ^ dy))
+    return jnp.stack(order).astype(jnp.int32)
+
+
+def scatter_order():
+    x, c, z, y = place()
+    order = []
+    for core in range(2):
+        for group, first in zip(GROUPS, ("y", "x")):
+            for one in (1, 0):
+                for second in (1, 0):
+                    dx, dy = (second, one) if first == "y" else (one, second)
+                    for shift in group:
+                        order.append(index(x ^ dx, c ^ core, (z + shift) % Z, y ^ dy))
+    return jnp.stack(order).astype(jnp.int32)
+
+
+def tie(value, other):
+    return lax.optimization_barrier((value, other))[0]
+
+
+def gather_z(block):
+    return [block] + [over_z(block, s) for s in (1, 2, 3)]
+
+
+def gather_xy(by_z):
+    even = jnp.stack([by_z[s] for s in GROUPS[0]])
+    odd = jnp.stack([by_z[s] for s in GROUPS[1]])
+    even = jnp.concatenate([even, over_x(even)])
+    odd = jnp.concatenate([odd, over_y(odd)])
+    return [even, over_y(even), odd, over_x(odd)]
+
+
+def gather_core(parts):
+    return parts + [over_core(p) for p in parts]
+
+
+def reduce_blocks(keep, send):
+    total = keep + over_core(send).astype(F32)
+    a, b = total[:8], total[8:]
+    a = a[4:] + over_y(a[:4].astype(BF)).astype(F32)
+    b = b[4:] + over_x(b[:4].astype(BF)).astype(F32)
+    a = a[2:] + over_x(a[:2].astype(BF)).astype(F32)
+    b = b[2:] + over_y(b[:2].astype(BF)).astype(F32)
+    r1, r2, r3 = over_z(b[0].astype(BF), 1), over_z(a[1].astype(BF), 2), over_z(b[1].astype(BF), 3)
+    return a[0] + r1.astype(F32) + r2.astype(F32) + r3.astype(F32)
+
+
+def unslab(block, width):
+    size = block.shape[0] * LANES // width
+    return jnp.concatenate([block[s * size : (s + 1) * size] for s in range(width // LANES)], axis=1)
+
+
+def slab(block):
+    return [block[:, s * LANES : (s + 1) * LANES] for s in range(block.shape[1] // LANES)]
+
+
+def local(fast, tokens, doc_lengths, cotangent, w_qkv, w_out, w_up, w_down,
           gain_attn, gain_inner, gain_ffn, gain_mid):
     row_count = doc_lengths.shape[0]
     seq = tokens.shape[0] // row_count
     wide = min(seq, 512) // BLOCK + 1
     blocks = seq // BLOCK
+    shards = (gain_attn, gain_inner, gain_ffn, gain_mid)
+    sizes = [g.shape[0] for g in shards]
+    if fast:
+        order, back = gather_order(), scatter_order()
+        gains_row = jnp.pad(jnp.concatenate(shards)[None], ((0, 7), (0, LANES - sum(sizes))))
+        first = gather_z(jnp.concatenate(slab(w_qkv) + [gains_row]))
+        mine = tie(jnp.concatenate([w_out] + slab(w_up)), first[1:])
+        second = gather_z(mine)
+        third = gather_z(tie(w_down, second[1:]))
+        parts_qkv = gather_xy(first)
+        parts_up = gather_xy([tie(second[0], parts_qkv)] + second[1:])
+        parts_down = gather_xy([tie(third[0], parts_up)] + third[1:])
+        parts_qkv, parts_up, parts_down = (gather_core(p) for p in (parts_qkv, parts_up, parts_down))
+        gains = None
+    else:
+        order = back = jnp.zeros((8,), jnp.int32)
+
+        def gather(v):
+            return lax.all_gather(v, AXES, axis=0, tiled=True)
+
+        parts_qkv, parts_up, parts_down = [gather(w_qkv)], [gather(w_out), gather(w_up)], [gather(w_down)]
+        gains = [gather(g).astype(F32).reshape(1, -1) for g in shards]
+
     start, position, valid = layout(doc_lengths, seq)
     cos, sin = tables(position)
     firsts = start[:, ::BLOCK] // BLOCK
@@ -543,29 +863,55 @@
     start_row = jnp.repeat(start, 8, axis=0)
     valid_col = valid.astype(jnp.int32).reshape(-1, 1)
 
-    f_qkv, f_out, f_up, f_down = (gather(w) for w in (w_qkv, w_out, w_up, w_down))
-    g_attn, g_inner, g_ffn, g_mid = (
-        gather(g).astype(F32).reshape(1, -1) for g in (gain_attn, gain_inner, gain_ffn, gain_mid)
-    )
-    h1, qkv = qkv_forward(tokens, f_qkv, g_attn, cos, sin)
+    h1, qkv, full_qkv, *rest = qkv_forward(
+        fast, order, tokens, cos, sin, parts_qkv, None if fast else gains[0], sizes
+    )
+    g_attn, g_inner, g_ffn, g_mid = rest if fast else gains
     mixed, lse = attention_forward(reach, qkv, start_col, row_count, wide)
-    a, x1, h2, m, slope, inv = up_forward(mixed, tokens, f_out, f_up, g_inner, g_ffn, g_mid)
-    result, dpre, grad_down, grad_mid = down_both(m, slope, inv, x1, cotangent, valid_col, f_down, g_mid)
-    dx1, d_mixed, grad_up, grad_out, grad_ffn, grad_inner = up_backward(
-        dpre, h2, x1, cotangent, valid_col, a, mixed, f_up, f_out, g_ffn, g_inner
+    a, x1, h2, m, slope, inv, full_out, full_up = up_forward(
+        fast, order, mixed, tokens, g_inner, g_ffn, g_mid, parts_up
+    )
+    result, dpre, grad_mid, *grad_down = down_both(
+        fast, order, back, m, slope, inv, x1, cotangent, valid_col, g_mid, parts_down
+    )
+    dx1, d_mixed, grad_ffn, grad_inner, *grad_up = up_backward(
+        fast, order, back, dpre, h2, x1, cotangent, valid_col, a, mixed, full_up, full_out, g_ffn, g_inner
     )
     dq, dk, dv = attention_backward(reach, qkv, d_mixed, mixed, lse, start_row, cos, sin, row_count, wide)
-    grad_qkv = qkv_weight_grad(h1, dq, dk, dv)
-    grad_tokens, grad_attn = qkv_backward(dq, dk, dv, tokens, dx1, f_qkv, g_attn)
-    weights = tuple(scatter(g.astype(BF)).astype(F32) for g in (grad_qkv, grad_out, grad_up, grad_down))
-    gains = tuple(scatter(g.reshape(-1)) for g in (grad_attn, grad_inner, grad_ffn, grad_mid))
-    return (result, grad_tokens) + weights + gains
+    grad_qkv = qkv_weight_grad(fast, order, back, h1, dq, dk, dv)
+    grad_tokens, grad_attn = qkv_backward(dq, dk, dv, tokens, dx1, full_qkv, g_attn)
+    gain_grads = (grad_attn, grad_inner, grad_ffn, grad_mid)
+    if fast:
+        own_down = reduce_blocks(*grad_down)
+        own_up = reduce_blocks(*grad_up)
+        own_qkv = reduce_blocks(*grad_qkv)
+        cut = w_out.shape[0]
+        weights = (unslab(own_qkv, w_qkv.shape[1]), own_up[:cut], unslab(own_up[cut:], w_up.shape[1]), own_down)
+        packed = jnp.concatenate([g.reshape(-1, LANES) for g in gain_grads])
+        packed = jnp.pad(packed, ((0, -packed.shape[0] % 8), (0, 0)))
+        for move in (over_core, over_x, over_y, lambda v: across_z(v, 1), lambda v: across_z(v, 2)):
+            packed = packed + move(packed)
+        me = index(*place())
+        summed, at = [], 0
+        for size, full in zip(sizes, gain_grads):
+            flat = packed[at : at + full.size // LANES].reshape(-1)
+            summed.append(lax.dynamic_slice(flat, (me * size,), (size,)))
+            at += full.size // LANES
+        return (result, grad_tokens) + weights + tuple(summed)
+
+    def scatter(g):
+        return lax.psum_scatter(g, AXES, scatter_dimension=0, tiled=True)
+
+    order_of = (grad_qkv[0], grad_up[0], grad_up[1], grad_down[0])
+    weights = tuple(scatter(g.astype(BF)).astype(F32) for g in order_of)
+    return (result, grad_tokens) + weights + tuple(scatter(g.reshape(-1)) for g in gain_grads)
 
 
 def solution(mesh):
     matrix, vector = P(AXES, None), P(AXES)
+    fast = mesh.shape["dp"] == 4 and mesh.shape["fsdp"] == 2 * Z
     return jax.shard_map(
-        local,
+        functools.partial(local, fast),
         mesh=mesh,
         in_specs=(matrix,) * 7 + (vector,) * 4,
         out_specs=(matrix,) * 6 + (vector,) * 4,

time: 772 us -> 418 us (0.54)
  waiting for transfers between devices: 445 us -> 113 us
  blocking collectives: 82.3 us -> 0 us
  starting transfers between devices: 0.53 us -> 63.4 us
  between operations: 14.6 us -> 1.96 us
  local copies, waits for them, and re-layouts: 21.2 us -> 31.9 us
    reduce_scatter x4 -> x0, waiting for transfers between devices: 303 us -> none  [scatter(): return lax.psum_scatter(g, AXES, scatter_dimension=0, tiled=True)]
    all_gather x4 -> x0, waiting for transfers between devices: 140 us -> none  [gather(): return lax.all_gather(x, AXES, axis=0, tiled=True)]
    ppermute x0 -> x62, waiting for transfers between devices: none -> 113 us  [permute(): lax.ppermute(value, AXES, [(index(*p), index(*move(*p))) for p in places])]
    unnamed x2 -> x0, blocking collectives: 82.3 us -> none
    ppermute x0 -> x62, starting transfers between devices: none -> 63.4 us  [permute(): lax.ppermute(value, AXES, [(index(*p), index(*move(*p))) for p in places])]
    convert_element_type x8 -> x0, other arithmetic: 24.5 us -> none  [the longest x4 18.2 us: local(): g.astype(BF)]
    another operation x0 -> x13, other arithmetic: none -> 9.26 us
    unnamed x52 -> x96, local copies, waits for them, and re-layouts: 19.1 us -> 21.1 us
  transfers between devices with their start and end apart: 8 -> 62, of which waited for: 7 -> 26; matrix products, arithmetic and copies ran while one was open for 4% -> 9% of each run, Pallas kernels for 14% -> 16%
where the time goes in v2:
time: 418 us; the launch traced here: 411 us
  Pallas kernels  176 us (42%)
  waiting for transfers between devices  113 us (27%)
  starting transfers between devices  63.4 us (15%)
  local copies, waits for them, and re-layouts  31.9 us (8%)
  other arithmetic  24.5 us (6%)
    ppermute x62, waiting for transfers between devices, permute(): lax.ppermute(value, AXES, [(index(*p), index(*move(*p))) for p in places])  113 us
    pallas_call x3, Pallas kernels, prefetched2(): pl.pallas_call(kernel, grid_spec=pltpu.PrefetchScalarGridSpec(num_scalar_...  77.7 us
    ppermute x62, starting transfers between devices, permute(): lax.ppermute(value, AXES, [(index(*p), index(*move(*p))) for p in places])  63.4 us
    pallas_call x1, Pallas kernels, attention_backward(): pl.pallas_call(functools.partial(attention_backward_kernel, wide), grid_s...  34.5 us
    pallas_call x2, Pallas kernels, prefetched(): pl.pallas_call(kernel, grid_spec=pltpu.PrefetchScalarGridSpec(num_scalar_...  33 us
    pallas_call x1, Pallas kernels, attention_forward(): pl.pallas_call(functools.partial(attention_forward_kernel, wide), grid_sp...  21.6 us
    unnamed x96, local copies, waits for them, and re-layouts  21.1 us
    pallas_call x1, Pallas kernels, qkv_backward(): pl.pallas_call(qkv_back_kernel, grid=(t // BLOCK,), in_specs=[rows(d)] *...  9.26 us
  transfers between devices with their start and end apart: 62, of which 26 were waited for; matrix products, arithmetic and copies ran while one was open for 9% of the time, Pallas kernels for 16%

profile of v2, /device:TPU:0, one launch (start us, length us, event | category | flops | bytes accessed | tf_op | source)
XLA Modules:
  0.0 411.1 jit_solution(12934423243689623623)
XLA Ops:
  14.4 4.2 %collective-permute-done = bf16[80,768]{1,0:T(8,128)(2,1)S(1)} collective-permute-done((bf16[80,768]{1,0:T(8,128)(2,1)S(1)}, bf16[80,768]{1,0:T(8,128)(2,1)S(1)}, u32[]{:S(2)}, u32[]{:S(2)}) %collective-permute-start) | collective-permute-done | bytes 122912 | tf_op jit(solution)/shard_map/ppermute | solution.py:735
  21.7 5.8 %collective-permute-done.1 = bf16[2,80,768]{2,1,0:T(8,128)(2,1)S(1)} collective-permute-done((bf16[2,80,768]{2,1,0:T(8,128)(2,1)S(1)}, bf16[2,80,768]{2,1,0:T(8,128)(2,1)S(1)}, u32[]{:S(2)}, u32[]{:S(2)}) %collective-permute-start.1) | collective-permute-done | bytes 245792 | tf_op jit(solution)/shard_map/ppermute | solution.py:735
  29.9 3.8 collective-permute-start.15
  33.7 5.6 %collective-permute-done.14 = bf16[120,768]{1,0:T(8,128)(2,1)S(1)} collective-permute-done((bf16[120,768]{1,0:T(8,128)(2,1)S(1)}, bf16[120,768]{1,0:T(8,128)(2,1)S(1)}, u32[]{:S(2)}, u32[]{:S(2)}) %collective-permute-start.14) | collective-permute-done | bytes 184352 | tf_op jit(solution)/shard_map/ppermute | solution.py:735
  40.1 5.9 %collective-permute-done.11 = bf16[120,768]{1,0:T(8,128)(2,1)S(1)} collective-permute-done((bf16[120,768]{1,0:T(8,128)(2,1)S(1)}, bf16[120,768]{1,0:T(8,128)(2,1)S(1)}, u32[]{:S(2)}, u32[]{:S(2)}) %collective-permute-start.11) | collective-permute-done | bytes 184352 | tf_op jit(solution)/shard_map/ppermute | solution.py:735
  53.3 4.4 %collective-permute-done.12 = bf16[2,120,768]{2,1,0:T(8,128)(2,1)S(1)} collective-permute-done((bf16[2,120,768]{2,1,0:T(8,128)(2,1)S(1)}, bf16[2,120,768]{2,1,0:T(8,128)(2,1)S(1)}, u32[]{:S(2)}, u32[]{:S(2)}) %collective-permute-start.12) | collective-permute-done | bytes 368672 | tf_op jit(solution)/shard_map/ppermute | solution.py:735
  62.9 15.7 %collective-permute-done.27 = bf16[2,96,768]{2,1,0:T(8,128)(2,1)} collective-permute-done((bf16[2,96,768]{2,1,0:T(8,128)(2,1)S(1)}, bf16[2,96,768]{2,1,0:T(8,128)(2,1)}, u32[]{:S(2)}, u32[]{:S(2)}) %collective-permute-start.27) | collective-permute-done | bytes 294944 | tf_op jit(solution)/shard_map/ppermute | solution.py:735
  84.6 11.3 %collective-permute-done.28.refs_12_ = bf16[4,96,768]{2,1,0:T(8,128)(2,1)S(1)} collective-permute-done((bf16[4,96,768]{2,1,0:T(8,128)(2,1)S(1)}, bf16[4,96,768]{2,1,0:T(8,128)(2,1)S(1)}, u32[]{:S(2)}, u32[]{:S(2)}) %collective-permute-start.28) | collective-permute-done | bytes 589856 | tf_op jit(solution)/shard_map/ppermute | solution.py:735
  95.9 6.0 %collective-permute-done.23 = bf16[2,96,768]{2,1,0:T(8,128)(2,1)} collective-permute-done((bf16[2,96,768]{2,1,0:T(8,128)(2,1)S(1)}, bf16[2,96,768]{2,1,0:T(8,128)(2,1)}, u32[]{:S(2)}, u32[]{:S(2)}) %collective-permute-start.23) | collective-permute-done | bytes 294944 | tf_op jit(solution)/shard_map/ppermute | solution.py:735
  110.8 10.6 %qkv_forward.1 = (bf16[1024,768]{1,0:T(8,128)(2,1)S(1)}, bf16[1024,2304]{1,0:T(8,128)(2,1)}, bf16[768,2304]{1,0:T(8,128)(2,1)S(1)}, f32[1,768]{1,0:T(1,128)S(1)}...) custom-call(s32[32]{0:T(128)S(1)} %stack.268.refs_0_, bf16[1024,768]{1,0:T(8,128)(2,1)S(1)} %copy-done.9, ...), custom_call_target="tpu_custom_call" | custom-call | flops 3623878656 | bytes 16515072 | tf_op jit(solution)/shard_map/qkv_forward/pallas_call | solution.py:181
  125.7 21.6 %attention_forward.1 = (f32[1024,768]{1,0:T(8,128)S(1)}, f32[6,8,1024]{2,1,0:T(8,128)S(1)}) custom-call(s32[4]{0:T(128)S(1)} %add_bitcast_fusion.reach, bf16[1024,2304]{1,0:T(8,128)(2,1)S(1)} %copy-done, bf16[1024,2304]{1,0:T(8,128)(2,1)S(1)} %copy-done, bf16[1024,2304]{1,0:T(8,128)(2,1)S(1)} %copy-done, s32[1024,1]{1,0:T(8,128)S(1)} %copy.22.start_ref), custom_call_target="tpu_custom_call" | custom-call | flops 1610612736 | bytes 9437184 | tf_op jit(solution)/shard_map/attention_forward/pallas_call | solution.py:292
  149.8 22.5 %up_forward.1 = (bf16[1024,768]{1,0:T(8,128)(2,1)}, f32[1024,768]{1,0:T(8,128)}, bf16[1024,768]{1,0:T(8,128)(2,1)}, bf16[1024,3072]{1,0:T(8,128)(2,1)}, bf16[102...) custom-call(s32[32]{0:T(128)} %copy-done.6, ...), custom_call_target="tpu_custom_call" | custom-call | flops 6039797760 | bytes 35389440 | tf_op jit(solution)/shard_map/up_forward/pallas_call | solution.py:181
  173.7 33.1 %down_both.1 = (bf16[1024,768]{1,0:T(8,128)(2,1)}, bf16[1024,3072]{1,0:T(8,128)(2,1)}, f32[1,3072]{1,0:T(1,128)}, f32[16,96,768]{2,1,0:T(8,128)}, bf16[16,96,768]{2,1,0:T(8,128)(2,1)}) custom-call(s32[32]{0:T(128)} %copy-done.6, s32[32]{0:T(128)} %stack.293.refs_1_, bf16[1024,3072]{1,0:T(8,128)(2,1)} %get-tuple-element.56.refs_2_, ...), custom_call_target="tpu_custom_call" | custom-call | flops 14495514624 | bytes 39321600 | tf_op jit(solution)/shard_map/down_both/pallas_call | solution.py:543
  206.8 33.3 %up_backward.1 = (f32[1024,768]{1,0:T(8,128)}, bf16[1024,768]{1,0:T(8,128)(2,1)}, f32[1,768]{1,0:T(1,128)}, f32[1,768]{1,0:T(1,128)}, f32[16,120,768]{2,1,0:T(8,128)}, /*index=5*/bf16[16,120,768]{2,1,0:T(8,128)(2,1)}) custom-call(s32[32]{0:T(128)} %copy-done.6, s32[32]{0:T(128)} %stack.293.refs_1_, bf16[1024,3072]{1,0:T(8,128)(2,1)} %get-tuple-element.63.refs_2_, ...), custom_call_target="tpu_custom_call" | custom-call | flops 12079595520 | bytes 42860544 | tf_op jit(solution)/shard_map/up_backward/pallas_call | solution.py:543
  242.6 34.5 %attention_backward.1 = (bf16[1024,768]{1,0:T(8,128)(2,1)S(1)}, bf16[1024,768]{1,0:T(8,128)(2,1)S(1)}, bf16[1024,768]{1,0:T(8,128)(2,1)S(1)}) custom-call(s32[4]{0:T(128)S(1)} %add_bitcast_fusion.reach, bf16[1024,2304]{1,0:T(8,128)(2,1)} %get-tuple-element.49.q_ref.k_ref.v_ref, bf16[1024,2304]{1,0:T(8,128)(2,1)} %get-tuple-element.49.q_ref.k_ref.v_ref, ...), custom_call_target="tpu_custom_call" | custom-call | flops 4026531840 | bytes 15728640 | tf_op jit(solution)/shard_map/attention_backward/pallas_call | solution.py:392
  277.2 11.3 %qkv_weight_grad.1 = (f32[16,72,768]{2,1,0:T(8,128)S(1)}, bf16[16,72,768]{2,1,0:T(8,128)(2,1)}) custom-call(s32[32]{0:T(128)S(1)} %copy-done.7, s32[32]{0:T(128)S(1)} %copy-done.8, bf16[1024,768]{1,0:T(8,128)(2,1)S(1)} %copy-done.22, bf16[1024,768]{1,0:T(8,128)(2,1)S(1)} %get-tuple-element.70.dq_ref.refs_3_, ...), custom_call_target="tpu_custom_call" | custom-call | flops 3623878656 | bytes 13369344 | tf_op jit(solution)/shard_map/qkv_weight_grad/pallas_call | solution.py:543
  297.1 9.3 %qkv_backward.1 = (f32[1024,768]{1,0:T(8,128)}, f32[1,768]{1,0:T(1,128)S(1)}) custom-call(bf16[1024,768]{1,0:T(8,128)(2,1)S(1)} %copy-done.11, bf16[1024,768]{1,0:T(8,128)(2,1)S(1)} %copy-done.13, bf16[1024,768]{1,0:T(8,128)(2,1)S(1)} %copy-done.15, bf16[1024,768]{1,0:T(8,128)(2,1)} %x_ref.1, f32[1024,768]{1,0:T(8,128)} %get-tuple-element.73.dx1_ref, ...), custom_call_target="tpu_custom_call" | custom-call | flops 3623878656 | bytes 16121856 | tf_op jit(solution)/shard_map/qkv_backward/pallas_call | solution.py:693
  320.5 4.4 %collective-permute-done.61 = f32[8,768]{1,0:T(8,128)} collective-permute-done((f32[8,768]{1,0:T(8,128)}, f32[8,768]{1,0:T(8,128)}, u32[]{:S(2)}, u32[]{:S(2)}) %collective-permute-start.61) | collective-permute-done | bytes 24608 | tf_op jit(solution)/shard_map/ppermute | solution.py:735
  334.7 4.5 %collective-permute-done.34 = bf16[4,72,768]{2,1,0:T(8,128)(2,1)S(1)} collective-permute-done((bf16[4,72,768]{2,1,0:T(8,128)(2,1)S(1)}, bf16[4,72,768]{2,1,0:T(8,128)(2,1)S(1)}, u32[]{:S(2)}, u32[]{:S(2)}) %collective-permute-start.34) | collective-permute-done | bytes 442400 | tf_op jit(solution)/shard_map/ppermute | solution.py:735
  343.1 4.0 fusion.26
  357.4 5.1 %collective-permute-done.39 = bf16[72,768]{1,0:T(8,128)(2,1)S(1)} collective-permute-done((bf16[72,768]{1,0:T(8,128)(2,1)S(1)}, bf16[72,768]{1,0:T(8,128)(2,1)S(1)}, u32[]{:S(2)}, u32[]{:S(2)}) %collective-permute-start.39) | collective-permute-done | bytes 110624 | tf_op jit(solution)/shard_map/ppermute | solution.py:735
  377.0 7.8 %collective-permute-done.42 = bf16[4,120,768]{2,1,0:T(8,128)(2,1)S(1)} collective-permute-done((bf16[4,120,768]{2,1,0:T(8,128)(2,1)S(1)}, bf16[4,120,768]{2,1,0:T(8,128)(2,1)S(1)}, u32[]{:S(2)}, u32[]{:S(2)}) %collective-permute-start.42) | collective-permute-done | bytes 737312 | tf_op jit(solution)/shard_map/ppermute | solution.py:735
  393.1 4.7 %collective-permute-done.43 = bf16[2,120,768]{2,1,0:T(8,128)(2,1)S(1)} collective-permute-done((bf16[2,120,768]{2,1,0:T(8,128)(2,1)S(1)}, bf16[2,120,768]{2,1,0:T(8,128)(2,1)S(1)}, u32[]{:S(2)}, u32[]{:S(2)}) %collective-permute-start.43) | collective-permute-done | bytes 368672 | tf_op jit(solution)/shard_map/ppermute | solution.py:735
  404.4 5.0 %collective-permute-done.47 = bf16[120,768]{1,0:T(8,128)(2,1)S(1)} collective-permute-done((bf16[120,768]{1,0:T(8,128)(2,1)S(1)}, bf16[120,768]{1,0:T(8,128)(2,1)S(1)}, u32[]{:S(2)}, u32[]{:S(2)}) %collective-permute-start.47) | collective-permute-done | bytes 184352 | tf_op jit(solution)/shard_map/ppermute | solution.py:735
  (286 shorter events, 134.8 us)
Async XLA Ops:
  21.0 19.0 %collective-permute-start.6 = (bf16[4,80,768]{2,1,0:T(8,128)(2,1)S(1)}, bf16[4,80,768]{2,1,0:T(8,128)(2,1)S(1)}, u32[]{:S(2)}, u32[]{:S(2)}) collective-permute-start(bf16[4,80,768]{2,1,0:T(8,128)(2,1)S(1)} %pad_maximum_fusion.5.refs_6_), channel_id=1, source_target_pairs={{0,16},{1,17},{2,18},{3,19},{4,20},{5,21},{6,22},{7,23},{8,24},{9,... | collective-permute-start | bytes 1474568 | tf_op jit(solution)/shard_map/ppermute | solution.py:735
  48.5 31.1 %collective-permute-start.17 = (bf16[4,120,768]{2,1,0:T(8,128)(2,1)}, bf16[4,120,768]{2,1,0:T(8,128)(2,1)}, u32[]{:S(2)}, u32[]{:S(2)}) collective-permute-start(bf16[4,120,768]{2,1,0:T(8,128)(2,1)} %pad_maximum_fusion.1.refs_8_), channel_id=1, source_target_pairs={{0,16},{1,17},{2,18},{3,19},{4,20},{5,21},{6,22},{7,23},{8,24},{9,... | collective-permute-start | bytes 2211848 | tf_op jit(solution)/shard_map/ppermute | solution.py:735
  58.6 23.3 %collective-permute-start.13 = (bf16[4,120,768]{2,1,0:T(8,128)(2,1)}, bf16[4,120,768]{2,1,0:T(8,128)(2,1)}, u32[]{:S(2)}, u32[]{:S(2)}) collective-permute-start(bf16[4,120,768]{2,1,0:T(8,128)(2,1)} %pad_maximum_fusion.refs_6_), channel_id=1, source_target_pairs={{0,1},{1,0},{2,3},{3,2},{4,5},{5,4},{6,7},{7,6},{8,9},{9,8},{10,11... | collective-permute-start | bytes 2211848 | tf_op jit(solution)/shard_map/ppermute | solution.py:735
  59.2 19.4 %collective-permute-start.27 = (bf16[2,96,768]{2,1,0:T(8,128)(2,1)S(1)}, bf16[2,96,768]{2,1,0:T(8,128)(2,1)}, u32[]{:S(2)}, u32[]{:S(2)}) collective-permute-start(bf16[2,96,768]{2,1,0:T(8,128)(2,1)S(1)} %pad_maximum_fusion.9), channel_id=1, source_target_pairs={{0,1},{1,0},{2,3},{3,2},{4,5},{5,4},{6,7},{7,6},{8,9},{9,8},{10,11... | collective-permute-start | bytes 884744 | tf_op jit(solution)/shard_map/ppermute | solution.py:735
  60.8 21.6 %collective-permute-start.9 = (bf16[4,80,768]{2,1,0:T(8,128)(2,1)S(1)}, bf16[4,80,768]{2,1,0:T(8,128)(2,1)S(1)}, u32[]{:S(2)}, u32[]{:S(2)}) collective-permute-start(bf16[4,80,768]{2,1,0:T(8,128)(2,1)S(1)} %pad_maximum_fusion.5.refs_6_), channel_id=1, source_target_pairs={{0,8},{1,9},{2,10},{3,11},{4,12},{5,13},{6,14},{7,15},{8,0},{9,1},... | collective-permute-start | bytes 1474568 | tf_op jit(solution)/shard_map/ppermute | solution.py:735
  61.0 21.1 %collective-permute-start.22 = (bf16[96,768]{1,0:T(8,128)(2,1)S(1)}, bf16[96,768]{1,0:T(8,128)(2,1)S(1)}, u32[]{:S(2)}, u32[]{:S(2)}) collective-permute-start(bf16[96,768]{1,0:T(8,128)(2,1)S(1)} %copy-done.26), channel_id=1, source_target_pairs={{0,4},{1,5},{2,6},{3,7},{4,0},{5,1},{6,2},{7,3},{8,12},{9,13},{10,... | collective-permute-start | bytes 442376 | tf_op jit(solution)/shard_map/ppermute | solution.py:735
  81.8 22.4 %collective-permute-start.10 = (bf16[4,80,768]{2,1,0:T(8,128)(2,1)S(1)}, bf16[4,80,768]{2,1,0:T(8,128)(2,1)}, u32[]{:S(2)}, u32[]{:S(2)}) collective-permute-start(bf16[4,80,768]{2,1,0:T(8,128)(2,1)S(1)} %collective-permute-done.6.refs_7_), channel_id=1, source_target_pairs={{0,8},{1,9},{2,10},{3,11},{4,12},{5,13},{6,14},{7,15},{8,0},{9,1},... | collective-permute-start | bytes 1474568 | tf_op jit(solution)/shard_map/ppermute | solution.py:735
  82.1 22.5 %collective-permute-start.8 = (bf16[4,80,768]{2,1,0:T(8,128)(2,1)S(1)}, bf16[4,80,768]{2,1,0:T(8,128)(2,1)}, u32[]{:S(2)}, u32[]{:S(2)}) collective-permute-start(bf16[4,80,768]{2,1,0:T(8,128)(2,1)S(1)} %collective-permute-done.2.refs_5_), channel_id=1, source_target_pairs={{0,8},{1,9},{2,10},{3,11},{4,12},{5,13},{6,14},{7,15},{8,0},{9,1},... | collective-permute-start | bytes 1474568 | tf_op jit(solution)/shard_map/ppermute | solution.py:735
  82.4 19.5 %collective-permute-start.23 = (bf16[2,96,768]{2,1,0:T(8,128)(2,1)S(1)}, bf16[2,96,768]{2,1,0:T(8,128)(2,1)}, u32[]{:S(2)}, u32[]{:S(2)}) collective-permute-start(bf16[2,96,768]{2,1,0:T(8,128)(2,1)S(1)} %pad_maximum_fusion.8), channel_id=1, source_target_pairs={{0,16},{1,17},{2,18},{3,19},{4,20},{5,21},{6,22},{7,23},{8,24},{9,... | collective-permute-start | bytes 884744 | tf_op jit(solution)/shard_map/ppermute | solution.py:735
  84.5 36.9 %collective-permute-start.20 = (bf16[4,120,768]{2,1,0:T(8,128)(2,1)}, bf16[4,120,768]{2,1,0:T(8,128)(2,1)}, u32[]{:S(2)}, u32[]{:S(2)}) collective-permute-start(bf16[4,120,768]{2,1,0:T(8,128)(2,1)} %pad_maximum_fusion.1.refs_8_), channel_id=1, source_target_pairs={{0,8},{1,9},{2,10},{3,11},{4,12},{5,13},{6,14},{7,15},{8,0},{9,1},... | collective-permute-start | bytes 2211848 | tf_op jit(solution)/shard_map/ppermute | solution.py:735
  95.9 25.6 %collective-permute-start.18 = (bf16[4,120,768]{2,1,0:T(8,128)(2,1)}, bf16[4,120,768]{2,1,0:T(8,128)(2,1)}, u32[]{:S(2)}, u32[]{:S(2)}) collective-permute-start(bf16[4,120,768]{2,1,0:T(8,128)(2,1)} %pad_maximum_fusion.refs_6_), channel_id=1, source_target_pairs={{0,8},{1,9},{2,10},{3,11},{4,12},{5,13},{6,14},{7,15},{8,0},{9,1},... | collective-permute-start | bytes 2211848 | tf_op jit(solution)/shard_map/ppermute | solution.py:735
  101.9 20.1 %collective-permute-start.21 = (bf16[4,120,768]{2,1,0:T(8,128)(2,1)}, bf16[4,120,768]{2,1,0:T(8,128)(2,1)}, u32[]{:S(2)}, u32[]{:S(2)}) collective-permute-start(bf16[4,120,768]{2,1,0:T(8,128)(2,1)} %collective-permute-done.17.refs_9_), channel_id=1, source_target_pairs={{0,8},{1,9},{2,10},{3,11},{4,12},{5,13},{6,14},{7,15},{8,0},{9,1},... | collective-permute-start | bytes 2211848 | tf_op jit(solution)/shard_map/ppermute | solution.py:735
  104.2 44.7 %collective-permute-start.19 = (bf16[4,120,768]{2,1,0:T(8,128)(2,1)}, bf16[4,120,768]{2,1,0:T(8,128)(2,1)S(1)}, u32[]{:S(2)}, u32[]{:S(2)}) collective-permute-start(bf16[4,120,768]{2,1,0:T(8,128)(2,1)} %collective-permute-done.13.refs_7_), channel_id=1, source_target_pairs={{0,8},{1,9},{2,10},{3,11},{4,12},{5,13},{6,14},{7,15},{8,0},{9,1},... | collective-permute-start | bytes 2211848 | tf_op jit(solution)/shard_map/ppermute | solution.py:735
  104.6 17.6 %collective-permute-start.24 = (bf16[4,96,768]{2,1,0:T(8,128)(2,1)S(1)}, bf16[4,96,768]{2,1,0:T(8,128)(2,1)S(1)}, u32[]{:S(2)}, u32[]{:S(2)}) collective-permute-start(bf16[4,96,768]{2,1,0:T(8,128)(2,1)S(1)} %pad_maximum_fusion.2.refs_9_), channel_id=1, source_target_pairs={{0,1},{1,0},{2,3},{3,2},{4,5},{5,4},{6,7},{7,6},{8,9},{9,8},{10,11... | collective-permute-start | bytes 1769480 | tf_op jit(solution)/shard_map/ppermute | solution.py:735
  121.4 50.9 %collective-permute-start.31 = (bf16[4,96,768]{2,1,0:T(8,128)(2,1)S(1)}, bf16[4,96,768]{2,1,0:T(8,128)(2,1)S(1)}, u32[]{:S(2)}, u32[]{:S(2)}) collective-permute-start(bf16[4,96,768]{2,1,0:T(8,128)(2,1)S(1)} %copy-done.29), channel_id=1, source_target_pairs={{0,8},{1,9},{2,10},{3,11},{4,12},{5,13},{6,14},{7,15},{8,0},{9,1},... | collective-permute-start | bytes 1769480 | tf_op jit(solution)/shard_map/ppermute | solution.py:735
  121.5 50.8 %collective-permute-start.32 = (bf16[4,96,768]{2,1,0:T(8,128)(2,1)S(1)}, bf16[4,96,768]{2,1,0:T(8,128)(2,1)S(1)}, u32[]{:S(2)}, u32[]{:S(2)}) collective-permute-start(bf16[4,96,768]{2,1,0:T(8,128)(2,1)S(1)} %copy-done.38), channel_id=1, source_target_pairs={{0,8},{1,9},{2,10},{3,11},{4,12},{5,13},{6,14},{7,15},{8,0},{9,1},... | collective-permute-start | bytes 1769480 | tf_op jit(solution)/shard_map/ppermute | solution.py:735
  122.0 50.3 %collective-permute-start.29 = (bf16[4,96,768]{2,1,0:T(8,128)(2,1)S(1)}, bf16[4,96,768]{2,1,0:T(8,128)(2,1)S(1)}, u32[]{:S(2)}, u32[]{:S(2)}) collective-permute-start(bf16[4,96,768]{2,1,0:T(8,128)(2,1)S(1)} %pad_maximum_fusion.2.refs_9_), channel_id=1, source_target_pairs={{0,8},{1,9},{2,10},{3,11},{4,12},{5,13},{6,14},{7,15},{8,0},{9,1},... | collective-permute-start | bytes 1769480 | tf_op jit(solution)/shard_map/ppermute | solution.py:735
  122.1 50.2 %collective-permute-start.30 = (bf16[4,96,768]{2,1,0:T(8,128)(2,1)S(1)}, bf16[4,96,768]{2,1,0:T(8,128)(2,1)S(1)}, u32[]{:S(2)}, u32[]{:S(2)}) collective-permute-start(bf16[4,96,768]{2,1,0:T(8,128)(2,1)S(1)} %collective-permute-done.24.refs_10_), channel_id=1, source_target_pairs={{0,8},{1,9},{2,10},{3,11},{4,12},{5,13},{6,14},{7,15},{8,0},{9,1},... | collective-permute-start | bytes 1769480 | tf_op jit(solution)/shard_map/ppermute | solution.py:735
  288.4 39.7 %collective-permute-start.33 = (bf16[16,72,768]{2,1,0:T(8,128)(2,1)}, bf16[16,72,768]{2,1,0:T(8,128)(2,1)}, u32[]{:S(2)}, u32[]{:S(2)}) collective-permute-start(bf16[16,72,768]{2,1,0:T(8,128)(2,1)} %get-tuple-element.79), channel_id=1, source_target_pairs={{0,8},{1,9},{2,10},{3,11},{4,12},{5,13},{6,14},{7,15},{8,0},{9,1},... | collective-permute-start | bytes 5308424 | tf_op jit(solution)/shard_map/ppermute | solution.py:735
  288.5 54.5 %collective-permute-start.49 = (bf16[16,96,768]{2,1,0:T(8,128)(2,1)}, bf16[16,96,768]{2,1,0:T(8,128)(2,1)}, u32[]{:S(2)}, u32[]{:S(2)}) collective-permute-start(bf16[16,96,768]{2,1,0:T(8,128)(2,1)} %get-tuple-element.83), channel_id=1, source_target_pairs={{0,8},{1,9},{2,10},{3,11},{4,12},{5,13},{6,14},{7,15},{8,0},{9,1},... | collective-permute-start | bytes 7077896 | tf_op jit(solution)/shard_map/ppermute | solution.py:735
  320.5 42.9 %collective-permute-start.41 = (bf16[16,120,768]{2,1,0:T(8,128)(2,1)}, bf16[16,120,768]{2,1,0:T(8,128)(2,1)}, u32[]{:S(2)}, u32[]{:S(2)}) collective-permute-start(bf16[16,120,768]{2,1,0:T(8,128)(2,1)} %get-tuple-element.81), channel_id=1, source_target_pairs={{0,8},{1,9},{2,10},{3,11},{4,12},{5,13},{6,14},{7,15},{8,0},{9,1},... | collective-permute-start | bytes 8847368 | tf_op jit(solution)/shard_map/ppermute | solution.py:735
  366.4 18.5 %collective-permute-start.42 = (bf16[4,120,768]{2,1,0:T(8,128)(2,1)S(1)}, bf16[4,120,768]{2,1,0:T(8,128)(2,1)S(1)}, u32[]{:S(2)}, u32[]{:S(2)}) collective-permute-start(bf16[4,120,768]{2,1,0:T(8,128)(2,1)S(1)} %get-tuple-element.101), channel_id=1, source_target_pairs={{0,1},{1,0},{2,3},{3,2},{4,5},{5,4},{6,7},{7,6},{8,9},{9,8},{10,11... | collective-permute-start | bytes 2211848 | tf_op jit(solution)/shard_map/ppermute | solution.py:735
  373.1 27.4 %collective-permute-start.54 = (bf16[96,768]{1,0:T(8,128)(2,1)S(1)}, bf16[96,768]{1,0:T(8,128)(2,1)S(1)}, u32[]{:S(2)}, u32[]{:S(2)}) collective-permute-start(bf16[96,768]{1,0:T(8,128)(2,1)S(1)} %get-tuple-element.113), channel_id=1, source_target_pairs={{0,2},{1,3},{2,4},{3,5},{4,6},{5,7},{6,0},{7,1},{8,10},{9,11},{10,... | collective-permute-start | bytes 442376 | tf_op jit(solution)/shard_map/ppermute | solution.py:735
  373.2 27.4 %collective-permute-start.56 = (bf16[96,768]{1,0:T(8,128)(2,1)S(1)}, bf16[96,768]{1,0:T(8,128)(2,1)S(1)}, u32[]{:S(2)}, u32[]{:S(2)}) collective-permute-start(bf16[96,768]{1,0:T(8,128)(2,1)S(1)} %get-tuple-element.114), channel_id=1, source_target_pairs={{0,6},{1,7},{2,0},{3,1},{4,2},{5,3},{6,4},{7,5},{8,14},{9,15},{10,... | collective-permute-start | bytes 442376 | tf_op jit(solution)/shard_map/ppermute | solution.py:735
  (84 other events, 939.5 us)

commit v3 on v2

--- a/solution.py
+++ b/solution.py
@@ -93,7 +93,7 @@
         pltpu.make_async_copy(buffer, buffer, sem).wait()
 
 
-def deal(order, total, keep_ref, send_ref, places):
+def deal(order, keep_ref, send_ref, places):
     half = keep_ref.shape[0]
 
     def one(j, target, at):
@@ -380,27 +380,27 @@
     dv_ref[...] = dv_acc[...].astype(BF)
 
 
-def attention_backward(reach, qkv, d_mixed, mixed, lse, start_row, cos, sin, row_count, wide):
+def attention_backward(reach, qkv, d_mixed, mixed, lse, start_row, cos, sin, row_count, wide, base, pairs):
     t = qkv.shape[0]
     seq = t // row_count
-    d = qkv.shape[1] // 3
+    d = pairs * PAIR
 
     def columns(part):
-        return pl.BlockSpec((seq, PAIR), lambda r, p, *_: (r, part * PAIRS + p))
+        return pl.BlockSpec((seq, PAIR), lambda r, p, *_: (r, part * PAIRS + base + p))
 
     table = pl.BlockSpec((seq, PAIR), lambda r, p, *_: (r, 0))
     return pl.pallas_call(
         functools.partial(attention_backward_kernel, wide),
         grid_spec=pltpu.PrefetchScalarGridSpec(
             num_scalar_prefetch=1,
-            grid=(row_count, PAIRS),
+            grid=(row_count, pairs),
             in_specs=[
                 columns(0), columns(1), columns(2), columns(0), columns(0),
-                pl.BlockSpec((1, 8, seq), lambda r, p, *_: (r * PAIRS + p, 0, 0)),
+                pl.BlockSpec((1, 8, seq), lambda r, p, *_: (r * PAIRS + base + p, 0, 0)),
                 pl.BlockSpec((8, seq), lambda r, p, *_: (r, 0)),
                 table, table,
             ],
-            out_specs=[columns(0)] * 3,
+            out_specs=[pl.BlockSpec((seq, PAIR), lambda r, p, *_: (r, p))] * 3,
             scratch_shapes=[
                 pltpu.VMEM((wide * BLOCK, seq), F32),
                 pltpu.VMEM((2, seq, PAIR), BF),
@@ -529,7 +529,7 @@
 
         @pl.when(step == pl.num_programs(0) - 1)
         def _():
-            deal(back, total, keep_ref, send_ref, [(0, f // 32, total, 0)])
+            deal(back, keep_ref, send_ref, [(0, f // 32, total, 0)])
 
 
 def dealt(split, size, shapes):
@@ -568,24 +568,17 @@
     )
 
 
-def up_back_kernel(split, *refs):
-    order, back, dpre_ref, h2_ref, x1_ref, ct_ref, valid_ref, a_ref, o_ref, wu_ref, wo_ref, gf_ref, gi_ref, *refs = refs
-    dx1_ref, do_ref, ggf_ref, ggi_ref, *refs = refs
-    if split:
-        keep_ref, send_ref, gwo_ref, gwu_ref = refs
-    else:
-        gwo_ref, gwu_ref = refs
+def up_back_kernel(dpre_ref, x1_ref, ct_ref, valid_ref, o_ref, wu_ref, wo_ref, gf_ref, gi_ref,
+                   dx1_ref, low_ref, do_ref, ggf_ref, ggi_ref):
     step = pl.program_id(0)
-    dpre = dpre_ref[...]
-    part_up = dot(h2_ref[...], dpre, ((0,), (0,)))
-    dh2 = dot(dpre, wu_ref[...], ((1,), (1,)))
+    dh2 = dot(dpre_ref[...], wu_ref[...], ((1,), (1,)))
     unit, inv = unit_norm(x1_ref[...])
     ffn_part = jnp.sum(dh2 * unit, axis=0, keepdims=True)
     gy = jnp.where(valid_ref[...] > 0, ct_ref[...].astype(F32), 0.0)
     dx1 = gy + norm_back(dh2, gf_ref[...], unit, inv)
     dx1_ref[...] = dx1
     low = dx1.astype(BF)
-    part_out = dot(a_ref[...], low, ((0,), (0,)))
+    low_ref[...] = low
     da = dot(low, wo_ref[...], ((1,), (1,)))
     unit, inv = unit_norm(o_ref[...])
     inner_part = jnp.sum(da * unit, axis=0, keepdims=True)
@@ -593,17 +586,52 @@
 
     @pl.when(step == 0)
     def _():
+        ggf_ref[...] = ffn_part
+        ggi_ref[...] = inner_part
+
+    @pl.when(step > 0)
+    def _():
+        ggf_ref[...] += ffn_part
+        ggi_ref[...] += inner_part
+
+
+def up_backward(dpre, x1, cotangent, valid, mixed, w_up, w_out, gain_ffn, gain_inner):
+    t, d = x1.shape
+    f = dpre.shape[1]
+    return pl.pallas_call(
+        up_back_kernel,
+        grid=(t // BLOCK,),
+        in_specs=[rows(f), rows(d), rows(d), rows(1), rows(d),
+                  whole((d, f)), whole((d, d)), whole((1, d)), whole((1, d))],
+        out_specs=[rows(d), rows(d), rows(d), whole((1, d)), whole((1, d))],
+        out_shape=[shaped((t, d), F32), shaped((t, d), BF), shaped((t, d), BF), shaped((1, d), F32), shaped((1, d), F32)],
+        compiler_params=params(40),
+        cost_estimate=pl.CostEstimate(
+            flops=2 * t * d * (d + f), transcendentals=0, bytes_accessed=2 * d * (d + f) + 2 * t * f + 24 * t * d
+        ),
+        name="up_backward",
+    )(dpre, x1, cotangent, valid, mixed, w_up, w_out, gain_ffn, gain_inner)
+
+
+def up_grad_kernel(split, *refs):
+    back, h2_ref, dpre_ref, a_ref, low_ref, *refs = refs
+    if split:
+        keep_ref, send_ref, gwo_ref, gwu_ref = refs
+    else:
+        gwo_ref, gwu_ref = refs
+    step = pl.program_id(0)
+    part_up = dot(h2_ref[...], dpre_ref[...], ((0,), (0,)))
+    part_out = dot(a_ref[...], low_ref[...], ((0,), (0,)))
+
+    @pl.when(step == 0)
+    def _():
         gwu_ref[...] = part_up
         gwo_ref[...] = part_out
-        ggf_ref[...] = ffn_part
-        ggi_ref[...] = inner_part
 
     @pl.when(step > 0)
     def _():
         gwu_ref[...] += part_up
         gwo_ref[...] += part_out
-        ggf_ref[...] += ffn_part
-        ggi_ref[...] += inner_part
 
     if split:
         d, f = gwu_ref.shape
@@ -611,37 +639,35 @@
 
         @pl.when(step == pl.num_programs(0) - 1)
         def _():
-            deal(back, None, keep_ref, send_ref, [(0, size, gwo_ref, 0)] + slabs(size, size, gwu_ref, f))
-
-
-def up_backward(split, order, back, dpre, h2, x1, cotangent, valid, a, mixed, w_up, w_out, gain_ffn, gain_inner):
-    t, d = x1.shape
+            deal(back, keep_ref, send_ref, [(0, size, gwo_ref, 0)] + slabs(size, size, gwu_ref, f))
+
+
+def up_weight_grad(split, back, h2, dpre, a, low):
+    t, d = h2.shape
     f = dpre.shape[1]
     out_specs, out_shape, scratch = dealt(split, (d + f) // 32, [(d, d), (d, f)])
-    return prefetched2(
-        functools.partial(up_back_kernel, split), order, back,
-        [dpre, h2, x1, cotangent, valid, a, mixed, w_up, w_out, gain_ffn, gain_inner],
-        [rows(f), rows(d), rows(d), rows(d), rows(1), rows(d), rows(d),
-         whole((d, f)), whole((d, d)), whole((1, d)), whole((1, d))],
-        [rows(d), rows(d), whole((1, d)), whole((1, d))] + out_specs,
-        [shaped((t, d), F32), shaped((t, d), BF), shaped((1, d), F32), shaped((1, d), F32)] + out_shape,
-        scratch, (t // BLOCK,), 60, "up_backward",
-        4 * t * d * (d + f), 6 * d * (d + f) + 2 * t * f + 24 * t * d,
+    return prefetched(
+        functools.partial(up_grad_kernel, split), back, [h2, dpre, a, low],
+        [rows(d), rows(f), rows(d), rows(d)], out_specs, out_shape, scratch, (t // BLOCK,), 56, "up_weight_grad",
+        2 * t * d * (d + f), 6 * d * (d + f) + 2 * t * f + 6 * t * d,
     )
 
 
 def qkv_grad_kernel(split, *refs):
-    order, back, h_ref, dq_ref, dk_ref, dv_ref, *refs = refs
+    back, h_ref, *refs = refs
+    count = len(refs) - 3 if split else len(refs) - 1
+    ins, refs = refs[:count], refs[count:]
     if split:
         keep_ref, send_ref, g_ref = refs
     else:
         (g_ref,) = refs
     step = pl.program_id(0)
     h = h_ref[...]
-    d = h.shape[1]
-    for c, ref in enumerate((dq_ref, dk_ref, dv_ref)):
+    at = 0
+    for ref in ins:
         part = dot(h, ref[...], ((0,), (0,)))
-        cols = slice(c * d, (c + 1) * d)
+        cols = slice(at, at + ref.shape[1])
+        at += ref.shape[1]
 
         @pl.when(step == 0)
         def _():
@@ -652,28 +678,32 @@
             g_ref[:, cols] += part
 
     if split:
+        d, n = g_ref.shape
 
         @pl.when(step == pl.num_programs(0) - 1)
         def _():
-            deal(back, None, keep_ref, send_ref, slabs(0, d // 32, g_ref, 3 * d))
-
-
-def qkv_weight_grad(split, order, back, h, dq, dk, dv):
+            deal(back, keep_ref, send_ref, slabs(0, d // 32, g_ref, n))
+
+
+def qkv_weight_grad(split, back, h, pieces):
     t, d = h.shape
-    out_specs, out_shape, scratch = dealt(split, 3 * d // 32, [(d, 3 * d)])
-    return prefetched2(
-        functools.partial(qkv_grad_kernel, split), order, back,
-        [h, dq, dk, dv], [rows(d)] * 4, out_specs, out_shape, scratch,
-        (t // BLOCK,), 40, "qkv_weight_grad", 6 * t * d * d, 12 * d * d + 8 * t * d,
-    )
-
-
-def qkv_back_kernel(dq_ref, dk_ref, dv_ref, x_ref, dx1_ref, w_ref, gain_ref, dx_ref, gg_ref):
+    n = sum(p.shape[1] for p in pieces)
+    out_specs, out_shape, scratch = dealt(split, n // 32, [(d, n)])
+    return prefetched(
+        functools.partial(qkv_grad_kernel, split), back, [h, *pieces],
+        [rows(d)] + [rows(p.shape[1]) for p in pieces], out_specs, out_shape, scratch,
+        (t // BLOCK,), 40, "qkv_weight_grad", 2 * t * d * n, 4 * d * n + 2 * t * (d + n),
+    )
+
+
+def qkv_back_kernel(starts, *refs):
+    count = len(starts)
+    pieces, refs = refs[:count], refs[count:]
+    x_ref, dx1_ref, w_ref, gain_ref, dx_ref, gg_ref = refs
     step = pl.program_id(0)
-    d = x_ref.shape[1]
     dh = None
-    for c, ref in enumerate((dq_ref, dk_ref, dv_ref)):
-        part = dot(ref[...], w_ref[:, c * d : (c + 1) * d], ((1,), (1,)))
+    for at, ref in zip(starts, pieces):
+        part = dot(ref[...], w_ref[:, at : at + ref.shape[1]], ((1,), (1,)))
         dh = part if dh is None else dh + part
     unit, inv = unit_norm(x_ref[...].astype(F32))
     gain_part = jnp.sum(dh * unit, axis=0, keepdims=True)
@@ -688,18 +718,18 @@
         gg_ref[...] += gain_part
 
 
-def qkv_backward(dq, dk, dv, tokens, dx1, w_qkv, gain):
+def qkv_backward(pieces, starts, tokens, dx1, w_qkv, gain):
     t, d = tokens.shape
     return pl.pallas_call(
-        qkv_back_kernel,
+        functools.partial(qkv_back_kernel, starts),
         grid=(t // BLOCK,),
-        in_specs=[rows(d)] * 5 + [whole((d, 3 * d)), whole((1, d))],
+        in_specs=[rows(p.shape[1]) for p in pieces] + [rows(d)] * 2 + [whole((d, 3 * d)), whole((1, d))],
         out_specs=[rows(d), whole((1, d))],
         out_shape=[shaped((t, d), F32), shaped((1, d), F32)],
         compiler_params=params(48),
         cost_estimate=pl.CostEstimate(flops=6 * t * d * d, transcendentals=0, bytes_accessed=6 * d * d + 16 * t * d),
         name="qkv_backward",
-    )(dq, dk, dv, tokens, dx1, w_qkv, gain)
+    )(*pieces, tokens, dx1, w_qkv, gain)
 
 
 def layout(doc_lengths, seq):
@@ -790,31 +820,74 @@
     return lax.optimization_barrier((value, other))[0]
 
 
-def gather_z(block):
-    return [block] + [over_z(block, s) for s in (1, 2, 3)]
-
-
-def gather_xy(by_z):
-    even = jnp.stack([by_z[s] for s in GROUPS[0]])
-    odd = jnp.stack([by_z[s] for s in GROUPS[1]])
-    even = jnp.concatenate([even, over_x(even)])
-    odd = jnp.concatenate([odd, over_y(odd)])
-    return [even, over_y(even), odd, over_x(odd)]
-
-
-def gather_core(parts):
-    return parts + [over_core(p) for p in parts]
-
-
-def reduce_blocks(keep, send):
-    total = keep + over_core(send).astype(F32)
-    a, b = total[:8], total[8:]
-    a = a[4:] + over_y(a[:4].astype(BF)).astype(F32)
-    b = b[4:] + over_x(b[:4].astype(BF)).astype(F32)
-    a = a[2:] + over_x(a[:2].astype(BF)).astype(F32)
-    b = b[2:] + over_y(b[:2].astype(BF)).astype(F32)
-    r1, r2, r3 = over_z(b[0].astype(BF), 1), over_z(a[1].astype(BF), 2), over_z(b[1].astype(BF), 3)
-    return a[0] + r1.astype(F32) + r2.astype(F32) + r3.astype(F32)
+class Gather:
+    def __init__(self, block):
+        self.by_z = [block]
+
+    def z(self, after=None):
+        block = self.by_z[0] if after is None else tie(self.by_z[0], after)
+        self.by_z = [block] + [over_z(block, s) for s in (1, 2, 3)]
+        return self.by_z[1:]
+
+    def first(self, after=None):
+        even = jnp.stack([self.by_z[s] for s in GROUPS[0]])
+        odd = jnp.stack([self.by_z[s] for s in GROUPS[1]])
+        if after is not None:
+            even, odd = tie((even, odd), after)
+        self.even = jnp.concatenate([even, over_x(even)])
+        self.odd = jnp.concatenate([odd, over_y(odd)])
+        return [self.even, self.odd]
+
+    def second(self, after=None):
+        even, odd = (self.even, self.odd) if after is None else tie((self.even, self.odd), after)
+        self.near = [even, odd, over_core(even), over_core(odd)]
+        self.far = [over_y(even), over_x(odd)]
+        return self.far
+
+    def core(self, after=None):
+        far = self.far if after is None else tie(self.far, after)
+        even, odd, even_core, odd_core = self.near
+        return [even, far[0], odd, far[1], even_core, over_core(far[0]), odd_core, over_core(far[1])]
+
+
+class Reduce:
+    def __init__(self, keep, send):
+        self.keep, self.send = keep, send
+
+    def core(self, after=None):
+        send = self.send if after is None else tie(self.send, after)
+        self.got = self.core_got = over_core(send)
+        return self.got
+
+    def first(self, after=None):
+        total = self.keep + self.got.astype(F32)
+        self.a, self.b = total[:8], total[8:]
+        sends = (self.a[:4].astype(BF), self.b[:4].astype(BF))
+        if after is not None:
+            sends = tie(sends, after)
+        self.got = (over_y(sends[0]), over_x(sends[1]))
+        return self.got
+
+    def second(self, after=None):
+        self.a = self.a[4:] + self.got[0].astype(F32)
+        self.b = self.b[4:] + self.got[1].astype(F32)
+        sends = (self.a[:2].astype(BF), self.b[:2].astype(BF))
+        if after is not None:
+            sends = tie(sends, after)
+        self.got = (over_x(sends[0]), over_y(sends[1]))
+        return self.got
+
+    def z(self, after=None):
+        self.a = self.a[2:] + self.got[0].astype(F32)
+        self.b = self.b[2:] + self.got[1].astype(F32)
+        sends = (self.b[0].astype(BF), self.a[1].astype(BF), self.b[1].astype(BF))
+        if after is not None:
+            sends = tie(sends, after)
+        self.got = [over_z(s, i + 1) for i, s in enumerate(sends)]
+        return self.got
+
+    def own(self):
+        return self.a[0] + sum(g.astype(F32) for g in self.got)
 
 
 def unslab(block, width):
@@ -830,30 +903,11 @@
           gain_attn, gain_inner, gain_ffn, gain_mid):
     row_count = doc_lengths.shape[0]
     seq = tokens.shape[0] // row_count
+    d = tokens.shape[1]
     wide = min(seq, 512) // BLOCK + 1
     blocks = seq // BLOCK
     shards = (gain_attn, gain_inner, gain_ffn, gain_mid)
     sizes = [g.shape[0] for g in shards]
-    if fast:
-        order, back = gather_order(), scatter_order()
-        gains_row = jnp.pad(jnp.concatenate(shards)[None], ((0, 7), (0, LANES - sum(sizes))))
-        first = gather_z(jnp.concatenate(slab(w_qkv) + [gains_row]))
-        mine = tie(jnp.concatenate([w_out] + slab(w_up)), first[1:])
-        second = gather_z(mine)
-        third = gather_z(tie(w_down, second[1:]))
-        parts_qkv = gather_xy(first)
-        parts_up = gather_xy([tie(second[0], parts_qkv)] + second[1:])
-        parts_down = gather_xy([tie(third[0], parts_up)] + third[1:])
-        parts_qkv, parts_up, parts_down = (gather_core(p) for p in (parts_qkv, parts_up, parts_down))
-        gains = None
-    else:
-        order = back = jnp.zeros((8,), jnp.int32)
-
-        def gather(v):
-            return lax.all_gather(v, AXES, axis=0, tiled=True)
-
-        parts_qkv, parts_up, parts_down = [gather(w_qkv)], [gather(w_out), gather(w_up)], [gather(w_down)]
-        gains = [gather(g).astype(F32).reshape(1, -1) for g in shards]
 
     start, position, valid = layout(doc_lengths, seq)
     cos, sin = tables(position)
@@ -863,48 +917,138 @@
     start_row = jnp.repeat(start, 8, axis=0)
     valid_col = valid.astype(jnp.int32).reshape(-1, 1)
 
-    h1, qkv, full_qkv, *rest = qkv_forward(
-        fast, order, tokens, cos, sin, parts_qkv, None if fast else gains[0], sizes
-    )
+    if fast:
+        order, back = gather_order(), scatter_order()
+        gains_row = jnp.pad(jnp.concatenate(shards)[None], ((0, 7), (0, LANES - sum(sizes))))
+        one = Gather(jnp.concatenate(slab(w_qkv) + [gains_row]))
+        two = Gather(jnp.concatenate([w_out] + slab(w_up)))
+        three = Gather(w_down)
+        seen = one.z()
+        seen = two.z(seen)
+        one.first()
+        far = one.second()
+        three.z((seen, far))
+        two.first(far)
+        parts_qkv = one.core()
+        gains = [None]
+    else:
+        order = back = jnp.zeros((8,), jnp.int32)
+
+        def gather(v):
+            return lax.all_gather(v, AXES, axis=0, tiled=True)
+
+        parts_qkv, parts_up, parts_down = [gather(w_qkv)], [gather(w_out), gather(w_up)], [gather(w_down)]
+        gains = [gather(g).astype(F32).reshape(1, -1) for g in shards]
+
+    h1, qkv, full_qkv, *rest = qkv_forward(fast, order, tokens, cos, sin, parts_qkv, gains[0], sizes)
     g_attn, g_inner, g_ffn, g_mid = rest if fast else gains
+    if fast:
+        two.second(g_attn)
+        three.first(g_attn)
     mixed, lse = attention_forward(reach, qkv, start_col, row_count, wide)
+    if fast:
+        parts_up = two.core(lse)
+        three.second(lse)
     a, x1, h2, m, slope, inv, full_out, full_up = up_forward(
         fast, order, mixed, tokens, g_inner, g_ffn, g_mid, parts_up
     )
+    if fast:
+        parts_down = three.core(inv)
     result, dpre, grad_mid, *grad_down = down_both(
         fast, order, back, m, slope, inv, x1, cotangent, valid_col, g_mid, parts_down
     )
-    dx1, d_mixed, grad_ffn, grad_inner, *grad_up = up_backward(
-        fast, order, back, dpre, h2, x1, cotangent, valid_col, a, mixed, full_up, full_out, g_ffn, g_inner
-    )
-    dq, dk, dv = attention_backward(reach, qkv, d_mixed, mixed, lse, start_row, cos, sin, row_count, wide)
-    grad_qkv = qkv_weight_grad(fast, order, back, h1, dq, dk, dv)
-    grad_tokens, grad_attn = qkv_backward(dq, dk, dv, tokens, dx1, full_qkv, g_attn)
+    if fast:
+        red_down = Reduce(*grad_down)
+        red_down.core()
+    dx1, low, d_mixed, grad_ffn, grad_inner = up_backward(
+        dpre, x1, cotangent, valid_col, mixed, full_up, full_out, g_ffn, g_inner
+    )
+    if fast:
+        first = red_down.first(grad_ffn)
+        low = tie(low, (grad_ffn, red_down.core_got))
+    grad_up = up_weight_grad(fast, back, h2, dpre, a, low)
+    if fast:
+        second = red_down.second(grad_up)
+        red_up = Reduce(*grad_up)
+        red_up.core()
+        lse = tie(lse, first)
+
+    def attend(base, pairs, lse):
+        return attention_backward(
+            reach, qkv, d_mixed, mixed, lse, start_row, cos, sin, row_count, wide, base, pairs
+        )
+
+    third = PAIRS // 3
+    lse = tie(lse, grad_up[-1])
+    g0 = attend(0, third, lse)
+    if fast:
+        down_z = red_down.z(g0)
+        first = red_up.first(g0)
+        lse = tie(lse, (second, red_up.core_got))
+    g1 = attend(third, third, tie(lse, g0))
+    if fast:
+        second = red_up.second(g1)
+        h1 = tie(h1, first)
+    grad_qkv = [qkv_weight_grad(fast, back, h1, [p for pair in zip(g0, g1) for p in pair])]
+    if fast:
+        red_most = Reduce(*grad_qkv[0])
+        red_most.core()
+        own_down = red_down.own()
+        lse = tie(lse, down_z)
+    g2 = attend(2 * third, third, tie(lse, grad_qkv[0][-1]))
+    if fast:
+        up_z = red_up.z(g2)
+        first = red_most.first(g2)
+        h1 = tie(h1, (second, red_most.core_got))
+    grad_qkv.append(qkv_weight_grad(fast, back, h1, list(g2)))
+    if fast:
+        red_last = Reduce(*grad_qkv[1])
+        red_last.core()
+        second = red_most.second(grad_qkv[1])
+        dx1 = tie(dx1, first)
+    pieces, starts = [], []
+    for g, group in enumerate((g0, g1, g2)):
+        for part, piece in enumerate(group):
+            pieces.append(piece if g or not fast else tie(piece, grad_qkv[1][-1]))
+            starts.append(part * d + g * third * PAIR)
+    grad_tokens, grad_attn = qkv_backward(pieces, starts, tokens, dx1, full_qkv, g_attn)
     gain_grads = (grad_attn, grad_inner, grad_ffn, grad_mid)
-    if fast:
-        own_down = reduce_blocks(*grad_down)
-        own_up = reduce_blocks(*grad_up)
-        own_qkv = reduce_blocks(*grad_qkv)
-        cut = w_out.shape[0]
-        weights = (unslab(own_qkv, w_qkv.shape[1]), own_up[:cut], unslab(own_up[cut:], w_up.shape[1]), own_down)
+    cut = 2 * third * PAIR
+    if fast:
+        red_last.first(grad_attn)
+        red_most.z(grad_attn)
+        red_last.second()
+        own_up = red_up.own()
+        red_last.z()
         packed = jnp.concatenate([g.reshape(-1, LANES) for g in gain_grads])
         packed = jnp.pad(packed, ((0, -packed.shape[0] % 8), (0, 0)))
-        for move in (over_core, over_x, over_y, lambda v: across_z(v, 1), lambda v: across_z(v, 2)):
-            packed = packed + move(packed)
+        packed = packed + over_core(packed)
+        packed = packed + over_x(packed)
+        packed = packed + over_y(packed)
+        packed = packed + over_z(packed, 1) + over_z(packed, 2) + over_z(packed, 3)
+        most, last = unslab(red_most.own(), 3 * cut), unslab(red_last.own(), 3 * (d - cut))
+        size = w_out.shape[0]
+        weights = (own_up[:size], unslab(own_up[size:], w_up.shape[1]), own_down)
         me = index(*place())
         summed, at = [], 0
         for size, full in zip(sizes, gain_grads):
             flat = packed[at : at + full.size // LANES].reshape(-1)
             summed.append(lax.dynamic_slice(flat, (me * size,), (size,)))
             at += full.size // LANES
-        return (result, grad_tokens) + weights + tuple(summed)
-
-    def scatter(g):
-        return lax.psum_scatter(g, AXES, scatter_dimension=0, tiled=True)
-
-    order_of = (grad_qkv[0], grad_up[0], grad_up[1], grad_down[0])
-    weights = tuple(scatter(g.astype(BF)).astype(F32) for g in order_of)
-    return (result, grad_tokens) + weights + tuple(scatter(g.reshape(-1)) for g in gain_grads)
+    else:
+
+        def scatter(g):
+            return lax.psum_scatter(g, AXES, scatter_dimension=0, tiled=True)
+
+        most, last, *weights = (
+            scatter(g.astype(BF)).astype(F32)
+            for g in (grad_qkv[0][0], grad_qkv[1][0], grad_up[0], grad_up[1], grad_down[0])
+        )
+        summed = [scatter(g.reshape(-1)) for g in gain_grads]
+    columns = []
+    for part in range(3):
+        columns += [most[:, part * cut : (part + 1) * cut], last[:, part * (d - cut) : (part + 1) * (d - cut)]]
+    return (result, grad_tokens, jnp.concatenate(columns, axis=1)) + tuple(weights) + tuple(summed)
 
 
 def solution(mesh):

time: 418 us -> 413 us (0.988)
  waiting for transfers between devices: 113 us -> 83.4 us
  Pallas kernels: 176 us -> 185 us
  local copies, waits for them, and re-layouts: 31.9 us -> 40.2 us
  starting transfers between devices: 63.4 us -> 71 us
    pallas_call x3 -> x1, Pallas kernels: 77.7 us -> 33.8 us  [prefetched2(): pl.pallas_call(kernel, grid_spec=pltpu.PrefetchScalarGridSpec(num_scalar_...]
    pallas_call x2 -> x5, Pallas kernels: 33 us -> 68.2 us  [prefetched(): pl.pallas_call(kernel, grid_spec=pltpu.PrefetchScalarGridSpec(num_scalar_...]
    ppermute x62 -> x71, waiting for transfers between devices: 113 us -> 83.4 us  [permute(): lax.ppermute(value, AXES, [(index(*p), index(*move(*p))) for p in places])]
    pallas_call x1 -> x2, Pallas kernels: 9.26 us -> 24.2 us  [the longest x1 15.2 us: up_backward(): pl.pallas_call(up_back_kernel, grid=(t // BLOCK,), in_specs=[rows(f), row...]
    unnamed x96 -> x150, local copies, waits for them, and re-layouts: 21.1 us -> 31.5 us
    ppermute x62 -> x71, starting transfers between devices: 63.4 us -> 71 us  [permute(): lax.ppermute(value, AXES, [(index(*p), index(*move(*p))) for p in places])]
    pallas_call x1 -> x3, Pallas kernels: 34.5 us -> 36.9 us  [attention_backward(): pl.pallas_call(functools.partial(attention_backward_kernel, wide), grid_s...]
    another operation x13 -> x15, other arithmetic: 9.26 us -> 10.9 us
  transfers between devices with their start and end apart: 62 -> 71, of which waited for: 26 -> 24; matrix products, arithmetic and copies ran while one was open for 9% -> 8% of each run, Pallas kernels for 16% -> 30%
where the time goes in v3:
time: 413 us; the launch traced here: 406 us
  Pallas kernels  185 us (45%)
  waiting for transfers between devices  83.4 us (20%)
  starting transfers between devices  71 us (17%)
  local copies, waits for them, and re-layouts  40.2 us (10%)
  other arithmetic  24 us (6%)
    ppermute x71, waiting for transfers between devices, permute(): lax.ppermute(value, AXES, [(index(*p), index(*move(*p))) for p in places])  83.4 us
    ppermute x71, starting transfers between devices, permute(): lax.ppermute(value, AXES, [(index(*p), index(*move(*p))) for p in places])  71 us
    pallas_call x5, Pallas kernels, prefetched(): pl.pallas_call(kernel, grid_spec=pltpu.PrefetchScalarGridSpec(num_scalar_...  68.2 us
    pallas_call x3, Pallas kernels, attention_backward(): pl.pallas_call(functools.partial(attention_backward_kernel, wide), grid_s...  36.9 us
    pallas_call x1, Pallas kernels, prefetched2(): pl.pallas_call(kernel, grid_spec=pltpu.PrefetchScalarGridSpec(num_scalar_...  33.8 us
    unnamed x150, local copies, waits for them, and re-layouts  31.5 us
    pallas_call x1, Pallas kernels, attention_forward(): pl.pallas_call(functools.partial(attention_forward_kernel, wide), grid_sp...  21.5 us
    pallas_call x1, Pallas kernels, up_backward(): pl.pallas_call(up_back_kernel, grid=(t // BLOCK,), in_specs=[rows(f), row...  15.2 us
  transfers between devices with their start and end apart: 71, of which 24 were waited for; matrix products, arithmetic and copies ran while one was open for 8% of the time, Pallas kernels for 30%

profile of v3, /device:TPU:0, one launch (start us, length us, event | category | flops | bytes accessed | tf_op | source)
XLA Modules:
  0.0 405.8 jit_solution(16237922305447079687)
XLA Ops:
  14.4 4.2 %collective-permute-done = bf16[80,768]{1,0:T(8,128)(2,1)S(1)} collective-permute-done((bf16[80,768]{1,0:T(8,128)(2,1)S(1)}, bf16[80,768]{1,0:T(8,128)(2,1)S(1)}, u32[]{:S(2)}, u32[]{:S(2)}) %collective-permute-start) | collective-permute-done | bytes 122912 | tf_op jit(solution)/shard_map/ppermute | solution.py:765
  21.8 5.8 %collective-permute-done.1 = bf16[2,80,768]{2,1,0:T(8,128)(2,1)S(1)} collective-permute-done((bf16[2,80,768]{2,1,0:T(8,128)(2,1)S(1)}, bf16[2,80,768]{2,1,0:T(8,128)(2,1)S(1)}, u32[]{:S(2)}, u32[]{:S(2)}) %collective-permute-start.1) | collective-permute-done | bytes 245792 | tf_op jit(solution)/shard_map/ppermute | solution.py:765
  29.2 3.8 collective-permute-start.13
  33.1 5.6 %collective-permute-done.12 = bf16[120,768]{1,0:T(8,128)(2,1)S(1)} collective-permute-done((bf16[120,768]{1,0:T(8,128)(2,1)S(1)}, bf16[120,768]{1,0:T(8,128)(2,1)S(1)}, u32[]{:S(2)}, u32[]{:S(2)}) %collective-permute-start.12) | collective-permute-done | bytes 184352 | tf_op jit(solution)/shard_map/ppermute | solution.py:765
  38.7 6.6 %collective-permute-done.11 = bf16[120,768]{1,0:T(8,128)(2,1)S(1)} collective-permute-done((bf16[120,768]{1,0:T(8,128)(2,1)S(1)}, bf16[120,768]{1,0:T(8,128)(2,1)S(1)}, u32[]{:S(2)}, u32[]{:S(2)}) %collective-permute-start.11) | collective-permute-done | bytes 184352 | tf_op jit(solution)/shard_map/ppermute | solution.py:765
  48.2 6.2 %collective-permute-done.15 = bf16[2,120,768]{2,1,0:T(8,128)(2,1)S(1)} collective-permute-done((bf16[2,120,768]{2,1,0:T(8,128)(2,1)S(1)}, bf16[2,120,768]{2,1,0:T(8,128)(2,1)S(1)}, u32[]{:S(2)}, u32[]{:S(2)}) %collective-permute-start.15) | collective-permute-done | bytes 368672 | tf_op jit(solution)/shard_map/ppermute | solution.py:765
  58.4 10.3 %qkv_forward.1 = (bf16[1024,768]{1,0:T(8,128)(2,1)S(1)}, bf16[1024,2304]{1,0:T(8,128)(2,1)}, bf16[768,2304]{1,0:T(8,128)(2,1)S(1)}, f32[1,768]{1,0:T(1,128)S(1)}...) custom-call(s32[32]{0:T(128)S(1)} %stack.268.refs_0_, bf16[1024,768]{1,0:T(8,128)(2,1)S(1)} %copy-done.16, ...), custom_call_target="tpu_custom_call" | custom-call | flops 3623878656 | bytes 16515072 | tf_op jit(solution)/shard_map/qkv_forward/pallas_call | solution.py:181
  75.8 4.0 collective-permute-start.24
  80.1 4.3 %collective-permute-done.23 = bf16[96,768]{1,0:T(8,128)(2,1)S(1)} collective-permute-done((bf16[96,768]{1,0:T(8,128)(2,1)S(1)}, bf16[96,768]{1,0:T(8,128)(2,1)S(1)}, u32[]{:S(2)}, u32[]{:S(2)}) %collective-permute-start.23) | collective-permute-done | bytes 147488 | tf_op jit(solution)/shard_map/ppermute | solution.py:765
  84.5 6.9 %collective-permute-done.22 = bf16[96,768]{1,0:T(8,128)(2,1)S(1)} collective-permute-done((bf16[96,768]{1,0:T(8,128)(2,1)S(1)}, bf16[96,768]{1,0:T(8,128)(2,1)S(1)}, u32[]{:S(2)}, u32[]{:S(2)}) %collective-permute-start.22) | collective-permute-done | bytes 147488 | tf_op jit(solution)/shard_map/ppermute | solution.py:765
  95.8 21.5 %attention_forward.1 = (f32[1024,768]{1,0:T(8,128)S(1)}, f32[6,8,1024]{2,1,0:T(8,128)S(1)}) custom-call(s32[4]{0:T(128)S(1)} %add_bitcast_fusion.reach, bf16[1024,2304]{1,0:T(8,128)(2,1)S(1)} %copy-done, bf16[1024,2304]{1,0:T(8,128)(2,1)S(1)} %copy-done, bf16[1024,2304]{1,0:T(8,128)(2,1)S(1)} %copy-done, s32[1024,1]{1,0:T(8,128)S(1)} %copy.22.start_ref), custom_call_target="tpu_custom_call" | custom-call | flops 1610612736 | bytes 9437184 | tf_op jit(solution)/shard_map/attention_forward/pallas_call | solution.py:292
  120.1 8.4 %collective-permute-done.25 = bf16[2,96,768]{2,1,0:T(8,128)(2,1)S(1)} collective-permute-done((bf16[2,96,768]{2,1,0:T(8,128)(2,1)S(1)}, bf16[2,96,768]{2,1,0:T(8,128)(2,1)S(1)}, u32[]{:S(2)}, u32[]{:S(2)}) %collective-permute-start.25) | collective-permute-done | bytes 294944 | tf_op jit(solution)/shard_map/ppermute | solution.py:765
  131.2 22.2 %up_forward.1 = (bf16[1024,768]{1,0:T(8,128)(2,1)}, f32[1024,768]{1,0:T(8,128)}, bf16[1024,768]{1,0:T(8,128)(2,1)}, bf16[1024,3072]{1,0:T(8,128)(2,1)}, bf16[102...) custom-call(s32[32]{0:T(128)} %copy-done.13, ...), custom_call_target="tpu_custom_call" | custom-call | flops 6039797760 | bytes 35389440 | tf_op jit(solution)/shard_map/up_forward/pallas_call | solution.py:181
  157.5 33.8 %down_both.1 = (bf16[1024,768]{1,0:T(8,128)(2,1)}, bf16[1024,3072]{1,0:T(8,128)(2,1)}, f32[1,3072]{1,0:T(1,128)}, f32[16,96,768]{2,1,0:T(8,128)}, bf16[16,96,768]{2,1,0:T(8,128)(2,1)}) custom-call(s32[32]{0:T(128)} %copy-done.13, s32[32]{0:T(128)} %stack.293.refs_1_.refs_0_, bf16[1024,3072]{1,0:T(8,128)(2,1)} %get-tuple-element.118.refs_2_, ...), custom_call_target="tpu_custom_call" | custom-call | flops 14495514624 | bytes 39321600 | tf_op jit(solution)/shard_map/down_both/pallas_call | solution.py:543
  194.8 15.2 %up_backward.1 = (f32[1024,768]{1,0:T(8,128)S(1)}, bf16[1024,768]{1,0:T(8,128)(2,1)S(1)}, bf16[1024,768]{1,0:T(8,128)(2,1)S(1)}, f32[1,768]{1,0:T(1,128)S(1)}, f32[1,768]{1,0:T(1,128)S(1)}) custom-call(bf16[1024,3072]{1,0:T(8,128)(2,1)} %get-tuple-element.130.dpre_ref.refs_2_, f32[1024,768]{1,0:T(8,128)S(1)} %copy-done.37, bf16[1024,768]{1,0:T(8,128)(2,1)S(1)} %copy-done.15, ...), custom_call_target="tpu_custom_call" | custom-call | flops 6039797760 | bytes 31064064 | tf_op jit(solution)/shard_map/up_backward/pallas_call | solution.py:601
  215.4 18.5 %up_weight_grad.1 = (f32[16,120,768]{2,1,0:T(8,128)}, bf16[16,120,768]{2,1,0:T(8,128)(2,1)}) custom-call(s32[32]{0:T(128)} %stack.293.refs_1_.refs_0_, bf16[1024,768]{1,0:T(8,128)(2,1)} %get-tuple-element.140.refs_1_, bf16[1024,3072]{1,0:T(8,128)(2,1)} %get-tuple-element.130.dpre_ref.refs_2_, bf16[1024,768]{1,0:T(8,128)(2,1)} %get-tuple-element.141.refs_3_, ...), custom_call_target="tpu_custom_call" | custom-call | flops 6039797760 | bytes 28704768 | tf_op jit(solution)/shard_map/up_weight_grad/pallas_call | solution.py:181
  238.0 12.6 %collective-permute-done.34 = bf16[4,96,768]{2,1,0:T(8,128)(2,1)S(1)} collective-permute-done((bf16[4,96,768]{2,1,0:T(8,128)(2,1)S(1)}, bf16[4,96,768]{2,1,0:T(8,128)(2,1)S(1)}, u32[]{:S(2)}, u32[]{:S(2)}) %collective-permute-start.34) | collective-permute-done | bytes 589856 | tf_op jit(solution)/shard_map/ppermute | solution.py:765
  263.5 12.2 %attention_backward.3 = (bf16[1024,256]{1,0:T(8,128)(2,1)S(1)}, bf16[1024,256]{1,0:T(8,128)(2,1)S(1)}, bf16[1024,256]{1,0:T(8,128)(2,1)S(1)}) custom-call(s32[4]{0:T(128)S(1)} %add_bitcast_fusion.reach, bf16[1024,2304]{1,0:T(8,128)(2,1)S(1)} %copy-done.1, bf16[1024,2304]{1,0:T(8,128)(2,1)S(1)} %copy-done.1, bf16[1024,2304]{1,0:T(8,128)(2,1)S(1)} %copy-done.1, ...), custom_call_target="tpu_custom_call" | custom-call | flops 1342177280 | bytes 5242880 | tf_op jit(solution)/shard_map/attention_backward/pallas_call | solution.py:392
  277.2 7.3 %fusion.26 = (bf16[16,120,768]{2,1,0:T(8,128)(2,1)S(1)}, f32[16,120,768]{2,1,0:T(8,128)}) fusion(f32[16,120,768]{2,1,0:T(8,128)} %get-tuple-element.148, bf16[16,120,768]{2,1,0:T(8,128)(2,1)} %collective-permute-done.36), kind=kLoop, calls=%fused_computation.120 | loop fusion | flops 4423680 | bytes 17694720 | tf_op jit(solution)/shard_map/convert.25
  291.6 12.3 %attention_backward.4 = (bf16[1024,256]{1,0:T(8,128)(2,1)S(1)}, bf16[1024,256]{1,0:T(8,128)(2,1)S(1)}, bf16[1024,256]{1,0:T(8,128)(2,1)S(1)}) custom-call(s32[4]{0:T(128)S(1)} %add_bitcast_fusion.reach, bf16[1024,2304]{1,0:T(8,128)(2,1)S(1)} %bitcast.123, bf16[1024,2304]{1,0:T(8,128)(2,1)S(1)} %bitcast.123, bf16[1024,2304]{1,0:T(8,128)(2,1)S(1)} %bitcast.123, ...), custom_call_target="tpu_custom_call" | custom-call | flops 1342177280 | bytes 5242880 | tf_op jit(solution)/shard_map/attention_backward/pallas_call | solution.py:392
  304.1 11.2 %qkv_weight_grad.2 = (f32[16,48,768]{2,1,0:T(8,128)S(1)}, bf16[16,48,768]{2,1,0:T(8,128)(2,1)S(1)}) custom-call(s32[32]{0:T(128)S(1)} %copy-done.14, bf16[1024,768]{1,0:T(8,128)(2,1)S(1)} %copy-done.39, bf16[1024,256]{1,0:T(8,128)(2,1)S(1)} %get-tuple-element.174.refs_2_.refs_0_, bf16[1024,256]{1,0:T(8,128)(2,1)S(1)} %get-tuple-element.158.refs_3_, ...), custom_call_target="tpu_custom_call" | custom-call | flops 2415919104 | bytes 9437184 | tf_op jit(solution)/shard_map/qkv_weight_grad/pallas_call | solution.py:181
  321.3 12.4 %attention_backward.5 = (bf16[1024,256]{1,0:T(8,128)(2,1)S(1)}, bf16[1024,256]{1,0:T(8,128)(2,1)S(1)}, bf16[1024,256]{1,0:T(8,128)(2,1)S(1)}) custom-call(s32[4]{0:T(128)S(1)} %add_bitcast_fusion.reach, bf16[1024,2304]{1,0:T(8,128)(2,1)S(1)} %bitcast.123, bf16[1024,2304]{1,0:T(8,128)(2,1)S(1)} %bitcast.123, bf16[1024,2304]{1,0:T(8,128)(2,1)S(1)} %bitcast.123, ...), custom_call_target="tpu_custom_call" | custom-call | flops 1342177280 | bytes 5242880 | tf_op jit(solution)/shard_map/attention_backward/pallas_call | solution.py:392
  340.7 6.0 %qkv_weight_grad.3 = (f32[16,24,768]{2,1,0:T(8,128)S(1)}, bf16[16,24,768]{2,1,0:T(8,128)(2,1)S(1)}) custom-call(s32[32]{0:T(128)S(1)} %copy-done.14, bf16[1024,768]{1,0:T(8,128)(2,1)S(1)} %copy-done.39, bf16[1024,256]{1,0:T(8,128)(2,1)S(1)} %get-tuple-element.170.refs_2_.refs_6_, bf16[1024,256]{1,0:T(8,128)(2,1)S(1)} %get-tuple-element.171.refs_3_.refs_7_, ...), custom_call_target="tpu_custom_call" | custom-call | flops 1207959552 | bytes 5505024 | tf_op jit(solution)/shard_map/qkv_weight_grad/pallas_call | solution.py:181
  349.9 9.1 %qkv_backward.1 = (f32[1024,768]{1,0:T(8,128)}, f32[1,768]{1,0:T(1,128)S(1)}) custom-call(bf16[1024,256]{1,0:T(8,128)(2,1)S(1)} %copy-done.18, bf16[1024,256]{1,0:T(8,128)(2,1)S(1)} %copy-done.20, bf16[1024,256]{1,0:T(8,128)(2,1)S(1)} %copy-done.22, bf16[1024,256]{1,0:T(8,128)(2,1)S(1)} %copy-done.24, bf16[1024,256]{1,0:T(8,128)(2,1)S(1)} %copy-done.26, ...), custom_call_target="tpu_custom_call" | custom-call | flops 3623878656 | bytes 16121856 | tf_op jit(solution)/shard_map/qkv_backward/pallas_call | solution.py:723
  (373 shorter events, 143.0 us)
Async XLA Ops:
  20.3 25.0 %collective-permute-start.6 = (bf16[4,80,768]{2,1,0:T(8,128)(2,1)S(1)}, bf16[4,80,768]{2,1,0:T(8,128)(2,1)S(1)}, u32[]{:S(2)}, u32[]{:S(2)}) collective-permute-start(bf16[4,80,768]{2,1,0:T(8,128)(2,1)S(1)} %pad_maximum_fusion.5.refs_6_), channel_id=1, source_target_pairs={{0,16},{1,17},{2,18},{3,19},{4,20},{5,21},{6,22},{7,23},{8,24},{9,... | collective-permute-start | bytes 1474568 | tf_op jit(solution)/shard_map/ppermute | solution.py:765
  72.8 46.2 %collective-permute-start.16 = (bf16[4,120,768]{2,1,0:T(8,128)(2,1)}, bf16[4,120,768]{2,1,0:T(8,128)(2,1)}, u32[]{:S(2)}, u32[]{:S(2)}) collective-permute-start(bf16[4,120,768]{2,1,0:T(8,128)(2,1)} %pad_maximum_fusion.refs_6_), channel_id=1, source_target_pairs={{0,1},{1,0},{2,3},{3,2},{4,5},{5,4},{6,7},{7,6},{8,9},{9,8},{10,11... | collective-permute-start | bytes 2211848 | tf_op jit(solution)/shard_map/ppermute | solution.py:765
  74.2 44.8 %collective-permute-start.17 = (bf16[4,120,768]{2,1,0:T(8,128)(2,1)S(1)}, bf16[4,120,768]{2,1,0:T(8,128)(2,1)}, u32[]{:S(2)}, u32[]{:S(2)}) collective-permute-start(bf16[4,120,768]{2,1,0:T(8,128)(2,1)S(1)} %pad_maximum_fusion.1.refs_8_), channel_id=1, source_target_pairs={{0,16},{1,17},{2,18},{3,19},{4,20},{5,21},{6,22},{7,23},{8,24},{9,... | collective-permute-start | bytes 2211848 | tf_op jit(solution)/shard_map/ppermute | solution.py:765
  91.4 37.3 %collective-permute-start.18 = (bf16[4,120,768]{2,1,0:T(8,128)(2,1)}, bf16[4,120,768]{2,1,0:T(8,128)(2,1)S(1)}, u32[]{:S(2)}, u32[]{:S(2)}) collective-permute-start(bf16[4,120,768]{2,1,0:T(8,128)(2,1)} %pad_maximum_fusion.refs_6_), channel_id=1, source_target_pairs={{0,8},{1,9},{2,10},{3,11},{4,12},{5,13},{6,14},{7,15},{8,0},{9,1},... | collective-permute-start | bytes 2211848 | tf_op jit(solution)/shard_map/ppermute | solution.py:765
  91.5 38.3 %collective-permute-start.20 = (bf16[4,120,768]{2,1,0:T(8,128)(2,1)S(1)}, bf16[4,120,768]{2,1,0:T(8,128)(2,1)S(1)}, u32[]{:S(2)}, u32[]{:S(2)}) collective-permute-start(bf16[4,120,768]{2,1,0:T(8,128)(2,1)S(1)} %pad_maximum_fusion.1.refs_8_), channel_id=1, source_target_pairs={{0,8},{1,9},{2,10},{3,11},{4,12},{5,13},{6,14},{7,15},{8,0},{9,1},... | collective-permute-start | bytes 2211848 | tf_op jit(solution)/shard_map/ppermute | solution.py:765
  91.9 27.6 %collective-permute-start.26 = (bf16[2,96,768]{2,1,0:T(8,128)(2,1)S(1)}, bf16[2,96,768]{2,1,0:T(8,128)(2,1)S(1)}, u32[]{:S(2)}, u32[]{:S(2)}) collective-permute-start(bf16[2,96,768]{2,1,0:T(8,128)(2,1)S(1)} %pad_maximum_fusion.9), channel_id=1, source_target_pairs={{0,1},{1,0},{2,3},{3,2},{4,5},{5,4},{6,7},{7,6},{8,9},{9,8},{10,11... | collective-permute-start | bytes 884744 | tf_op jit(solution)/shard_map/ppermute | solution.py:765
  128.6 24.9 %collective-permute-start.27 = (bf16[4,96,768]{2,1,0:T(8,128)(2,1)S(1)}, bf16[4,96,768]{2,1,0:T(8,128)(2,1)S(1)}, u32[]{:S(2)}, u32[]{:S(2)}) collective-permute-start(bf16[4,96,768]{2,1,0:T(8,128)(2,1)S(1)} %pad_maximum_fusion.2.refs_9_), channel_id=1, source_target_pairs={{0,1},{1,0},{2,3},{3,2},{4,5},{5,4},{6,7},{7,6},{8,9},{9,8},{10,11... | collective-permute-start | bytes 1769480 | tf_op jit(solution)/shard_map/ppermute | solution.py:765
  128.7 24.8 %collective-permute-start.28 = (bf16[4,96,768]{2,1,0:T(8,128)(2,1)S(1)}, bf16[4,96,768]{2,1,0:T(8,128)(2,1)}, u32[]{:S(2)}, u32[]{:S(2)}) collective-permute-start(bf16[4,96,768]{2,1,0:T(8,128)(2,1)S(1)} %pad_maximum_fusion.3.refs_11_), channel_id=1, source_target_pairs={{0,16},{1,17},{2,18},{3,19},{4,20},{5,21},{6,22},{7,23},{8,24},{9,... | collective-permute-start | bytes 1769480 | tf_op jit(solution)/shard_map/ppermute | solution.py:765
  129.7 26.9 %collective-permute-start.29 = (bf16[4,96,768]{2,1,0:T(8,128)(2,1)S(1)}, bf16[4,96,768]{2,1,0:T(8,128)(2,1)S(1)}, u32[]{:S(2)}, u32[]{:S(2)}) collective-permute-start(bf16[4,96,768]{2,1,0:T(8,128)(2,1)S(1)} %pad_maximum_fusion.2.refs_9_), channel_id=1, source_target_pairs={{0,8},{1,9},{2,10},{3,11},{4,12},{5,13},{6,14},{7,15},{8,0},{9,1},... | collective-permute-start | bytes 1769480 | tf_op jit(solution)/shard_map/ppermute | solution.py:765
  129.8 26.9 %collective-permute-start.31 = (bf16[4,96,768]{2,1,0:T(8,128)(2,1)S(1)}, bf16[4,96,768]{2,1,0:T(8,128)(2,1)}, u32[]{:S(2)}, u32[]{:S(2)}) collective-permute-start(bf16[4,96,768]{2,1,0:T(8,128)(2,1)S(1)} %pad_maximum_fusion.3.refs_11_), channel_id=1, source_target_pairs={{0,8},{1,9},{2,10},{3,11},{4,12},{5,13},{6,14},{7,15},{8,0},{9,1},... | collective-permute-start | bytes 1769480 | tf_op jit(solution)/shard_map/ppermute | solution.py:765
  191.3 22.6 %collective-permute-start.33 = (bf16[16,96,768]{2,1,0:T(8,128)(2,1)}, bf16[16,96,768]{2,1,0:T(8,128)(2,1)S(1)}, u32[]{:S(2)}, u32[]{:S(2)}) collective-permute-start(bf16[16,96,768]{2,1,0:T(8,128)(2,1)} %get-tuple-element.135), channel_id=1, source_target_pairs={{0,8},{1,9},{2,10},{3,11},{4,12},{5,13},{6,14},{7,15},{8,0},{9,1},... | collective-permute-start | bytes 7077896 | tf_op jit(solution)/shard_map/ppermute | solution.py:765
  233.9 43.3 %collective-permute-start.36 = (bf16[16,120,768]{2,1,0:T(8,128)(2,1)}, bf16[16,120,768]{2,1,0:T(8,128)(2,1)}, u32[]{:S(2)}, u32[]{:S(2)}) collective-permute-start(bf16[16,120,768]{2,1,0:T(8,128)(2,1)} %get-tuple-element.144), channel_id=1, source_target_pairs={{0,8},{1,9},{2,10},{3,11},{4,12},{5,13},{6,14},{7,15},{8,0},{9,1},... | collective-permute-start | bytes 8847368 | tf_op jit(solution)/shard_map/ppermute | solution.py:765
  254.6 21.1 %collective-permute-start.39 = (bf16[2,96,768]{2,1,0:T(8,128)(2,1)}, bf16[2,96,768]{2,1,0:T(8,128)(2,1)}, u32[]{:S(2)}, u32[]{:S(2)}) collective-permute-start(bf16[2,96,768]{2,1,0:T(8,128)(2,1)} %slice.495), channel_id=1, source_target_pairs={{0,16},{1,17},{2,18},{3,19},{4,20},{5,21},{6,22},{7,23},{8,24},{9,... | collective-permute-start | bytes 884744 | tf_op jit(solution)/shard_map/ppermute | solution.py:765
  257.2 29.8 %collective-permute-start.40 = (bf16[2,96,768]{2,1,0:T(8,128)(2,1)}, bf16[2,96,768]{2,1,0:T(8,128)(2,1)S(1)}, u32[]{:S(2)}, u32[]{:S(2)}) collective-permute-start(bf16[2,96,768]{2,1,0:T(8,128)(2,1)} %slice.494), channel_id=1, source_target_pairs={{0,1},{1,0},{2,3},{3,2},{4,5},{5,4},{6,7},{7,6},{8,9},{9,8},{10,11... | collective-permute-start | bytes 884744 | tf_op jit(solution)/shard_map/ppermute | solution.py:765
  284.7 19.4 %collective-permute-start.37 = (bf16[4,120,768]{2,1,0:T(8,128)(2,1)S(1)}, bf16[4,120,768]{2,1,0:T(8,128)(2,1)S(1)}, u32[]{:S(2)}, u32[]{:S(2)}) collective-permute-start(bf16[4,120,768]{2,1,0:T(8,128)(2,1)S(1)} %get-tuple-element.151), channel_id=1, source_target_pairs={{0,1},{1,0},{2,3},{3,2},{4,5},{5,4},{6,7},{7,6},{8,9},{9,8},{10,11... | collective-permute-start | bytes 2211848 | tf_op jit(solution)/shard_map/ppermute | solution.py:765
  285.1 18.9 %collective-permute-start.38 = (bf16[4,120,768]{2,1,0:T(8,128)(2,1)S(1)}, bf16[4,120,768]{2,1,0:T(8,128)(2,1)S(1)}, u32[]{:S(2)}, u32[]{:S(2)}) collective-permute-start(bf16[4,120,768]{2,1,0:T(8,128)(2,1)S(1)} %get-tuple-element.152), channel_id=1, source_target_pairs={{0,16},{1,17},{2,18},{3,19},{4,20},{5,21},{6,22},{7,23},{8,24},{9,... | collective-permute-start | bytes 2211848 | tf_op jit(solution)/shard_map/ppermute | solution.py:765
  287.8 29.9 %collective-permute-start.44 = (bf16[96,768]{1,0:T(8,128)(2,1)}, bf16[96,768]{1,0:T(8,128)(2,1)}, u32[]{:S(2)}, u32[]{:S(2)}) collective-permute-start(bf16[96,768]{1,0:T(8,128)(2,1)} %get-tuple-element.165), channel_id=1, source_target_pairs={{0,2},{1,3},{2,4},{3,5},{4,6},{5,7},{6,0},{7,1},{8,10},{9,11},{10,... | collective-permute-start | bytes 442376 | tf_op jit(solution)/shard_map/ppermute | solution.py:765
  287.8 29.9 %collective-permute-start.45 = (bf16[96,768]{1,0:T(8,128)(2,1)S(1)}, bf16[96,768]{1,0:T(8,128)(2,1)}, u32[]{:S(2)}, u32[]{:S(2)}) collective-permute-start(bf16[96,768]{1,0:T(8,128)(2,1)S(1)} %fusion.9), channel_id=1, source_target_pairs={{0,4},{1,5},{2,6},{3,7},{4,0},{5,1},{6,2},{7,3},{8,12},{9,13},{10,... | collective-permute-start | bytes 442376 | tf_op jit(solution)/shard_map/ppermute | solution.py:765
  289.1 28.7 %collective-permute-start.46 = (bf16[96,768]{1,0:T(8,128)(2,1)S(1)}, bf16[96,768]{1,0:T(8,128)(2,1)}, u32[]{:S(2)}, u32[]{:S(2)}) collective-permute-start(bf16[96,768]{1,0:T(8,128)(2,1)S(1)} %get-tuple-element.167), channel_id=1, source_target_pairs={{0,6},{1,7},{2,0},{3,1},{4,2},{5,3},{6,4},{7,5},{8,14},{9,15},{10,... | collective-permute-start | bytes 442376 | tf_op jit(solution)/shard_map/ppermute | solution.py:765
  315.3 18.6 %collective-permute-start.43 = (bf16[16,48,768]{2,1,0:T(8,128)(2,1)S(1)}, bf16[16,48,768]{2,1,0:T(8,128)(2,1)S(1)}, u32[]{:S(2)}, u32[]{:S(2)}) collective-permute-start(bf16[16,48,768]{2,1,0:T(8,128)(2,1)S(1)} %get-tuple-element.163), channel_id=1, source_target_pairs={{0,8},{1,9},{2,10},{3,11},{4,12},{5,13},{6,14},{7,15},{8,0},{9,1},... | collective-permute-start | bytes 3538952 | tf_op jit(solution)/shard_map/ppermute | solution.py:765
  336.8 22.3 %collective-permute-start.62 = (bf16[120,768]{1,0:T(8,128)(2,1)S(1)}, bf16[120,768]{1,0:T(8,128)(2,1)S(1)}, u32[]{:S(2)}, u32[]{:S(2)}) collective-permute-start(bf16[120,768]{1,0:T(8,128)(2,1)S(1)} %get-tuple-element.193), channel_id=1, source_target_pairs={{0,2},{1,3},{2,4},{3,5},{4,6},{5,7},{6,0},{7,1},{8,10},{9,11},{10,... | collective-permute-start | bytes 552968 | tf_op jit(solution)/shard_map/ppermute | solution.py:765
  336.8 22.2 %collective-permute-start.63 = (bf16[120,768]{1,0:T(8,128)(2,1)S(1)}, bf16[120,768]{1,0:T(8,128)(2,1)S(1)}, u32[]{:S(2)}, u32[]{:S(2)}) collective-permute-start(bf16[120,768]{1,0:T(8,128)(2,1)S(1)} %fusion.8), channel_id=1, source_target_pairs={{0,4},{1,5},{2,6},{3,7},{4,0},{5,1},{6,2},{7,3},{8,12},{9,13},{10,... | collective-permute-start | bytes 552968 | tf_op jit(solution)/shard_map/ppermute | solution.py:765
  338.0 21.1 %collective-permute-start.64 = (bf16[120,768]{1,0:T(8,128)(2,1)S(1)}, bf16[120,768]{1,0:T(8,128)(2,1)S(1)}, u32[]{:S(2)}, u32[]{:S(2)}) collective-permute-start(bf16[120,768]{1,0:T(8,128)(2,1)S(1)} %get-tuple-element.195), channel_id=1, source_target_pairs={{0,6},{1,7},{2,0},{3,1},{4,2},{5,3},{6,4},{7,5},{8,14},{9,15},{10,... | collective-permute-start | bytes 552968 | tf_op jit(solution)/shard_map/ppermute | solution.py:765
  365.3 18.0 %collective-permute-start.54 = (bf16[16,24,768]{2,1,0:T(8,128)(2,1)S(1)}, bf16[16,24,768]{2,1,0:T(8,128)(2,1)}, u32[]{:S(2)}, u32[]{:S(2)}) collective-permute-start(bf16[16,24,768]{2,1,0:T(8,128)(2,1)S(1)} %get-tuple-element.173), channel_id=1, source_target_pairs={{0,8},{1,9},{2,10},{3,11},{4,12},{5,13},{6,14},{7,15},{8,0},{9,1},... | collective-permute-start | bytes 1769480 | tf_op jit(solution)/shard_map/ppermute | solution.py:765
  (118 other events, 1165.1 us)

commit v4 on v3

--- a/solution.py
+++ b/solution.py
@@ -72,18 +72,19 @@
 
 
 def fetch(order, parts, places, sem):
-    if order is None:
+    if len(parts) < 8 and parts[0].ndim == 2:
         for part, (_, _, buffer, _) in zip(parts, places):
             pltpu.make_async_copy(part, buffer, sem).start()
         return
     count = parts[0].shape[0]
     for p, part in enumerate(parts):
         for b in range(count):
-            owner = order[p * count + b]
+            owner = b if order is None else order[p * count + b]
             for first, size, buffer, column in places:
+                row = owner * size if order is None else pl.multiple_of(owner * size, 8)
                 pltpu.make_async_copy(
                     part.at[b, pl.ds(first, size), :],
-                    buffer.at[pl.ds(pl.multiple_of(owner * size, 8), size), pl.ds(column, LANES)],
+                    buffer.at[pl.ds(row, size), pl.ds(column, LANES)],
                     sem,
                 ).start()
 
@@ -421,24 +422,24 @@
     )(reach, qkv, qkv, qkv, d_mixed, mixed, lse, start_row, cos, sin)
 
 
-def up_kernel(split, *refs):
-    order, o_ref, x_ref, gi_ref, gf_ref, gm_ref, *refs = refs
-    count = 8 if split else 2
+def up_kernel(split, o_ref, x_ref, ct_ref, valid_ref, gi_ref, gf_ref, gm_ref, *refs):
+    count = 1 if split else 2
     parts, refs = refs[:count], refs[count:]
-    a_ref, x1_ref, h2_ref, m_ref, slope_ref, inv_ref, wo_ref, wu_ref, sem = refs
+    a_ref, x1_ref, h2_ref, m_ref, slope_ref, inv_ref, wo_ref, wu_ref, grad_ref, total, sem = refs
     d, f = wu_ref.shape
     size = d // 32
+    step = pl.program_id(0)
     places = [(0, size, wo_ref, 0)] + slabs(size, size, wu_ref, f) if split else [(0, 0, wo_ref, 0), (0, 0, wu_ref, 0)]
 
-    @pl.when(pl.program_id(0) == 0)
-    def _():
-        fetch(order if split else None, parts, places, sem)
+    @pl.when(step == 0)
+    def _():
+        fetch(None, parts, places, sem)
 
     unit, _ = unit_norm(o_ref[...])
     a = (unit * gi_ref[...]).astype(BF)
     a_ref[...] = a
 
-    @pl.when(pl.program_id(0) == 0)
+    @pl.when(step == 0)
     def _():
         arrive([wo_ref, wu_ref], sem)
 
@@ -452,57 +453,61 @@
     slope = cdf + hidden * (jnp.exp(-0.5 * hidden * hidden) * INV_ROOT_TAU)
     slope_ref[...] = slope.astype(BF)
     unit, inv = unit_norm(hidden * cdf)
-    m_ref[...] = (unit * gm_ref[...]).astype(BF)
+    m = (unit * gm_ref[...]).astype(BF)
+    m_ref[...] = m
     inv_ref[...] = jnp.broadcast_to(inv, inv_ref.shape)
-
-
-def up_forward(split, order, mixed, tokens, gain_inner, gain_ffn, gain_mid, parts):
+    gy = jnp.where(valid_ref[...] > 0, ct_ref[...], jnp.zeros_like(ct_ref))
+    part = dot(m, gy, ((0,), (0,)))
+
+    @pl.when(step == 0)
+    def _():
+        total[...] = part
+
+    @pl.when(step > 0)
+    def _():
+        total[...] += part
+
+    @pl.when(step == pl.num_programs(0) - 1)
+    def _():
+        grad_ref[...] = total[...].astype(BF)
+
+
+def up_forward(split, mixed, tokens, cotangent, valid, gain_inner, gain_ffn, gain_mid, parts):
     t, d = tokens.shape
     f = gain_mid.shape[1]
-    return prefetched(
-        functools.partial(up_kernel, split), order,
-        [mixed, tokens, gain_inner, gain_ffn, gain_mid, *parts],
-        [rows(d), rows(d), whole((1, d)), whole((1, d)), whole((1, f))] + [hbm()] * len(parts),
-        [rows(d), rows(d), rows(d), rows(f), rows(f), rows(PAIR), whole((d, d)), whole((d, f))],
-        [
+    return pl.pallas_call(
+        functools.partial(up_kernel, split),
+        grid=(t // BLOCK,),
+        in_specs=[rows(d), rows(d), rows(d), rows(1), whole((1, d)), whole((1, d)), whole((1, f))] + [hbm()] * len(parts),
+        out_specs=[rows(d), rows(d), rows(d), rows(f), rows(f), rows(PAIR), whole((d, d)), whole((d, f)), whole((f, d))],
+        out_shape=[
             shaped((t, d), BF), shaped((t, d), F32), shaped((t, d), BF),
             shaped((t, f), BF), shaped((t, f), BF), shaped((t, PAIR), F32),
-            shaped((d, d), BF), shaped((d, f), BF),
+            shaped((d, d), BF), shaped((d, f), BF), shaped((f, d), BF),
         ],
-        [pltpu.SemaphoreType.DMA], (t // BLOCK,), 56, "up_forward",
-        2 * t * d * (d + f), 4 * d * (d + f) + 4 * t * f + 14 * t * d,
-    )
-
-
-def down_kernel(split, *refs):
-    order, back, m_ref, slope_ref, inv_ref, x1_ref, ct_ref, valid_ref, gm_ref, *refs = refs
-    count = 8 if split else 1
-    parts, refs = refs[:count], refs[count:]
-    y_ref, dpre_ref, gg_ref, *refs = refs
-    if split:
-        keep_ref, send_ref, wd_ref, total, sem = refs
-    else:
-        total, wd_ref, sem = refs
+        scratch_shapes=[pltpu.VMEM((f, d), F32), pltpu.SemaphoreType.DMA],
+        compiler_params=params(60),
+        cost_estimate=pl.CostEstimate(
+            flops=2 * t * d * (d + 2 * f), transcendentals=2 * t * f,
+            bytes_accessed=4 * d * (d + f) + 2 * d * f + 4 * t * f + 16 * t * d,
+        ),
+        name="up_forward",
+    )(mixed, tokens, cotangent, valid, gain_inner, gain_ffn, gain_mid, *parts)
+
+
+def down_kernel(split, m_ref, slope_ref, inv_ref, x1_ref, ct_ref, valid_ref, gm_ref, part_ref,
+                y_ref, dpre_ref, gg_ref, wd_ref, sem):
     f, d = wd_ref.shape
     step = pl.program_id(0)
 
     @pl.when(step == 0)
     def _():
-        fetch(order if split else None, parts, [(0, f // 32, wd_ref, 0)], sem)
+        first = part_ref.shape[1] - f // 32 if split else 0
+        fetch(None, [part_ref], [(first, f // 32, wd_ref, 0)], sem)
+        arrive([wd_ref], sem)
 
     m = m_ref[...]
     gy = jnp.where(valid_ref[...] > 0, ct_ref[...], jnp.zeros_like(ct_ref))
-    part = dot(m, gy, ((0,), (0,)))
-
-    @pl.when(step == 0)
-    def _():
-        total[...] = part
-        arrive([wd_ref], sem)
-
-    @pl.when(step > 0)
-    def _():
-        total[...] += part
-
     dm = dot(gy, wd_ref[...], ((1,), (1,)))
     gain = gm_ref[...]
     mf = m.astype(F32)
@@ -525,12 +530,6 @@
     def _():
         gg_ref[...] += gain_part
 
-    if split:
-
-        @pl.when(step == pl.num_programs(0) - 1)
-        def _():
-            deal(back, keep_ref, send_ref, [(0, f // 32, total, 0)])
-
 
 def dealt(split, size, shapes):
     if split:
@@ -539,33 +538,22 @@
     return [whole(s) for s in shapes], [shaped(s, F32) for s in shapes], []
 
 
-def prefetched2(kernel, order, back, inputs, in_specs, out_specs, out_shape, scratch, grid, mib, name, flops, data):
-    return pl.pallas_call(
-        kernel,
-        grid_spec=pltpu.PrefetchScalarGridSpec(
-            num_scalar_prefetch=2, grid=grid, in_specs=in_specs, out_specs=out_specs, scratch_shapes=scratch,
-        ),
-        out_shape=out_shape,
-        compiler_params=params(mib),
-        cost_estimate=pl.CostEstimate(flops=flops, transcendentals=0, bytes_accessed=data),
-        name=name,
-    )(order, back, *inputs)
-
-
-def down_both(split, order, back, m, slope, inv, x1, cotangent, valid, gain_mid, parts):
+def down_both(split, m, slope, inv, x1, cotangent, valid, gain_mid, part):
     t, d = x1.shape
     f = m.shape[1]
-    out_specs, out_shape, scratch = dealt(split, f // 32, [(f, d)])
-    weight = [pltpu.VMEM((f, d), BF)]
-    return prefetched2(
-        functools.partial(down_kernel, split), order, back,
-        [m, slope, inv, x1, cotangent, valid, gain_mid, *parts],
-        [rows(f), rows(f), rows(PAIR), rows(d), rows(d), rows(1), whole((1, f))] + [hbm()] * len(parts),
-        [rows(d), rows(f), whole((1, f))] + out_specs,
-        [shaped((t, d), BF), shaped((t, f), BF), shaped((1, f), F32)] + out_shape,
-        weight + scratch + [pltpu.SemaphoreType.DMA], (t // BLOCK,), 60, "down_both",
-        6 * t * d * f, 6 * d * f + 6 * t * f + 8 * t * d,
-    )
+    return pl.pallas_call(
+        functools.partial(down_kernel, split),
+        grid=(t // BLOCK,),
+        in_specs=[rows(f), rows(f), rows(PAIR), rows(d), rows(d), rows(1), whole((1, f)), hbm()],
+        out_specs=[rows(d), rows(f), whole((1, f))],
+        out_shape=[shaped((t, d), BF), shaped((t, f), BF), shaped((1, f), F32)],
+        scratch_shapes=[pltpu.VMEM((f, d), BF), pltpu.SemaphoreType.DMA],
+        compiler_params=params(48),
+        cost_estimate=pl.CostEstimate(
+            flops=4 * t * d * f, transcendentals=0, bytes_accessed=2 * d * f + 6 * t * f + 8 * t * d
+        ),
+        name="down_both",
+    )(m, slope, inv, x1, cotangent, valid, gain_mid, part)
 
 
 def up_back_kernel(dpre_ref, x1_ref, ct_ref, valid_ref, o_ref, wu_ref, wo_ref, gf_ref, gi_ref,
@@ -917,61 +905,44 @@
     start_row = jnp.repeat(start, 8, axis=0)
     valid_col = valid.astype(jnp.int32).reshape(-1, 1)
 
+    def scatter(g):
+        return lax.psum_scatter(g, AXES, scatter_dimension=0, tiled=True)
+
+    def gather(v):
+        return lax.all_gather(v, AXES, axis=0, tiled=True)
+
     if fast:
         order, back = gather_order(), scatter_order()
         gains_row = jnp.pad(jnp.concatenate(shards)[None], ((0, 7), (0, LANES - sum(sizes))))
+        rest_of = jnp.concatenate([w_out] + slab(w_up) + [w_down])
+        parts_up = [gather(rest_of).reshape(-1, *rest_of.shape)]
+        part_down = parts_up[0]
         one = Gather(jnp.concatenate(slab(w_qkv) + [gains_row]))
-        two = Gather(jnp.concatenate([w_out] + slab(w_up)))
-        three = Gather(w_down)
-        seen = one.z()
-        seen = two.z(seen)
+        one.z()
         one.first()
-        far = one.second()
-        three.z((seen, far))
-        two.first(far)
+        one.second()
         parts_qkv = one.core()
         gains = [None]
     else:
         order = back = jnp.zeros((8,), jnp.int32)
-
-        def gather(v):
-            return lax.all_gather(v, AXES, axis=0, tiled=True)
-
-        parts_qkv, parts_up, parts_down = [gather(w_qkv)], [gather(w_out), gather(w_up)], [gather(w_down)]
+        parts_qkv, parts_up, part_down = [gather(w_qkv)], [gather(w_out), gather(w_up)], gather(w_down)
         gains = [gather(g).astype(F32).reshape(1, -1) for g in shards]
 
     h1, qkv, full_qkv, *rest = qkv_forward(fast, order, tokens, cos, sin, parts_qkv, gains[0], sizes)
     g_attn, g_inner, g_ffn, g_mid = rest if fast else gains
-    if fast:
-        two.second(g_attn)
-        three.first(g_attn)
     mixed, lse = attention_forward(reach, qkv, start_col, row_count, wide)
-    if fast:
-        parts_up = two.core(lse)
-        three.second(lse)
-    a, x1, h2, m, slope, inv, full_out, full_up = up_forward(
-        fast, order, mixed, tokens, g_inner, g_ffn, g_mid, parts_up
+    a, x1, h2, m, slope, inv, full_out, full_up, grad_down = up_forward(
+        fast, mixed, tokens, cotangent, valid_col, g_inner, g_ffn, g_mid, parts_up
     )
-    if fast:
-        parts_down = three.core(inv)
-    result, dpre, grad_mid, *grad_down = down_both(
-        fast, order, back, m, slope, inv, x1, cotangent, valid_col, g_mid, parts_down
-    )
-    if fast:
-        red_down = Reduce(*grad_down)
-        red_down.core()
+    own_down = scatter(grad_down).astype(F32)
+    result, dpre, grad_mid = down_both(fast, m, slope, inv, x1, cotangent, valid_col, g_mid, part_down)
     dx1, low, d_mixed, grad_ffn, grad_inner = up_backward(
         dpre, x1, cotangent, valid_col, mixed, full_up, full_out, g_ffn, g_inner
     )
-    if fast:
-        first = red_down.first(grad_ffn)
-        low = tie(low, (grad_ffn, red_down.core_got))
     grad_up = up_weight_grad(fast, back, h2, dpre, a, low)
     if fast:
-        second = red_down.second(grad_up)
         red_up = Reduce(*grad_up)
         red_up.core()
-        lse = tie(lse, first)
 
     def attend(base, pairs, lse):
         return attention_backward(
@@ -982,53 +953,41 @@
     lse = tie(lse, grad_up[-1])
     g0 = attend(0, third, lse)
     if fast:
-        down_z = red_down.z(g0)
         first = red_up.first(g0)
-        lse = tie(lse, (second, red_up.core_got))
+        lse = tie(lse, red_up.core_got)
     g1 = attend(third, third, tie(lse, g0))
     if fast:
         second = red_up.second(g1)
-        h1 = tie(h1, first)
-    grad_qkv = [qkv_weight_grad(fast, back, h1, [p for pair in zip(g0, g1) for p in pair])]
-    if fast:
-        red_most = Reduce(*grad_qkv[0])
-        red_most.core()
-        own_down = red_down.own()
-        lse = tie(lse, down_z)
-    g2 = attend(2 * third, third, tie(lse, grad_qkv[0][-1]))
+        lse = tie(lse, first)
+    g2 = attend(2 * third, third, tie(lse, g1))
     if fast:
         up_z = red_up.z(g2)
-        first = red_most.first(g2)
-        h1 = tie(h1, (second, red_most.core_got))
-    grad_qkv.append(qkv_weight_grad(fast, back, h1, list(g2)))
+        h1, own_down = tie((h1, own_down), second)
+    pieces, starts = [], []
+    for part in range(3):
+        for g, group in enumerate((g0, g1, g2)):
+            pieces.append(group[part])
+            starts.append(part * d + g * third * PAIR)
+    grad_qkv = qkv_weight_grad(fast, back, h1, pieces)
     if fast:
-        red_last = Reduce(*grad_qkv[1])
-        red_last.core()
-        second = red_most.second(grad_qkv[1])
-        dx1 = tie(dx1, first)
-    pieces, starts = [], []
-    for g, group in enumerate((g0, g1, g2)):
-        for part, piece in enumerate(group):
-            pieces.append(piece if g or not fast else tie(piece, grad_qkv[1][-1]))
-            starts.append(part * d + g * third * PAIR)
+        red_qkv = Reduce(*grad_qkv)
+        red_qkv.core()
+        dx1 = tie(dx1, (up_z, grad_qkv[-1]))
     grad_tokens, grad_attn = qkv_backward(pieces, starts, tokens, dx1, full_qkv, g_attn)
     gain_grads = (grad_attn, grad_inner, grad_ffn, grad_mid)
-    cut = 2 * third * PAIR
     if fast:
-        red_last.first(grad_attn)
-        red_most.z(grad_attn)
-        red_last.second()
         own_up = red_up.own()
-        red_last.z()
+        red_qkv.first()
+        second = red_qkv.second(grad_attn)
+        red_qkv.z()
         packed = jnp.concatenate([g.reshape(-1, LANES) for g in gain_grads])
         packed = jnp.pad(packed, ((0, -packed.shape[0] % 8), (0, 0)))
         packed = packed + over_core(packed)
         packed = packed + over_x(packed)
         packed = packed + over_y(packed)
         packed = packed + over_z(packed, 1) + over_z(packed, 2) + over_z(packed, 3)
-        most, last = unslab(red_most.own(), 3 * cut), unslab(red_last.own(), 3 * (d - cut))
         size = w_out.shape[0]
-        weights = (own_up[:size], unslab(own_up[size:], w_up.shape[1]), own_down)
+        weights = (unslab(red_qkv.own(), w_qkv.shape[1]), own_up[:size], unslab(own_up[size:], w_up.shape[1]))
         me = index(*place())
         summed, at = [], 0
         for size, full in zip(sizes, gain_grads):
@@ -1036,19 +995,9 @@
             summed.append(lax.dynamic_slice(flat, (me * size,), (size,)))
             at += full.size // LANES
     else:
-
-        def scatter(g):
-            return lax.psum_scatter(g, AXES, scatter_dimension=0, tiled=True)
-
-        most, last, *weights = (
-            scatter(g.astype(BF)).astype(F32)
-            for g in (grad_qkv[0][0], grad_qkv[1][0], grad_up[0], grad_up[1], grad_down[0])
-        )
+        weights = tuple(scatter(g.astype(BF)).astype(F32) for g in (grad_qkv[0], grad_up[0], grad_up[1]))
         summed = [scatter(g.reshape(-1)) for g in gain_grads]
-    columns = []
-    for part in range(3):
-        columns += [most[:, part * cut : (part + 1) * cut], last[:, part * (d - cut) : (part + 1) * (d - cut)]]
-    return (result, grad_tokens, jnp.concatenate(columns, axis=1)) + tuple(weights) + tuple(summed)
+    return (result, grad_tokens) + weights + (own_down,) + tuple(summed)
 
 
 def solution(mesh):

time: 413 us -> 407 us (0.985)
  starting transfers between devices: 71 us -> 37.1 us
  local copies, waits for them, and re-layouts: 40.2 us -> 59.5 us
  between operations: 2.52 us -> 15.2 us
  waiting for transfers between devices: 83.4 us -> 75.7 us
    ppermute x71 -> x33, starting transfers between devices: 71 us -> 37 us  [permute(): lax.ppermute(value, AXES, [(index(*p), index(*move(*p))) for p in places])]
    pallas_call x1 -> x2, Pallas kernels: 33.8 us -> 57.9 us  [the longest x1 35.8 us: up_forward(): pl.pallas_call(functools.partial(up_kernel, split), grid=(t // BLOCK,), i...]
    pallas_call x5 -> x3, Pallas kernels: 68.2 us -> 46.2 us  [prefetched(): pl.pallas_call(kernel, grid_spec=pltpu.PrefetchScalarGridSpec(num_scalar_...]
    unnamed x150 -> x135, local copies, waits for them, and re-layouts: 31.5 us -> 49.4 us
    ppermute x71 -> x33, waiting for transfers between devices: 83.4 us -> 68 us  [permute(): lax.ppermute(value, AXES, [(index(*p), index(*move(*p))) for p in places])]
    all_gather x0 -> x1, waiting for transfers between devices: none -> 7.66 us  [gather(): return lax.all_gather(v, AXES, axis=0, tiled=True)]
    another operation x8 -> x4, other arithmetic: 10.7 us -> 11.5 us
  transfers between devices with their start and end apart: 71 -> 35, of which waited for: 24 -> 18; matrix products, arithmetic and copies ran while one was open for 8% -> 8% of each run, Pallas kernels for 30% -> 34%
where the time goes in v4:
time: 407 us; the launch traced here: 402 us
  Pallas kernels  188 us (46%)
  waiting for transfers between devices  75.7 us (19%)
  local copies, waits for them, and re-layouts  59.5 us (15%)
  starting transfers between devices  37.1 us (9%)
  other arithmetic  26.3 us (6%)
  between operations  15.2 us (4%)
    ppermute x33, waiting for transfers between devices, permute(): lax.ppermute(value, AXES, [(index(*p), index(*move(*p))) for p in places])  68 us
    unnamed x135, local copies, waits for them, and re-layouts  49.4 us
    pallas_call x3, Pallas kernels, prefetched(): pl.pallas_call(kernel, grid_spec=pltpu.PrefetchScalarGridSpec(num_scalar_...  46.2 us
    ppermute x33, starting transfers between devices, permute(): lax.ppermute(value, AXES, [(index(*p), index(*move(*p))) for p in places])  37 us
    pallas_call x3, Pallas kernels, attention_backward(): pl.pallas_call(functools.partial(attention_backward_kernel, wide), grid_s...  37 us
    pallas_call x1, Pallas kernels, up_forward(): pl.pallas_call(functools.partial(up_kernel, split), grid=(t // BLOCK,), i...  35.8 us
    pallas_call x1, Pallas kernels, down_both(): pl.pallas_call(functools.partial(down_kernel, split), grid=(t // BLOCK,),...  22.1 us
    pallas_call x1, Pallas kernels, attention_forward(): pl.pallas_call(functools.partial(attention_forward_kernel, wide), grid_sp...  21.5 us
  transfers between devices with their start and end apart: 35, of which 18 were waited for; matrix products, arithmetic and copies ran while one was open for 8% of the time, Pallas kernels for 34%

profile of v4, /device:TPU:0, one launch (start us, length us, event | category | flops | bytes accessed | tf_op | source)
XLA Modules:
  0.0 401.8 jit_solution(10136621886657455364)
XLA Ops:
  20.6 3.1 collective-permute-done.3
  26.6 8.2 %collective-permute-done = bf16[80,768]{1,0:T(8,128)(2,1)S(1)} collective-permute-done((bf16[80,768]{1,0:T(8,128)(2,1)S(1)}, bf16[80,768]{1,0:T(8,128)(2,1)S(1)}, u32[]{:S(2)}, u32[]{:S(2)}) %collective-permute-start) | collective-permute-done | bytes 122912 | tf_op jit(solution)/shard_map/ppermute | solution.py:753
  37.0 6.7 %collective-permute-done.1 = bf16[2,80,768]{2,1,0:T(8,128)(2,1)S(1)} collective-permute-done((bf16[2,80,768]{2,1,0:T(8,128)(2,1)S(1)}, bf16[2,80,768]{2,1,0:T(8,128)(2,1)S(1)}, u32[]{:S(2)}, u32[]{:S(2)}) %collective-permute-start.1) | collective-permute-done | bytes 245792 | tf_op jit(solution)/shard_map/ppermute | solution.py:753
  49.3 11.5 %collective-permute-done.6.refs_7_ = bf16[4,80,768]{2,1,0:T(8,128)(2,1)} collective-permute-done((bf16[4,80,768]{2,1,0:T(8,128)(2,1)S(1)}, bf16[4,80,768]{2,1,0:T(8,128)(2,1)}, u32[]{:S(2)}, u32[]{:S(2)}) %collective-permute-start.6) | collective-permute-done | bytes 491552 | tf_op jit(solution)/shard_map/ppermute | solution.py:753
  64.3 9.9 %qkv_forward.1 = (bf16[1024,768]{1,0:T(8,128)(2,1)S(1)}, bf16[1024,2304]{1,0:T(8,128)(2,1)}, bf16[768,2304]{1,0:T(8,128)(2,1)S(1)}, f32[1,768]{1,0:T(1,128)S(1)}...) custom-call(s32[32]{0:T(128)S(1)} %stack.232.refs_0_, bf16[1024,768]{1,0:T(8,128)(2,1)S(1)} %copy-done.13, ...), custom_call_target="tpu_custom_call" | custom-call | flops 3623878656 | bytes 16515072 | tf_op jit(solution)/shard_map/qkv_forward/pallas_call | solution.py:182
  80.8 21.5 %attention_forward.1 = (f32[1024,768]{1,0:T(8,128)S(1)}, f32[6,8,1024]{2,1,0:T(8,128)S(1)}) custom-call(s32[4]{0:T(128)S(1)} %add_bitcast_fusion.reach, bf16[1024,2304]{1,0:T(8,128)(2,1)S(1)} %copy-done, bf16[1024,2304]{1,0:T(8,128)(2,1)S(1)} %copy-done, bf16[1024,2304]{1,0:T(8,128)(2,1)S(1)} %copy-done, s32[1024,1]{1,0:T(8,128)S(1)} %copy.22.start_ref), custom_call_target="tpu_custom_call" | custom-call | flops 1610612736 | bytes 9437184 | tf_op jit(solution)/shard_map/attention_forward/pallas_call | solution.py:293
  104.0 7.7 %all-gather.2.cloned.1.call-done = bf16[6912,768]{1,0:T(8,128)(2,1)} async-done(((bf16[216,768]{1,0:T(8,128)(2,1)}), bf16[6912,768]{1,0:T(8,128)(2,1)}) %all-gather.2.cloned.1.call-update) | async-done | bytes 10616848 | tf_op jit(solution)/shard_map/all_gather | solution.py:912
  111.7 35.8 %up_forward.1 = (bf16[1024,768]{1,0:T(8,128)(2,1)}, f32[1024,768]{1,0:T(8,128)}, bf16[1024,768]{1,0:T(8,128)(2,1)}, bf16[1024,3072]{1,0:T(8,128)(2,1)}, bf16[102...) custom-call(f32[1024,768]{1,0:T(8,128)} %copy-done.1, ...), custom_call_target="tpu_custom_call" | custom-call | flops 10871635968 | bytes 41680896 | tf_op jit(solution)/shard_map/up_forward/pallas_call | solution.py:478
  151.1 22.1 %down_both.1 = (bf16[1024,768]{1,0:T(8,128)(2,1)}, bf16[1024,3072]{1,0:T(8,128)(2,1)}, f32[1,3072]{1,0:T(1,128)S(1)}) custom-call(bf16[1024,3072]{1,0:T(8,128)(2,1)} %get-tuple-element.73.m_ref, bf16[1024,3072]{1,0:T(8,128)(2,1)} %get-tuple-element.74.slope_ref, f32[1024,128]{1,0:T(8,128)S(1)} %copy-done.49, f32[1024,768]{1,0:T(8,128)S(1)} %copy-done.43, ...), custom_call_target="tpu_custom_call" | custom-call | flops 9663676416 | bytes 29884416 | tf_op jit(solution)/shard_map/down_both/pallas_call | solution.py:544
  173.8 16.1 %up_backward.1 = (f32[1024,768]{1,0:T(8,128)S(1)}, bf16[1024,768]{1,0:T(8,128)(2,1)S(1)}, bf16[1024,768]{1,0:T(8,128)(2,1)S(1)}, f32[1,768]{1,0:T(1,128)S(1)}, f32[1,768]{1,0:T(1,128)S(1)}) custom-call(bf16[1024,3072]{1,0:T(8,128)(2,1)} %get-tuple-element.78.dpre_ref.refs_2_, f32[1024,768]{1,0:T(8,128)S(1)} %copy-done.44, bf16[1024,768]{1,0:T(8,128)(2,1)S(1)} %copy-done.12, ...), custom_call_target="tpu_custom_call" | custom-call | flops 6039797760 | bytes 31064064 | tf_op jit(solution)/shard_map/up_backward/pallas_call | solution.py:589
  193.9 19.2 %up_weight_grad.1 = (f32[16,120,768]{2,1,0:T(8,128)}, bf16[16,120,768]{2,1,0:T(8,128)(2,1)}) custom-call(s32[32]{0:T(128)} %stack.263.refs_0_, bf16[1024,768]{1,0:T(8,128)(2,1)} %get-tuple-element.83.refs_1_, bf16[1024,3072]{1,0:T(8,128)(2,1)} %get-tuple-element.78.dpre_ref.refs_2_, bf16[1024,768]{1,0:T(8,128)(2,1)} %get-tuple-element.84.refs_3_, ...), custom_call_target="tpu_custom_call" | custom-call | flops 6039797760 | bytes 28704768 | tf_op jit(solution)/shard_map/up_weight_grad/pallas_call | solution.py:182
  216.9 12.3 %attention_backward.3 = (bf16[1024,256]{1,0:T(8,128)(2,1)S(1)}, bf16[1024,256]{1,0:T(8,128)(2,1)S(1)}, bf16[1024,256]{1,0:T(8,128)(2,1)S(1)}) custom-call(s32[4]{0:T(128)S(1)} %add_bitcast_fusion.reach, bf16[1024,2304]{1,0:T(8,128)(2,1)S(1)} %bitcast.96, bf16[1024,2304]{1,0:T(8,128)(2,1)S(1)} %bitcast.96, bf16[1024,2304]{1,0:T(8,128)(2,1)S(1)} %bitcast.96, ...), custom_call_target="tpu_custom_call" | custom-call | flops 1342177280 | bytes 5242880 | tf_op jit(solution)/shard_map/attention_backward/pallas_call | solution.py:393
  230.8 6.9 %fusion.18 = (bf16[16,120,768]{2,1,0:T(8,128)(2,1)S(1)}, f32[16,120,768]{2,1,0:T(8,128)}) fusion(f32[16,120,768]{2,1,0:T(8,128)} %get-tuple-element.94, bf16[16,120,768]{2,1,0:T(8,128)(2,1)} %copy-done.56), kind=kLoop, calls=%fused_computation.78 | loop fusion | flops 4423680 | bytes 17694720 | tf_op jit(solution)/shard_map/convert.13
  239.5 12.3 %attention_backward.4 = (bf16[1024,256]{1,0:T(8,128)(2,1)S(1)}, bf16[1024,256]{1,0:T(8,128)(2,1)S(1)}, bf16[1024,256]{1,0:T(8,128)(2,1)S(1)}) custom-call(s32[4]{0:T(128)S(1)} %add_bitcast_fusion.reach, bf16[1024,2304]{1,0:T(8,128)(2,1)S(1)} %bitcast.96, bf16[1024,2304]{1,0:T(8,128)(2,1)S(1)} %bitcast.96, bf16[1024,2304]{1,0:T(8,128)(2,1)S(1)} %bitcast.96, ...), custom_call_target="tpu_custom_call" | custom-call | flops 1342177280 | bytes 5242880 | tf_op jit(solution)/shard_map/attention_backward/pallas_call | solution.py:393
  251.8 5.7 %collective-permute-done.12 = bf16[4,120,768]{2,1,0:T(8,128)(2,1)S(1)} collective-permute-done((bf16[4,120,768]{2,1,0:T(8,128)(2,1)S(1)}, bf16[4,120,768]{2,1,0:T(8,128)(2,1)S(1)}, u32[]{:S(2)}, u32[]{:S(2)}) %collective-permute-start.12) | collective-permute-done | bytes 737312 | tf_op jit(solution)/shard_map/ppermute | solution.py:753
  263.2 12.4 %attention_backward.5 = (bf16[1024,256]{1,0:T(8,128)(2,1)S(1)}, bf16[1024,256]{1,0:T(8,128)(2,1)S(1)}, bf16[1024,256]{1,0:T(8,128)(2,1)S(1)}) custom-call(s32[4]{0:T(128)S(1)} %add_bitcast_fusion.reach, bf16[1024,2304]{1,0:T(8,128)(2,1)S(1)} %bitcast.96, bf16[1024,2304]{1,0:T(8,128)(2,1)S(1)} %bitcast.96, bf16[1024,2304]{1,0:T(8,128)(2,1)S(1)} %bitcast.96, ...), custom_call_target="tpu_custom_call" | custom-call | flops 1342177280 | bytes 5242880 | tf_op jit(solution)/shard_map/attention_backward/pallas_call | solution.py:393
  293.0 17.1 %qkv_weight_grad.1 = (f32[16,72,768]{2,1,0:T(8,128)S(1)}, bf16[16,72,768]{2,1,0:T(8,128)(2,1)}) custom-call(s32[32]{0:T(128)S(1)} %copy-done.11, bf16[1024,768]{1,0:T(8,128)(2,1)S(1)} %copy-done.48, bf16[1024,256]{1,0:T(8,128)(2,1)S(1)} %copy-done.15, bf16[1024,256]{1,0:T(8,128)(2,1)S(1)} %copy-done.24, bf16[1024,256]{1,0:T(8,128)(2,1)S(1)} %copy-done.33, ...), custom_call_target="tpu_custom_call" | custom-call | flops 3623878656 | bytes 13369344 | tf_op jit(solution)/shard_map/qkv_weight_grad/pallas_call | solution.py:182
  311.6 3.4 collective-permute-start.18
  320.5 7.5 %collective-permute-done.17 = bf16[120,768]{1,0:T(8,128)(2,1)} collective-permute-done((bf16[120,768]{1,0:T(8,128)(2,1)}, bf16[120,768]{1,0:T(8,128)(2,1)}, u32[]{:S(2)}, u32[]{:S(2)}) %collective-permute-start.17) | collective-permute-done | bytes 184352 | tf_op jit(solution)/shard_map/ppermute | solution.py:753
  337.4 9.2 %qkv_backward.1 = (f32[1024,768]{1,0:T(8,128)}, f32[1,768]{1,0:T(1,128)S(1)}) custom-call(bf16[1024,256]{1,0:T(8,128)(2,1)S(1)} %copy-done.16, bf16[1024,256]{1,0:T(8,128)(2,1)S(1)} %copy-done.25, bf16[1024,256]{1,0:T(8,128)(2,1)S(1)} %copy-done.34, bf16[1024,256]{1,0:T(8,128)(2,1)S(1)} %copy-done.19, bf16[1024,256]{1,0:T(8,128)(2,1)S(1)} %copy-done.28, ...), custom_call_target="tpu_custom_call" | custom-call | flops 3623878656 | bytes 16121856 | tf_op jit(solution)/shard_map/qkv_backward/pallas_call | solution.py:711
  355.7 4.0 collective-permute-start.30
  362.1 3.7 fusion.17
  367.9 7.8 %collective-permute-done.20 = bf16[4,72,768]{2,1,0:T(8,128)(2,1)S(1)} collective-permute-done((bf16[4,72,768]{2,1,0:T(8,128)(2,1)S(1)}, bf16[4,72,768]{2,1,0:T(8,128)(2,1)S(1)}, u32[]{:S(2)}, u32[]{:S(2)}) %collective-permute-start.20) | collective-permute-done | bytes 442400 | tf_op jit(solution)/shard_map/ppermute | solution.py:753
  383.5 3.8 collective-permute-start.26
  (258 shorter events, 118.7 us)
Async XLA Ops:
  7.2 104.5 %all-gather.2.cloned.1.call-start = ((), (), s32[]{:S(2)}) async-start(), calls=%async_computation.1 | async-start | bytes 10948608 | tf_op jit(solution)/shard_map/all_gather | solution.py:912
  12.8 267.7 %reduce-scatter.2.cloned.1.call-start = ((), (), s32[]{:S(2)}) async-start(), calls=%async_computation.2 | async-start | bytes 4866048 | tf_op jit(solution)/shard_map/reduce_scatter | solution.py:909
  14.4 9.3 %collective-permute-start.3 = (bf16[80,768]{1,0:T(8,128)(2,1)S(1)}, bf16[80,768]{1,0:T(8,128)(2,1)S(1)}, u32[]{:S(2)}, u32[]{:S(2)}) collective-permute-start(bf16[80,768]{1,0:T(8,128)(2,1)S(1)} %fusion.8), channel_id=1, source_target_pairs={{0,2},{1,3},{2,4},{3,5},{4,6},{5,7},{6,0},{7,1},{8,10},{9,11},{10,... | collective-permute-start | bytes 368648 | tf_op jit(solution)/shard_map/ppermute | solution.py:753
  19.6 15.1 %collective-permute-start = (bf16[80,768]{1,0:T(8,128)(2,1)S(1)}, bf16[80,768]{1,0:T(8,128)(2,1)S(1)}, u32[]{:S(2)}, u32[]{:S(2)}) collective-permute-start(bf16[80,768]{1,0:T(8,128)(2,1)S(1)} %fusion.8), channel_id=1, source_target_pairs={{0,4},{1,5},{2,6},{3,7},{4,0},{5,1},{6,2},{7,3},{8,12},{9,13},{10,... | collective-permute-start | bytes 368648 | tf_op jit(solution)/shard_map/ppermute | solution.py:753
  25.0 11.4 %collective-permute-start.5 = (bf16[2,80,768]{2,1,0:T(8,128)(2,1)S(1)}, bf16[2,80,768]{2,1,0:T(8,128)(2,1)S(1)}, u32[]{:S(2)}, u32[]{:S(2)}) collective-permute-start(bf16[2,80,768]{2,1,0:T(8,128)(2,1)S(1)} %pad_maximum_fusion.4), channel_id=1, source_target_pairs={{0,1},{1,0},{2,3},{3,2},{4,5},{5,4},{6,7},{7,6},{8,9},{9,8},{10,11... | collective-permute-start | bytes 737288 | tf_op jit(solution)/shard_map/ppermute | solution.py:753
  34.8 8.9 %collective-permute-start.1 = (bf16[2,80,768]{2,1,0:T(8,128)(2,1)S(1)}, bf16[2,80,768]{2,1,0:T(8,128)(2,1)S(1)}, u32[]{:S(2)}, u32[]{:S(2)}) collective-permute-start(bf16[2,80,768]{2,1,0:T(8,128)(2,1)S(1)} %pad_maximum_fusion.3), channel_id=1, source_target_pairs={{0,16},{1,17},{2,18},{3,19},{4,20},{5,21},{6,22},{7,23},{8,24},{9,... | collective-permute-start | bytes 737288 | tf_op jit(solution)/shard_map/ppermute | solution.py:753
  36.5 24.4 %collective-permute-start.6 = (bf16[4,80,768]{2,1,0:T(8,128)(2,1)S(1)}, bf16[4,80,768]{2,1,0:T(8,128)(2,1)}, u32[]{:S(2)}, u32[]{:S(2)}) collective-permute-start(bf16[4,80,768]{2,1,0:T(8,128)(2,1)S(1)} %pad_maximum_fusion.1.refs_6_), channel_id=1, source_target_pairs={{0,16},{1,17},{2,18},{3,19},{4,20},{5,21},{6,22},{7,23},{8,24},{9,... | collective-permute-start | bytes 1474568 | tf_op jit(solution)/shard_map/ppermute | solution.py:753
  43.8 17.1 %collective-permute-start.2 = (bf16[4,80,768]{2,1,0:T(8,128)(2,1)S(1)}, bf16[4,80,768]{2,1,0:T(8,128)(2,1)}, u32[]{:S(2)}, u32[]{:S(2)}) collective-permute-start(bf16[4,80,768]{2,1,0:T(8,128)(2,1)S(1)} %pad_maximum_fusion.refs_4_), channel_id=1, source_target_pairs={{0,1},{1,0},{2,3},{3,2},{4,5},{5,4},{6,7},{7,6},{8,9},{9,8},{10,11... | collective-permute-start | bytes 1474568 | tf_op jit(solution)/shard_map/ppermute | solution.py:753
  48.7 15.5 %collective-permute-start.9 = (bf16[4,80,768]{2,1,0:T(8,128)(2,1)S(1)}, bf16[4,80,768]{2,1,0:T(8,128)(2,1)}, u32[]{:S(2)}, u32[]{:S(2)}) collective-permute-start(bf16[4,80,768]{2,1,0:T(8,128)(2,1)S(1)} %pad_maximum_fusion.1.refs_6_), channel_id=1, source_target_pairs={{0,8},{1,9},{2,10},{3,11},{4,12},{5,13},{6,14},{7,15},{8,0},{9,1},... | collective-permute-start | bytes 1474568 | tf_op jit(solution)/shard_map/ppermute | solution.py:753
  48.8 15.5 %collective-permute-start.7 = (bf16[4,80,768]{2,1,0:T(8,128)(2,1)S(1)}, bf16[4,80,768]{2,1,0:T(8,128)(2,1)}, u32[]{:S(2)}, u32[]{:S(2)}) collective-permute-start(bf16[4,80,768]{2,1,0:T(8,128)(2,1)S(1)} %pad_maximum_fusion.refs_4_), channel_id=1, source_target_pairs={{0,8},{1,9},{2,10},{3,11},{4,12},{5,13},{6,14},{7,15},{8,0},{9,1},... | collective-permute-start | bytes 1474568 | tf_op jit(solution)/shard_map/ppermute | solution.py:753
  213.1 16.1 %collective-permute-start.11 = (bf16[16,120,768]{2,1,0:T(8,128)(2,1)}, bf16[16,120,768]{2,1,0:T(8,128)(2,1)S(1)}, u32[]{:S(2)}, u32[]{:S(2)}) collective-permute-start(bf16[16,120,768]{2,1,0:T(8,128)(2,1)} %get-tuple-element.86), channel_id=1, source_target_pairs={{0,8},{1,9},{2,10},{3,11},{4,12},{5,13},{6,14},{7,15},{8,0},{9,1},... | collective-permute-start | bytes 8847368 | tf_op jit(solution)/shard_map/ppermute | solution.py:753
  237.9 19.7 %collective-permute-start.12 = (bf16[4,120,768]{2,1,0:T(8,128)(2,1)S(1)}, bf16[4,120,768]{2,1,0:T(8,128)(2,1)S(1)}, u32[]{:S(2)}, u32[]{:S(2)}) collective-permute-start(bf16[4,120,768]{2,1,0:T(8,128)(2,1)S(1)} %get-tuple-element.95), channel_id=1, source_target_pairs={{0,1},{1,0},{2,3},{3,2},{4,5},{5,4},{6,7},{7,6},{8,9},{9,8},{10,11... | collective-permute-start | bytes 2211848 | tf_op jit(solution)/shard_map/ppermute | solution.py:753
  238.3 20.2 %collective-permute-start.13 = (bf16[4,120,768]{2,1,0:T(8,128)(2,1)S(1)}, bf16[4,120,768]{2,1,0:T(8,128)(2,1)S(1)}, u32[]{:S(2)}, u32[]{:S(2)}) collective-permute-start(bf16[4,120,768]{2,1,0:T(8,128)(2,1)S(1)} %get-tuple-element.96), channel_id=1, source_target_pairs={{0,16},{1,17},{2,18},{3,19},{4,20},{5,21},{6,22},{7,23},{8,24},{9,... | collective-permute-start | bytes 2211848 | tf_op jit(solution)/shard_map/ppermute | solution.py:753
  260.9 17.2 %collective-permute-start.15 = (bf16[2,120,768]{2,1,0:T(8,128)(2,1)S(1)}, bf16[2,120,768]{2,1,0:T(8,128)(2,1)S(1)}, u32[]{:S(2)}, u32[]{:S(2)}) collective-permute-start(bf16[2,120,768]{2,1,0:T(8,128)(2,1)S(1)} %slice.284), channel_id=1, source_target_pairs={{0,16},{1,17},{2,18},{3,19},{4,20},{5,21},{6,22},{7,23},{8,24},{9,... | collective-permute-start | bytes 1105928 | tf_op jit(solution)/shard_map/ppermute | solution.py:753
  261.6 18.1 %collective-permute-start.14 = (bf16[2,120,768]{2,1,0:T(8,128)(2,1)S(1)}, bf16[2,120,768]{2,1,0:T(8,128)(2,1)S(1)}, u32[]{:S(2)}, u32[]{:S(2)}) collective-permute-start(bf16[2,120,768]{2,1,0:T(8,128)(2,1)S(1)} %slice.283), channel_id=1, source_target_pairs={{0,1},{1,0},{2,3},{3,2},{4,5},{5,4},{6,7},{7,6},{8,9},{9,8},{10,11... | collective-permute-start | bytes 1105928 | tf_op jit(solution)/shard_map/ppermute | solution.py:753
  310.1 52.0 %collective-permute-start.19 = (bf16[16,72,768]{2,1,0:T(8,128)(2,1)}, bf16[16,72,768]{2,1,0:T(8,128)(2,1)}, u32[]{:S(2)}, u32[]{:S(2)}) collective-permute-start(bf16[16,72,768]{2,1,0:T(8,128)(2,1)} %get-tuple-element.113), channel_id=1, source_target_pairs={{0,8},{1,9},{2,10},{3,11},{4,12},{5,13},{6,14},{7,15},{8,0},{9,1},... | collective-permute-start | bytes 5308424 | tf_op jit(solution)/shard_map/ppermute | solution.py:753
  310.8 9.7 %collective-permute-start.16 = (bf16[120,768]{1,0:T(8,128)(2,1)}, bf16[120,768]{1,0:T(8,128)(2,1)}, u32[]{:S(2)}, u32[]{:S(2)}) collective-permute-start(bf16[120,768]{1,0:T(8,128)(2,1)} %get-tuple-element.107), channel_id=1, source_target_pairs={{0,2},{1,3},{2,4},{3,5},{4,6},{5,7},{6,0},{7,1},{8,10},{9,11},{10,... | collective-permute-start | bytes 552968 | tf_op jit(solution)/shard_map/ppermute | solution.py:753
  311.6 16.4 %collective-permute-start.17 = (bf16[120,768]{1,0:T(8,128)(2,1)}, bf16[120,768]{1,0:T(8,128)(2,1)}, u32[]{:S(2)}, u32[]{:S(2)}) collective-permute-start(bf16[120,768]{1,0:T(8,128)(2,1)} %fusion.7), channel_id=1, source_target_pairs={{0,4},{1,5},{2,6},{3,7},{4,0},{5,1},{6,2},{7,3},{8,12},{9,13},{10,... | collective-permute-start | bytes 552968 | tf_op jit(solution)/shard_map/ppermute | solution.py:753
  311.6 16.4 %collective-permute-start.18 = (bf16[120,768]{1,0:T(8,128)(2,1)}, bf16[120,768]{1,0:T(8,128)(2,1)}, u32[]{:S(2)}, u32[]{:S(2)}) collective-permute-start(bf16[120,768]{1,0:T(8,128)(2,1)} %get-tuple-element.109), channel_id=1, source_target_pairs={{0,6},{1,7},{2,0},{3,1},{4,2},{5,3},{6,4},{7,5},{8,14},{9,15},{10,... | collective-permute-start | bytes 552968 | tf_op jit(solution)/shard_map/ppermute | solution.py:753
  355.7 11.5 %collective-permute-start.30 = (f32[8,768]{1,0:T(8,128)S(1)}, f32[8,768]{1,0:T(8,128)S(1)}, u32[]{:S(2)}, u32[]{:S(2)}) collective-permute-start(f32[8,768]{1,0:T(8,128)S(1)} %add.722), channel_id=1, source_target_pairs={{0,2},{1,3},{2,4},{3,5},{4,6},{5,7},{6,0},{7,1},{8,10},{9,11},{10,... | collective-permute-start | bytes 73736 | tf_op jit(solution)/shard_map/ppermute | solution.py:753
  359.7 7.5 %collective-permute-start.31 = (f32[8,768]{1,0:T(8,128)S(1)}, f32[8,768]{1,0:T(8,128)S(1)}, u32[]{:S(2)}, u32[]{:S(2)}) collective-permute-start(f32[8,768]{1,0:T(8,128)S(1)} %add.722), channel_id=1, source_target_pairs={{0,4},{1,5},{2,6},{3,7},{4,0},{5,1},{6,2},{7,3},{8,12},{9,13},{10,... | collective-permute-start | bytes 73736 | tf_op jit(solution)/shard_map/ppermute | solution.py:753
  359.7 7.5 %collective-permute-start.32 = (f32[8,768]{1,0:T(8,128)S(1)}, f32[8,768]{1,0:T(8,128)S(1)}, u32[]{:S(2)}, u32[]{:S(2)}) collective-permute-start(f32[8,768]{1,0:T(8,128)S(1)} %add.722), channel_id=1, source_target_pairs={{0,6},{1,7},{2,0},{3,1},{4,2},{5,3},{6,4},{7,5},{8,14},{9,15},{10,... | collective-permute-start | bytes 73736 | tf_op jit(solution)/shard_map/ppermute | solution.py:753
  365.9 9.8 %collective-permute-start.20 = (bf16[4,72,768]{2,1,0:T(8,128)(2,1)S(1)}, bf16[4,72,768]{2,1,0:T(8,128)(2,1)S(1)}, u32[]{:S(2)}, u32[]{:S(2)}) collective-permute-start(bf16[4,72,768]{2,1,0:T(8,128)(2,1)S(1)} %get-tuple-element.137), channel_id=1, source_target_pairs={{0,1},{1,0},{2,3},{3,2},{4,5},{5,4},{6,7},{7,6},{8,9},{9,8},{10,11... | collective-permute-start | bytes 1327112 | tf_op jit(solution)/shard_map/ppermute | solution.py:753
  365.9 9.8 %collective-permute-start.21 = (bf16[4,72,768]{2,1,0:T(8,128)(2,1)S(1)}, bf16[4,72,768]{2,1,0:T(8,128)(2,1)S(1)}, u32[]{:S(2)}, u32[]{:S(2)}) collective-permute-start(bf16[4,72,768]{2,1,0:T(8,128)(2,1)S(1)} %get-tuple-element.136), channel_id=1, source_target_pairs={{0,16},{1,17},{2,18},{3,19},{4,20},{5,21},{6,22},{7,23},{8,24},{9,... | collective-permute-start | bytes 1327112 | tf_op jit(solution)/shard_map/ppermute | solution.py:753
  (76 other events, 470.6 us)
Sparse Core Ops, SparseCore 0:
  12.9 98.7 all-gather.1
  147.7 105.8 reduce-scatter.1
